TPU v7x, 32 devices: a whole 2x2x4 slice. The times are simulated.
32 devices in a mesh: seq: 8 (over z, core), dp: 4 (over y, x).
Axes of the slice: x: 2, y: 2, z: 4, core: 2. Of those that a mesh axis runs over, the one named last changes fastest.
Arguments:
- tokens: bfloat16 [8, 512, 768], P('dp', 'seq'), may hold values from -6 to 6
- segments: int32 [8, 512], P('dp', 'seq'), may hold values from 0 to 1, never falling along the last dimension, each value on 1 to 384 neighbouring positions
- padding: int32 [8, 512], P('dp', 'seq'), may hold values from 0 to 1, as said below
- w_qkv: bfloat16 [768, 2304], P(('seq', 'dp')), may hold values from -0.21875 to 0.21875
- w_out: bfloat16 [768, 768], P(('seq', 'dp')), may hold values from -0.625 to 0.625
- w_gate_up: bfloat16 [768, 6144], P(('seq', 'dp')), may hold values from -0.21875 to 0.21875
- w_down: bfloat16 [3072, 768], P(('seq', 'dp')), may hold values from -0.15625 to 0.15625
- biases: bfloat16 [4608], P(('seq', 'dp')), may hold values from -2 to 2
- norm_gains: bfloat16 [1536], P(('seq', 'dp')), may hold values from 0.25 to 1.75
- cotangent: bfloat16 [8, 512, 768], P('dp', 'seq'), may hold values from -6 to 6
Outputs:
- layer_out: bfloat16 [8, 512, 768], P('dp', 'seq')
- grad_tokens: float32 [8, 512, 768], P('dp', 'seq')
- grad_w_qkv: float32 [768, 2304], P(('seq', 'dp'))
- grad_w_out: float32 [768, 768], P(('seq', 'dp'))
- grad_w_gate_up: float32 [768, 6144], P(('seq', 'dp'))
- grad_w_down: float32 [3072, 768], P(('seq', 'dp'))
- grad_biases: float32 [4608], P(('seq', 'dp'))
- grad_norm_gains: float32 [1536], P(('seq', 'dp'))
Inputs may be any that keep to these rules, and one draw needn't show every extreme that they name: `segments`: within a sequence the segment numbers never fall; each number 0 to 1 marks one document of 1 to 384 tokens. `padding`: in each sequence the zeros, if any, form its tail.
All inputs are finite; a program needn't handle non-finite values.
Results may differ from a plain program's by a relative error of at most 0.02.
Values may be sent and summed in bfloat16 or wider, within the bound.
No kernel may reach another device: no remote copies, remote signals or barrier semaphores. Data moves between devices by JAX's collectives and lax.ppermute only.
A program may use at most 128 MiB of HBM per device.

v0:
```python
import math

import jax
import jax.numpy as jnp
import numpy as np
from jax import lax
from jax.experimental import pallas as pl
from jax.experimental.pallas import tpu as pltpu
from jax.sharding import PartitionSpec as P


D = 768
H = 12
HD = 64
FF = 3072
GROUP = 4
QUERY_BLOCK = 128

NEG_FILL = -1e30
EPSILON = 1e-12
LOW = jnp.bfloat16
WIDE = jnp.float32


def slope_table(head_count):
    nearest = 2 ** int(math.floor(math.log2(head_count)))
    leading = [2.0 ** (-8.0 * (counter + 1) / nearest) for counter in range(nearest)]
    further = [2.0 ** (-8.0 * (counter + 1) / (2 * nearest)) for counter in range(2 * nearest)]
    return np.array(leading + further[0::2][: head_count - nearest], np.float32)


def dot(left, right):
    return jnp.dot(left, right, preferred_element_type=WIDE)


def dot_t(left, right):
    return lax.dot_general(left, right, (((1,), (1,)), ((), ())), preferred_element_type=WIDE)


def dot_w(left, right):
    return lax.dot_general(left, right, (((0,), (0,)), ((), ())), preferred_element_type=WIDE)


def swap(value, axis, size, mask):
    return lax.ppermute(value, axis, [(i, i ^ mask) for i in range(size)])


def put(buffer, value, index, axis):
    starts = [0] * buffer.ndim
    starts[axis] = index
    return lax.dynamic_update_slice(buffer, jnp.expand_dims(value, axis), starts)


def swapped(value, name, size, step=1):
    total = lax.axis_size(name)
    return (value,) + tuple(swap(value, name, total, mask * step) for mask in range(1, size))


def in_order(pieces, place, axis):
    value = pieces[0]
    shape = value.shape[:axis] + (len(pieces),) + value.shape[axis:]
    result = jnp.zeros(shape, value.dtype)
    for mask, piece in enumerate(pieces):
        result = put(result, piece, place ^ mask, axis)
    return result


def gather_by_swaps(value, name, size, place, axis, step=1):
    return in_order(swapped(value, name, size, step), place, axis)


def scatter_swaps(value, name, size, place, axis, step=1):
    total = lax.axis_size(name)
    pieces = [lax.dynamic_index_in_dim(value, place, axis, False)]
    for mask in range(1, size):
        part = lax.dynamic_index_in_dim(value, place ^ mask, axis, False).astype(LOW)
        pieces.append(swap(part, name, total, mask * step))
    return tuple(pieces)


def add_up(pieces):
    result = pieces[0].astype(WIDE)
    for piece in pieces[1:]:
        result = result + piece.astype(WIDE)
    return result


def scatter_by_swaps(value, name, size, place, axis, step=1):
    return add_up(scatter_swaps(value, name, size, place, axis, step))


def group_gather(rows, seq_count):
    partner = swap(rows, "seq", seq_count, 1)
    across = swap(rows, "seq", seq_count, 2)
    corner = swap(across, "seq", seq_count, 1)
    return jnp.concatenate([rows, partner, across, corner], axis=0)


def group_scatter(partial, seq_count):
    rows = partial.shape[0] // GROUP
    blocks = partial.reshape(GROUP, rows, partial.shape[1])
    sent = jnp.stack([blocks[1], blocks[3]]).astype(LOW)
    came = swap(sent, "seq", seq_count, 1).astype(WIDE)
    across = swap((blocks[2] + came[1]).astype(LOW), "seq", seq_count, 2).astype(WIDE)
    return blocks[0] + came[0] + across


def sequence_reduce(blocks, seq_count, seq_at, sequences):
    total, step = blocks, 1
    while total.shape[0] > sequences:
        halves = total.reshape((total.shape[0] // 2, 2) + total.shape[1:])
        bit = (seq_at // step) % 2
        sent = lax.dynamic_index_in_dim(halves, 1 - bit, 1, False).astype(LOW)
        kept = lax.dynamic_index_in_dim(halves, bit, 1, False).astype(WIDE)
        total = kept + swap(sent, "seq", seq_count, step).astype(WIDE)
        step *= 2
    return total


def sequence_swap(total, seq_count, seq_at, sequences):
    step = seq_count // sequences
    own = seq_at // step
    result = put(jnp.zeros_like(total), lax.dynamic_index_in_dim(total, own, 0, False), own, 0)
    for mask in range(1, sequences):
        sent = lax.dynamic_index_in_dim(total, own ^ mask, 0, False).astype(LOW)
        came = swap(sent, "seq", seq_count, mask * step).astype(WIDE)
        result = put(result, came, own ^ mask, 0)
    return result


def head_columns(head, width):
    column = lax.broadcasted_iota(jnp.int32, (1, width), 1)
    return ((column >= head * HD) & (column < (head + 1) * HD)).astype(WIDE).astype(LOW)


def block_scores(query_rows, keys, slope, start, marks_column, marks_row):
    shape = (query_rows.shape[0], keys.shape[0])
    row = lax.broadcasted_iota(jnp.int32, shape, 0) + start
    column = lax.broadcasted_iota(jnp.int32, shape, 1)
    distance = jnp.abs(row - column).astype(WIDE)
    allowed = (marks_column[:, 0:1] == marks_row[0:1]) & (marks_row[1:2] >= marks_column[:, 1:2])
    return jnp.where(allowed, dot_t(query_rows, keys) * 0.125 - slope * distance, NEG_FILL)


def attend_kernel(heads, width, slopes, qkv, marks_column, marks_row, out, sums):
    keys, values = qkv[:, width : 2 * width], qkv[:, 2 * width :]

    def block(index, carry):
        start = pl.multiple_of(index * QUERY_BLOCK, QUERY_BLOCK)
        here = pl.ds(start, QUERY_BLOCK)
        queries, marks = qkv[here, :width], marks_column[here, :]
        blended = jnp.zeros((QUERY_BLOCK, width), WIDE)
        for head in range(heads):
            mask = head_columns(head, width)
            scores = block_scores(queries * mask, keys, slopes[head], start, marks, marks_row[...])
            top_score = jnp.max(scores, axis=-1, keepdims=True)
            exponent = jnp.exp(scores - top_score)
            total = jnp.sum(exponent, axis=-1, keepdims=True)
            blended = blended + dot((exponent / total).astype(LOW), values * mask)
            sums[here, head : head + 1] = top_score + jnp.log(total)
        out[here, :] = blended.astype(LOW)
        return carry

    lax.fori_loop(0, qkv.shape[0] // QUERY_BLOCK, block, 0)


def attend_back_kernel(
    heads, width, slopes, qkv, grad_out, sums, marks_column, marks_row, grad_proj, totals, acc
):
    keys, values = qkv[:, width : 2 * width], qkv[:, 2 * width :]
    acc[...] = jnp.zeros(acc.shape, WIDE)
    totals[...] = jnp.zeros(totals.shape, WIDE)

    def block(index, carry):
        start = pl.multiple_of(index * QUERY_BLOCK, QUERY_BLOCK)
        here = pl.ds(start, QUERY_BLOCK)
        queries, marks, grads = qkv[here, :width], marks_column[here, :], grad_out[here, :]
        grad_query = jnp.zeros((QUERY_BLOCK, width), WIDE)
        grad_key = jnp.zeros((qkv.shape[0], width), WIDE)
        grad_value = jnp.zeros((qkv.shape[0], width), WIDE)
        for head in range(heads):
            mask = head_columns(head, width)
            own_query, own_grad = queries * mask, grads * mask
            scores = block_scores(own_query, keys, slopes[head], start, marks, marks_row[...])
            soft = jnp.exp(scores - sums[here, head : head + 1])
            grad_soft = dot_t(own_grad, values)
            delta = jnp.sum(soft * grad_soft, axis=-1, keepdims=True)
            grad_scores = (soft * (grad_soft - delta)).astype(LOW)
            grad_query = grad_query + dot(grad_scores, keys * mask)
            grad_key = grad_key + dot_w(grad_scores, own_query)
            grad_value = grad_value + dot_w(soft.astype(LOW), own_grad)
        grad_query = grad_query * 0.125
        grad_proj[here, :width] = grad_query.astype(LOW)
        totals[0:1] = totals[0:1] + jnp.sum(grad_query, axis=0, keepdims=True)
        acc[0] = acc[0] + grad_key
        acc[1] = acc[1] + grad_value
        return carry

    lax.fori_loop(0, qkv.shape[0] // QUERY_BLOCK, block, 0)
    grad_proj[:, width : 2 * width] = (acc[0] * 0.125).astype(LOW)
    grad_proj[:, 2 * width :] = acc[1].astype(LOW)
    totals[1:2] = jnp.sum(acc[1], axis=0, keepdims=True)


def attend(heads, width, slopes, qkv, marks_column, marks_row):
    length = qkv.shape[0]
    return pl.pallas_call(
        lambda *refs: attend_kernel(heads, width, *refs),
        out_shape=(
            jax.ShapeDtypeStruct((length, width), LOW),
            jax.ShapeDtypeStruct((length, heads), WIDE),
        ),
        in_specs=[pl.BlockSpec(memory_space=pltpu.SMEM)]
        + [pl.BlockSpec(memory_space=pltpu.VMEM)] * 3,
        out_specs=[pl.BlockSpec(memory_space=pltpu.VMEM)] * 2,
        name="attend",
    )(slopes, qkv, marks_column, marks_row)


def attend_back(heads, width, slopes, qkv, grad_out, sums, marks_column, marks_row):
    length = qkv.shape[0]
    return pl.pallas_call(
        lambda *refs: attend_back_kernel(heads, width, *refs),
        out_shape=(
            jax.ShapeDtypeStruct((length, 3 * width), LOW),
            jax.ShapeDtypeStruct((8, width), WIDE),
        ),
        in_specs=[pl.BlockSpec(memory_space=pltpu.SMEM)]
        + [pl.BlockSpec(memory_space=pltpu.VMEM)] * 5,
        out_specs=[pl.BlockSpec(memory_space=pltpu.VMEM)] * 2,
        scratch_shapes=[pltpu.VMEM((2, length, width), WIDE)],
        name="attend_back",
    )(slopes, qkv, grad_out, sums, marks_column, marks_row)


def norm_forward(resid, norm_gain, norm_bias):
    centre = resid - jnp.mean(resid, axis=-1, keepdims=True)
    inverse = lax.rsqrt(jnp.mean(centre * centre, axis=-1, keepdims=True) + EPSILON)
    normed = centre * inverse
    return (normed * norm_gain + norm_bias, normed, inverse)


def norm_backward(grad_rows, normed, inverse, norm_gain):
    scaled = grad_rows * norm_gain
    first_mean = jnp.mean(scaled, axis=-1, keepdims=True)
    second_mean = jnp.mean(scaled * normed, axis=-1, keepdims=True)
    return inverse * (scaled - first_mean - normed * second_mean)


def geglu(gate_in, up_in):
    return jax.nn.gelu(gate_in, approximate=False) * up_in


def exchange(value):
    return lax.all_to_all(value, "seq", 0, 0)


def together(*values):
    return lax.optimization_barrier(values)


def local(
    tokens, segments, padding, w_qkv, w_out, w_gate_up, w_down, biases, norm_gains, cotangent
):
    sequences, seq_rows = tokens.shape[:2]
    seq_count, dp_count = lax.axis_size("seq"), lax.axis_size("dp")
    seq_at, dp_at = lax.axis_index("seq"), lax.axis_index("dp")
    halves = seq_count // GROUP
    half_at = seq_at // GROUP
    rows = sequences * seq_rows
    length = seq_count * seq_rows
    head_groups = seq_count // sequences
    heads = -(-H // head_groups)
    padded = heads * head_groups
    width = heads * HD
    own_seq, own_heads = seq_at // head_groups, seq_at % head_groups
    wide_rows = w_qkv.shape[0]
    down_rows = w_down.shape[0]
    bias_part, gain_part = biases.shape[0], norm_gains.shape[0]
    run = dp_count * down_rows

    tokens_flat = tokens.reshape(rows, D)

    by_heads = w_qkv.reshape(wide_rows, 3, H, HD)
    by_heads = jnp.pad(by_heads, ((0, 0), (0, 0), (0, padded - H), (0, 0)))
    by_heads = by_heads.reshape(wide_rows, 3, head_groups, width).transpose(2, 0, 1, 3)
    by_heads = by_heads.reshape(1, head_groups, wide_rows, 3 * width)
    by_heads = jnp.broadcast_to(by_heads, (sequences,) + by_heads.shape[1:])
    by_heads = by_heads.reshape(seq_count, wide_rows, 3 * width)
    small_columns = (bias_part + gain_part) // wide_rows
    small = jnp.concatenate([biases, norm_gains]).reshape(1, wide_rows, small_columns)
    small = jnp.broadcast_to(small, (seq_count, wide_rows, small_columns))
    qkv_rows = exchange(jnp.concatenate([by_heads, small], axis=-1))
    qkv_rows, gate_up_in, down_in = together(qkv_rows, w_gate_up, w_down)
    qkv_own = gather_by_swaps(qkv_rows, "dp", dp_count, dp_at, 1)

    marks = jnp.concatenate([segments.reshape(-1), padding.reshape(-1)]).astype(LOW)
    extra_rows = -(-marks.shape[0] // (8 * D)) * 8
    marks = jnp.pad(marks, (0, extra_rows * D - marks.shape[0])).reshape(extra_rows, D)
    packed = jnp.concatenate([tokens_flat, marks], axis=0)
    line = lax.all_gather(packed, "seq", axis=0, tiled=False)
    token_rows = lax.dynamic_slice_in_dim(line[:, :rows], own_seq * seq_rows, seq_rows, 1)
    token_rows = token_rows.reshape(length, D)
    mark_line = line[:, rows:].reshape(seq_count, extra_rows * D)[:, : 2 * rows]
    mark_line = mark_line.reshape(seq_count, 2, sequences, seq_rows)
    mark_line = lax.dynamic_index_in_dim(mark_line, own_seq, 2, False).astype(WIDE)
    marks_row = jnp.stack([mark_line[:, 0].reshape(length), mark_line[:, 1].reshape(length)])
    marks_column = marks_row.T

    out_part = gather_by_swaps(w_out, "dp", dp_count, dp_at, 0).reshape(-1, D)
    out_full = lax.all_gather(out_part, "seq", axis=0, tiled=True)

    columns = gate_up_in.reshape(wide_rows, 2, halves, GROUP, run).transpose(3, 0, 1, 2, 4)
    columns = columns.reshape(1, GROUP, wide_rows, 2 * halves * run)
    columns = jnp.broadcast_to(columns, (halves,) + columns.shape[1:])
    hidden = halves * run
    gate_up_rows = exchange(columns.reshape(seq_count, wide_rows, 2 * hidden))
    gate_up_pieces = swapped(gate_up_rows, "dp", dp_count)
    down_part = gather_by_swaps(down_in, "seq", halves, half_at, 0, GROUP)
    down_pieces = swapped(down_part, "dp", dp_count)

    vectors = qkv_own[..., 3 * width :].reshape(seq_count, dp_count, bias_part + gain_part)
    bias_vector = vectors[:, :, :bias_part].reshape(6 * D).astype(WIDE)
    gain_vector = vectors[:, :, bias_part:].reshape(2 * D).astype(WIDE)
    qkv_own = qkv_own[..., : 3 * width].reshape(D, 3 * width)

    def own_part(vector):
        spread = jnp.pad(vector, (0, padded * HD - D))
        return lax.dynamic_slice_in_dim(spread, own_heads * width, width, 0)

    own_bias = jnp.concatenate(
        [own_part(bias_vector[0:D]), jnp.zeros((width,), WIDE), own_part(bias_vector[D : 2 * D])]
    )
    qkv = (dot(token_rows, qkv_own) + own_bias).astype(LOW)
    slopes = jnp.pad(jnp.asarray(slope_table(H)), (0, padded - H))
    slopes = lax.dynamic_slice_in_dim(slopes, own_heads * heads, heads, 0)
    blended, log_sums = attend(heads, width, slopes, qkv, marks_column, marks_row)
    blended = blended.reshape(seq_count, seq_rows, width)

    def to_rows(by_head):
        arrived = exchange(by_head).reshape(sequences, head_groups, seq_rows, -1, width)
        arrived = arrived.transpose(0, 2, 3, 1, 4).reshape(rows, -1, padded * HD)
        return arrived[:, :, :D].reshape(rows, -1)

    attended = to_rows(blended)
    token_wide = tokens_flat.astype(WIDE)
    resid_one = token_wide + (dot(attended, out_full) + bias_vector[2 * D : 3 * D])
    resid_one, gate_up_pieces, down_pieces = together(resid_one, gate_up_pieces, down_pieces)
    gate_up_own = in_order(gate_up_pieces, dp_at, 1).reshape(D, 2 * hidden)
    down_own = in_order(down_pieces, dp_at, 1).reshape(hidden, D)
    hidden_one, normed_one, inverse_one = norm_forward(
        resid_one, gain_vector[0:D], bias_vector[4 * D : 5 * D]
    )
    hidden_rows = group_gather(hidden_one.astype(LOW), seq_count)
    gate_up = dot(hidden_rows, gate_up_own)
    activated_wide, geglu_back = jax.vjp(geglu, gate_up[:, :hidden], gate_up[:, hidden:])
    activated = activated_wide.astype(LOW)
    mlp_out = group_scatter(dot(activated, down_own), seq_count)
    resid_two = hidden_one + (mlp_out + bias_vector[3 * D : 4 * D])
    normed_out, normed_two, inverse_two = norm_forward(
        resid_two, gain_vector[D : 2 * D], bias_vector[5 * D : 6 * D]
    )
    valid_mask = padding.reshape(rows, 1).astype(WIDE)
    layer_out = (normed_out * valid_mask).astype(LOW)

    grad_final = cotangent.reshape(rows, D).astype(WIDE) * valid_mask
    grad_gain_two = jnp.sum(grad_final * normed_two, axis=0)
    grad_bias_two = jnp.sum(grad_final, axis=0)
    grad_resid_two = norm_backward(grad_final, normed_two, inverse_two, gain_vector[D : 2 * D])
    grad_bias_down = jnp.sum(grad_resid_two, axis=0)
    grad_mlp_rows = group_gather(grad_resid_two.astype(LOW), seq_count)
    grad_activated = dot_t(grad_mlp_rows, down_own)
    grad_gate, grad_up = geglu_back(grad_activated)
    grad_gate_up_low = jnp.concatenate([grad_gate, grad_up], axis=-1).astype(LOW)
    grad_hidden = grad_resid_two + group_scatter(dot_t(grad_gate_up_low, gate_up_own), seq_count)
    grad_down = dot_w(activated, grad_mlp_rows)
    grad_gate_up = dot_w(hidden_rows, grad_gate_up_low)
    grad_gate_up = grad_gate_up.reshape(seq_count, dp_count, wide_rows, 2 * hidden)
    grad_gate_up = scatter_swaps(grad_gate_up, "dp", dp_count, dp_at, 1)
    shard_down = grad_down.reshape(halves, dp_count, down_rows, D)
    shard_down = scatter_by_swaps(shard_down, "dp", dp_count, dp_at, 1)
    shard_down = scatter_by_swaps(shard_down, "seq", halves, half_at, 0, GROUP)

    grad_gain_one = jnp.sum(grad_hidden * normed_one, axis=0)
    grad_bias_one = jnp.sum(grad_hidden, axis=0)
    grad_resid_one = norm_backward(grad_hidden, normed_one, inverse_one, gain_vector[0:D])
    grad_bias_attn = jnp.sum(grad_resid_one, axis=0)
    grad_attn_low = grad_resid_one.astype(LOW)
    grad_attended = dot_t(grad_attn_low, out_full).astype(LOW)
    grad_out_w = dot_w(attended, grad_attn_low)
    grad_out_w = grad_out_w.reshape(seq_count, dp_count, wide_rows, D)
    grad_out_w = scatter_by_swaps(grad_out_w, "dp", dp_count, dp_at, 1).astype(LOW)

    spread = grad_attended.reshape(sequences, seq_rows, D)
    spread = jnp.pad(spread, ((0, 0), (0, 0), (0, padded * HD - D)))
    spread = spread.reshape(sequences, seq_rows, head_groups, width).transpose(0, 2, 1, 3)
    grad_blended = exchange(spread.reshape(seq_count, seq_rows, width))
    grad_blended, grad_gate_up = together(grad_blended, grad_gate_up)
    grad_gate_up = add_up(grad_gate_up).astype(LOW)
    grad_blended = grad_blended.reshape(length, width)
    grad_proj, totals = attend_back(
        heads, width, slopes, qkv, grad_blended, log_sums, marks_column, marks_row
    )

    def whole_part(vector):
        spread = jnp.zeros((padded * HD,), WIDE)
        return lax.dynamic_update_slice(spread, vector, (own_heads * width,))[:D]

    grad_bias_query = whole_part(totals[0])
    grad_bias_value = whole_part(totals[1])
    grad_rows = dot_t(grad_proj, qkv_own).astype(LOW).reshape(seq_count, seq_rows, D)
    grad_rows = sequence_reduce(grad_rows, seq_count, seq_at, sequences)
    grad_qkv = dot_w(token_rows, grad_proj)

    early = exchange(grad_gate_up).astype(WIDE)
    shard_gate_up = early.reshape(halves, GROUP, wide_rows, 2 * hidden)
    shard_gate_up = jnp.sum(shard_gate_up, axis=0).reshape(GROUP, wide_rows, 2, halves, run)
    shard_gate_up = shard_gate_up.transpose(1, 2, 3, 0, 4).reshape(wide_rows, 2 * FF)

    grad_biases = jnp.concatenate(
        [
            grad_bias_query,
            grad_bias_value,
            grad_bias_attn,
            grad_bias_down,
            grad_bias_one,
            grad_bias_two,
        ]
    ).reshape(seq_count, dp_count, bias_part)
    grad_gains = jnp.concatenate([grad_gain_one, grad_gain_two])
    grad_gains = grad_gains.reshape(seq_count, dp_count, gain_part)
    grad_small = jnp.concatenate([grad_biases, grad_gains], axis=-1)
    grad_small = grad_small.reshape(seq_count, dp_count, wide_rows, small_columns)
    late = jnp.concatenate(
        [grad_qkv.reshape(seq_count, dp_count, wide_rows, 3 * width), grad_small], axis=-1
    )
    late = scatter_swaps(late, "dp", dp_count, dp_at, 1)
    late, grad_rows = together(late, grad_rows)
    late = add_up(late).astype(LOW)
    grad_rows = sequence_swap(grad_rows, seq_count, seq_at, sequences)
    grad_tokens = grad_resid_one + grad_rows.reshape(rows, D)
    late = jnp.concatenate([late, grad_out_w], axis=-1)
    late = exchange(late).astype(WIDE)
    small_end = 3 * width + small_columns
    shard_small = jnp.sum(late[:, :, 3 * width : small_end], axis=0).reshape(-1)
    shard_out = jnp.sum(late[:, :, small_end:], axis=0)
    shard_qkv = late[:, :, : 3 * width].reshape(sequences, head_groups, wide_rows, 3, width)
    shard_qkv = jnp.sum(shard_qkv, axis=0).transpose(1, 2, 0, 3)
    shard_qkv = shard_qkv.reshape(wide_rows, 3, padded * HD)[:, :, :D].reshape(wide_rows, 3 * D)

    shape = (sequences, seq_rows, D)
    return (
        layer_out.reshape(shape),
        grad_tokens.reshape(shape),
        shard_qkv,
        shard_out,
        shard_gate_up,
        shard_down,
        shard_small[:bias_part],
        shard_small[bias_part:],
    )


def solution(mesh):
    in_specs = (
        P("dp", "seq", None),
        P("dp", "seq"),
        P("dp", "seq"),
        P(("seq", "dp"), None),
        P(("seq", "dp"), None),
        P(("seq", "dp"), None),
        P(("seq", "dp"), None),
        P(("seq", "dp")),
        P(("seq", "dp")),
        P("dp", "seq", None),
    )
    out_specs = (
        P("dp", "seq", None),
        P("dp", "seq", None),
        P(("seq", "dp"), None),
        P(("seq", "dp"), None),
        P(("seq", "dp"), None),
        P(("seq", "dp"), None),
        P(("seq", "dp")),
        P(("seq", "dp")),
    )

    return jax.shard_map(local, mesh=mesh, in_specs=in_specs, out_specs=out_specs, check_vma=False)
```

profile of v0, /device:TPU:0, one launch (start us, length us, event | category | flops | bytes accessed | tf_op | source)
XLA Modules:
  0.0 317.0 jit_solution(2606662096877964161)
XLA Ops:
  9.5 1.6 pad_maximum_fusion.9
  11.1 3.0 collective-permute-start.3
  14.1 1.5 collective-permute-start.4
  18.7 5.3 %all-to-all-start = ((bf16[8,24,584]{2,1,0:T(8,128)(2,1)}), bf16[8,24,584]{2,1,0:T(8,128)(2,1)S(1)}, u32[]{:S(2)}, u32[]{:S(2)}) async-start(bf16[8,24,584]{2,1,0:T(8,128)(2,1)} %pad_maximum_fusion.8), calls=%async_computation | async-start | bytes 491520 | tf_op jit(solution)/shard_map/all_to_all | solution.py:255
  25.6 14.8 %all-to-all-done = bf16[8,24,584]{2,1,0:T(8,128)(2,1)S(1)} async-done(((bf16[8,24,584]{2,1,0:T(8,128)(2,1)}), bf16[8,24,584]{2,1,0:T(8,128)(2,1)S(1)}, u32[]{:S(2)}, u32[]{:S(2)}) %all-to-all-start) | async-done | bytes 224288 | tf_op jit(solution)/shard_map/all_to_all | solution.py:255
  45.4 3.5 %all-to-all-start.2 = ((bf16[8,24,1536]{2,1,0:T(8,128)(2,1)}), bf16[8,24,1536]{2,1,0:T(8,128)(2,1)S(1)}, u32[]{:S(2)}, u32[]{:S(2)}) async-start(bf16[8,24,1536]{2,1,0:T(8,128)(2,1)} %bitcast.21), calls=%async_computation.2 | async-start | bytes 1179648 | tf_op jit(solution)/shard_map/all_to_all | solution.py:255
  49.0 2.8 collective-permute-start.9
  52.8 28.7 %collective-permute-done.9 = bf16[96,768]{1,0:T(8,128)(2,1)S(1)} collective-permute-done((bf16[96,768]{1,0:T(8,128)(2,1)}, bf16[96,768]{1,0:T(8,128)(2,1)S(1)}, u32[]{:S(2)}, u32[]{:S(2)}) %collective-permute-start.9) | collective-permute-done | bytes 147488 | tf_op jit(solution)/shard_map/ppermute | solution.py:45
  81.5 1.5 collective-permute-start.10
  87.2 2.4 collective-permute-start.8
  92.4 1.6 fusion.7.refs_1_
  95.5 6.9 %attend.1 = (bf16[512,192]{1,0:T(8,128)(2,1)}, f32[512,3]{1,0:T(8,128)}) custom-call(f32[3]{0:T(128)} %dynamic_slice.96.refs_0_, bf16[512,576]{1,0:T(8,128)(2,1)} %fusion.7.refs_1_, f32[512,2]{1,0:T(8,128)} %copy.133.refs_2_.refs_4_, f32[2,512]{1,0:T(2,128)} %get-tuple-element.108.refs_3_.refs_5_), custom_call_target="tpu_custom_call" | custom-call | tf_op jit(solution)/shard_map/attend/pallas_call | solution.py:207
  102.4 3.4 %all-to-all-start.1 = ((bf16[8,64,192]{2,1,0:T(8,128)(2,1)}), bf16[8,64,192]{2,1,0:T(8,128)(2,1)S(1)}, u32[]{:S(2)}, u32[]{:S(2)}) async-start(bf16[8,64,192]{2,1,0:T(8,128)(2,1)} %bitcast.314), calls=%async_computation.1 | async-start | bytes 524288 | tf_op jit(solution)/shard_map/all_to_all | solution.py:255
  107.1 8.3 %all-to-all-done.1 = bf16[8,64,192]{2,1,0:T(8,128)(2,1)S(1)} async-done(((bf16[8,64,192]{2,1,0:T(8,128)(2,1)}), bf16[8,64,192]{2,1,0:T(8,128)(2,1)S(1)}, u32[]{:S(2)}, u32[]{:S(2)}) %all-to-all-start.1) | async-done | bytes 196640 | tf_op jit(solution)/shard_map/all_to_all | solution.py:255
  115.9 1.6 fusion.8
  117.6 5.0 %collective-permute-done.12 = bf16[2,96,768]{2,1,0:T(8,128)(2,1)S(1)} collective-permute-done((bf16[2,96,768]{2,1,0:T(8,128)(2,1)S(1)}, bf16[2,96,768]{2,1,0:T(8,128)(2,1)S(1)}, u32[]{:S(2)}, u32[]{:S(2)}) %collective-permute-start.12) | collective-permute-done | bytes 294944 | tf_op jit(solution)/shard_map/ppermute | solution.py:45
  132.7 4.3 %multiply_convert_fusion.1 = (bf16[512,768]{1,0:T(8,128)(2,1)S(1)}, f32[512,768]{1,0:T(8,128)}) fusion(f32[512,1536]{1,0:T(8,128)S(1)} %fusion.60), kind=kLoop, calls=%fused_computation.13 | loop fusion | flops 25952256 | bytes 5505024 | tf_op jit(solution)/shard_map/convert_element_type | solution.py:357
  137.0 2.0 fusion.84
  142.8 1.7 fusion.43
  146.5 1.7 fusion.37
  148.2 1.9 collective-permute-start.17
  152.0 3.7 %collective-permute-done.17 = bf16[128,768]{1,0:T(8,128)(2,1)} collective-permute-done((bf16[128,768]{1,0:T(8,128)(2,1)}, bf16[128,768]{1,0:T(8,128)(2,1)}, u32[]{:S(2)}, u32[]{:S(2)}) %collective-permute-start.17) | collective-permute-done | bytes 196640 | tf_op jit(solution)/shard_map/ppermute | solution.py:45
  161.1 1.7 collective-permute-start.19
  162.9 4.9 %collective-permute-done.19 = bf16[128,768]{1,0:T(8,128)(2,1)} collective-permute-done((bf16[128,768]{1,0:T(8,128)(2,1)}, bf16[128,768]{1,0:T(8,128)(2,1)}, u32[]{:S(2)}, u32[]{:S(2)}) %collective-permute-start.19) | collective-permute-done | bytes 196640 | tf_op jit(solution)/shard_map/ppermute | solution.py:45
  167.7 2.3 copy.144
  170.1 1.7 copy.155
  171.9 2.5 fusion.59
  178.7 2.0 fusion.58
  180.9 1.5 collective-permute-start.37
  186.0 1.6 collective-permute-start.22
  188.9 3.7 %collective-permute-done.22 = bf16[128,768]{1,0:T(8,128)(2,1)S(1)} collective-permute-done((bf16[128,768]{1,0:T(8,128)(2,1)S(1)}, bf16[128,768]{1,0:T(8,128)(2,1)S(1)}, u32[]{:S(2)}, u32[]{:S(2)}) %collective-permute-start.22) | collective-permute-done | bytes 196640 | tf_op jit(solution)/shard_map/ppermute | solution.py:45
  202.6 2.7 collective-permute-done.34
  207.9 3.6 %all-to-all-start.3 = ((bf16[8,64,192]{2,1,0:T(8,128)(2,1)}), bf16[8,64,192]{2,1,0:T(8,128)(2,1)S(1)}, u32[]{:S(2)}, u32[]{:S(2)}) async-start(bf16[8,64,192]{2,1,0:T(8,128)(2,1)} %bitcast.53), calls=%async_computation.3 | async-start | bytes 524288 | tf_op jit(solution)/shard_map/all_to_all | solution.py:255
  211.5 1.6 fusion.57
  213.3 22.4 %collective-permute-done.33 = bf16[8,24,768]{2,1,0:T(8,128)(2,1)} collective-permute-done((bf16[8,24,768]{2,1,0:T(8,128)(2,1)}, bf16[8,24,768]{2,1,0:T(8,128)(2,1)}, u32[]{:S(2)}, u32[]{:S(2)}) %collective-permute-start.33) | collective-permute-done | bytes 294944 | tf_op jit(solution)/shard_map/ppermute | solution.py:45
  235.6 1.8 collective-permute-start.38
  239.5 9.5 %attend_back.1 = (bf16[512,576]{1,0:T(8,128)(2,1)}, f32[8,192]{1,0:T(8,128)}) custom-call(f32[3]{0:T(128)} %dynamic_slice.96.refs_0_, bf16[512,576]{1,0:T(8,128)(2,1)} %fusion.7.refs_1_, bf16[512,192]{1,0:T(8,128)(2,1)} %bitcast.300, f32[512,3]{1,0:T(8,128)} %get-tuple-element.48.refs_3_, f32[512,2]{1,0:T(8,128)} %copy.133.refs_2_.refs_4_, ...), custom_call_target="tpu_custom_call" | custom-call | tf_op jit(solution)/shard_map/attend_back/pallas_call | solution.py:222
  250.4 2.0 convolution_convert_fusion
  253.2 2.5 add_convert_fusion.1
  256.0 3.6 %all-to-all-start.5 = ((bf16[8,24,1536]{2,1,0:T(8,128)(2,1)}), bf16[8,24,1536]{2,1,0:T(8,128)(2,1)S(1)}, u32[]{:S(2)}, u32[]{:S(2)}) async-start(bf16[8,24,1536]{2,1,0:T(8,128)(2,1)} %add_convert_fusion.1), calls=%async_computation.5 | async-start | bytes 1179648 | tf_op jit(solution)/shard_map/all_to_all | solution.py:255
  259.5 1.9 fusion.11
  262.6 2.0 collective-permute-start.30
  268.4 8.0 %collective-permute-done.30 = bf16[2,64,768]{2,1,0:T(8,128)(2,1)S(1)} collective-permute-done((bf16[2,64,768]{2,1,0:T(8,128)(2,1)S(1)}, bf16[2,64,768]{2,1,0:T(8,128)(2,1)S(1)}, u32[]{:S(2)}, u32[]{:S(2)}) %collective-permute-start.30) | collective-permute-done | bytes 196640 | tf_op jit(solution)/shard_map/ppermute | solution.py:45
  277.1 1.6 collective-permute-done.28
  279.8 3.7 %all-to-all-start.4 = ((bf16[8,24,1352]{2,1,0:T(8,128)(2,1)}), bf16[8,24,1352]{2,1,0:T(8,128)(2,1)S(1)}, u32[]{:S(2)}, u32[]{:S(2)}) async-start(bf16[8,24,1352]{2,1,0:T(8,128)(2,1)} %pad_maximum_fusion.5), calls=%async_computation.4 | async-start | bytes 1081344 | tf_op jit(solution)/shard_map/all_to_all | solution.py:255
  283.4 1.7 bitcast_add_fusion.4
  285.1 3.0 collective-permute-start.31
  288.1 15.2 %collective-permute-done.31 = bf16[64,768]{1,0:T(8,128)(2,1)S(1)} collective-permute-done((bf16[64,768]{1,0:T(8,128)(2,1)S(1)}, bf16[64,768]{1,0:T(8,128)(2,1)S(1)}, u32[]{:S(2)}, u32[]{:S(2)}) %collective-permute-start.31) | collective-permute-done | bytes 98336 | tf_op jit(solution)/shard_map/ppermute | solution.py:45
  (314 shorter events, 85.4 us)
Async XLA Ops:
  7.2 82.4 %all-gather.6.cloned.1.call-start = ((), (), s32[]{:S(2)}) async-start(), calls=%async_computation.7 | async-start | bytes 1880064 | tf_op jit(solution)/shard_map/all_gather | solution.py:301
  11.1 13.7 %collective-permute-start.3 = (bf16[24,768]{1,0:T(8,128)(2,1)}, bf16[24,768]{1,0:T(8,128)(2,1)S(1)}, u32[]{:S(2)}, u32[]{:S(2)}) collective-permute-start(bf16[24,768]{1,0:T(8,128)(2,1)} %param.15), channel_id=1, source_target_pairs={{0,1},{1,0},{2,3},{3,2},{4,5},{5,4},{6,7},{7,6},{8,9},{9,8},{10,11... | collective-permute-start | bytes 110600 | tf_op jit(solution)/shard_map/ppermute | solution.py:45
  14.1 10.7 %collective-permute-start.4 = (bf16[24,768]{1,0:T(8,128)(2,1)}, bf16[24,768]{1,0:T(8,128)(2,1)S(1)}, u32[]{:S(2)}, u32[]{:S(2)}) collective-permute-start(bf16[24,768]{1,0:T(8,128)(2,1)} %param.15), channel_id=1, source_target_pairs={{0,2},{1,3},{2,0},{3,1},{4,6},{5,7},{6,4},{7,5},{8,10},{9,11},{10,... | collective-permute-start | bytes 110600 | tf_op jit(solution)/shard_map/ppermute | solution.py:45
  15.7 9.2 %collective-permute-start.5 = (bf16[24,768]{1,0:T(8,128)(2,1)}, bf16[24,768]{1,0:T(8,128)(2,1)S(1)}, u32[]{:S(2)}, u32[]{:S(2)}) collective-permute-start(bf16[24,768]{1,0:T(8,128)(2,1)} %param.15), channel_id=1, source_target_pairs={{0,3},{1,2},{2,1},{3,0},{4,7},{5,6},{6,5},{7,4},{8,11},{9,10},{10,... | collective-permute-start | bytes 110600 | tf_op jit(solution)/shard_map/ppermute | solution.py:45
  18.7 21.6 %all-to-all-start = ((bf16[8,24,584]{2,1,0:T(8,128)(2,1)}), bf16[8,24,584]{2,1,0:T(8,128)(2,1)S(1)}, u32[]{:S(2)}, u32[]{:S(2)}) async-start(bf16[8,24,584]{2,1,0:T(8,128)(2,1)} %pad_maximum_fusion.8), calls=%async_computation | async-start | bytes 491520 | tf_op jit(solution)/shard_map/all_to_all | solution.py:255
  24.0 91.9 %all-gather.4.cloned.1.call-start = ((), (), s32[]{:S(2)}) async-start(), calls=%async_computation.6 | async-start | bytes 1327104 | tf_op jit(solution)/shard_map/all_gather | solution.py:311
  40.3 44.2 %collective-permute-start = (bf16[8,24,584]{2,1,0:T(8,128)(2,1)S(1)}, bf16[8,24,584]{2,1,0:T(8,128)(2,1)S(1)}, u32[]{:S(2)}, u32[]{:S(2)}) collective-permute-start(bf16[8,24,584]{2,1,0:T(8,128)(2,1)S(1)} %all-to-all-done), channel_id=1, source_target_pairs={{0,1},{1,0},{2,3},{3,2},{4,5},{5,4},{6,7},{7,6},{8,9},{9,8},{10,11... | collective-permute-start | bytes 672776 | tf_op jit(solution)/shard_map/ppermute | solution.py:45
  41.8 42.8 %collective-permute-start.1 = (bf16[8,24,584]{2,1,0:T(8,128)(2,1)S(1)}, bf16[8,24,584]{2,1,0:T(8,128)(2,1)S(1)}, u32[]{:S(2)}, u32[]{:S(2)}) collective-permute-start(bf16[8,24,584]{2,1,0:T(8,128)(2,1)S(1)} %all-to-all-done), channel_id=1, source_target_pairs={{0,2},{1,3},{2,0},{3,1},{4,6},{5,7},{6,4},{7,5},{8,10},{9,11},{10,... | collective-permute-start | bytes 672776 | tf_op jit(solution)/shard_map/ppermute | solution.py:45
  43.3 41.4 %collective-permute-start.2 = (bf16[8,24,584]{2,1,0:T(8,128)(2,1)S(1)}, bf16[8,24,584]{2,1,0:T(8,128)(2,1)S(1)}, u32[]{:S(2)}, u32[]{:S(2)}) collective-permute-start(bf16[8,24,584]{2,1,0:T(8,128)(2,1)S(1)} %all-to-all-done), channel_id=1, source_target_pairs={{0,3},{1,2},{2,1},{3,0},{4,7},{5,6},{6,5},{7,4},{8,11},{9,10},{10,... | collective-permute-start | bytes 672776 | tf_op jit(solution)/shard_map/ppermute | solution.py:45
  45.4 40.6 %all-to-all-start.2 = ((bf16[8,24,1536]{2,1,0:T(8,128)(2,1)}), bf16[8,24,1536]{2,1,0:T(8,128)(2,1)S(1)}, u32[]{:S(2)}, u32[]{:S(2)}) async-start(bf16[8,24,1536]{2,1,0:T(8,128)(2,1)} %bitcast.21), calls=%async_computation.2 | async-start | bytes 1179648 | tf_op jit(solution)/shard_map/all_to_all | solution.py:255
  49.0 32.5 %collective-permute-start.9 = (bf16[96,768]{1,0:T(8,128)(2,1)}, bf16[96,768]{1,0:T(8,128)(2,1)S(1)}, u32[]{:S(2)}, u32[]{:S(2)}) collective-permute-start(bf16[96,768]{1,0:T(8,128)(2,1)} %param.17), channel_id=1, source_target_pairs={{0,16},{4,20},{8,24},{12,28},{16,0},{20,4},{24,8},{28,12},{1,17},{... | collective-permute-start | bytes 442376 | tf_op jit(solution)/shard_map/ppermute | solution.py:45
  81.5 24.4 %collective-permute-start.10 = (bf16[2,96,768]{2,1,0:T(8,128)(2,1)S(1)}, bf16[2,96,768]{2,1,0:T(8,128)(2,1)}, u32[]{:S(2)}, u32[]{:S(2)}) collective-permute-start(bf16[2,96,768]{2,1,0:T(8,128)(2,1)S(1)} %bitcast_dynamic-update-slice_fusion.12), channel_id=1, source_target_pairs={{0,1},{1,0},{2,3},{3,2},{4,5},{5,4},{6,7},{7,6},{8,9},{9,8},{10,11... | collective-permute-start | bytes 884744 | tf_op jit(solution)/shard_map/ppermute | solution.py:45
  83.0 34.6 %collective-permute-start.11 = (bf16[2,96,768]{2,1,0:T(8,128)(2,1)S(1)}, bf16[2,96,768]{2,1,0:T(8,128)(2,1)}, u32[]{:S(2)}, u32[]{:S(2)}) collective-permute-start(bf16[2,96,768]{2,1,0:T(8,128)(2,1)S(1)} %bitcast_dynamic-update-slice_fusion.12), channel_id=1, source_target_pairs={{0,2},{1,3},{2,0},{3,1},{4,6},{5,7},{6,4},{7,5},{8,10},{9,11},{10,... | collective-permute-start | bytes 884744 | tf_op jit(solution)/shard_map/ppermute | solution.py:45
  86.1 36.6 %collective-permute-start.6 = (bf16[8,24,1536]{2,1,0:T(8,128)(2,1)S(1)}, bf16[8,24,1536]{2,1,0:T(8,128)(2,1)}, u32[]{:S(2)}, u32[]{:S(2)}) collective-permute-start(bf16[8,24,1536]{2,1,0:T(8,128)(2,1)S(1)} %all-to-all-done.2), channel_id=1, source_target_pairs={{0,1},{1,0},{2,3},{3,2},{4,5},{5,4},{6,7},{7,6},{8,9},{9,8},{10,11... | collective-permute-start | bytes 1769480 | tf_op jit(solution)/shard_map/ppermute | solution.py:45
  86.6 36.3 %collective-permute-start.7 = (bf16[8,24,1536]{2,1,0:T(8,128)(2,1)S(1)}, bf16[8,24,1536]{2,1,0:T(8,128)(2,1)}, u32[]{:S(2)}, u32[]{:S(2)}) collective-permute-start(bf16[8,24,1536]{2,1,0:T(8,128)(2,1)S(1)} %all-to-all-done.2), channel_id=1, source_target_pairs={{0,2},{1,3},{2,0},{3,1},{4,6},{5,7},{6,4},{7,5},{8,10},{9,11},{10,... | collective-permute-start | bytes 1769480 | tf_op jit(solution)/shard_map/ppermute | solution.py:45
  87.2 35.8 %collective-permute-start.8 = (bf16[8,24,1536]{2,1,0:T(8,128)(2,1)S(1)}, bf16[8,24,1536]{2,1,0:T(8,128)(2,1)}, u32[]{:S(2)}, u32[]{:S(2)}) collective-permute-start(bf16[8,24,1536]{2,1,0:T(8,128)(2,1)S(1)} %all-to-all-done.2), channel_id=1, source_target_pairs={{0,3},{1,2},{2,1},{3,0},{4,7},{5,6},{6,5},{7,4},{8,11},{9,10},{10,... | collective-permute-start | bytes 1769480 | tf_op jit(solution)/shard_map/ppermute | solution.py:45
  102.4 13.1 %all-to-all-start.1 = ((bf16[8,64,192]{2,1,0:T(8,128)(2,1)}), bf16[8,64,192]{2,1,0:T(8,128)(2,1)S(1)}, u32[]{:S(2)}, u32[]{:S(2)}) async-start(bf16[8,64,192]{2,1,0:T(8,128)(2,1)} %bitcast.314), calls=%async_computation.1 | async-start | bytes 524288 | tf_op jit(solution)/shard_map/all_to_all | solution.py:255
  105.9 16.8 %collective-permute-start.12 = (bf16[2,96,768]{2,1,0:T(8,128)(2,1)S(1)}, bf16[2,96,768]{2,1,0:T(8,128)(2,1)S(1)}, u32[]{:S(2)}, u32[]{:S(2)}) collective-permute-start(bf16[2,96,768]{2,1,0:T(8,128)(2,1)S(1)} %bitcast_dynamic-update-slice_fusion.12), channel_id=1, source_target_pairs={{0,3},{1,2},{2,1},{3,0},{4,7},{5,6},{6,5},{7,4},{8,11},{9,10},{10,... | collective-permute-start | bytes 884744 | tf_op jit(solution)/shard_map/ppermute | solution.py:45
  123.4 6.2 %collective-permute-start.14 = (bf16[128,768]{1,0:T(8,128)(2,1)S(1)}, bf16[128,768]{1,0:T(8,128)(2,1)S(1)}, u32[]{:S(2)}, u32[]{:S(2)}) collective-permute-start(bf16[128,768]{1,0:T(8,128)(2,1)S(1)} %fusion.44), channel_id=1, source_target_pairs={{0,8},{4,12},{8,0},{12,4},{16,24},{20,28},{24,16},{28,20},{1,9},{5... | collective-permute-start | bytes 589832 | tf_op jit(solution)/shard_map/ppermute | solution.py:45
  123.5 6.7 %collective-permute-start.13 = (bf16[128,768]{1,0:T(8,128)(2,1)S(1)}, bf16[128,768]{1,0:T(8,128)(2,1)S(1)}, u32[]{:S(2)}, u32[]{:S(2)}) collective-permute-start(bf16[128,768]{1,0:T(8,128)(2,1)S(1)} %fusion.44), channel_id=1, source_target_pairs={{0,4},{4,0},{8,12},{12,8},{16,20},{20,16},{24,28},{28,24},{1,5},{5... | collective-permute-start | bytes 589832 | tf_op jit(solution)/shard_map/ppermute | solution.py:45
  129.6 1.6 collective-permute-start.15
  139.8 4.8 %collective-permute-start.16 = (bf16[2,128,768]{2,1,0:T(8,128)(2,1)}, bf16[2,128,768]{2,1,0:T(8,128)(2,1)}, u32[]{:S(2)}, u32[]{:S(2)}) collective-permute-start(bf16[2,128,768]{2,1,0:T(8,128)(2,1)} %pad_maximum_fusion.6), channel_id=1, source_target_pairs={{0,4},{4,0},{8,12},{12,8},{16,20},{20,16},{24,28},{28,24},{1,5},{5... | collective-permute-start | bytes 1179656 | tf_op jit(solution)/shard_map/ppermute | solution.py:45
  148.2 7.5 %collective-permute-start.17 = (bf16[128,768]{1,0:T(8,128)(2,1)}, bf16[128,768]{1,0:T(8,128)(2,1)}, u32[]{:S(2)}, u32[]{:S(2)}) collective-permute-start(bf16[128,768]{1,0:T(8,128)(2,1)} %fusion.37), channel_id=1, source_target_pairs={{0,8},{4,12},{8,0},{12,4},{16,24},{20,28},{24,16},{28,20},{1,9},{5... | collective-permute-start | bytes 589832 | tf_op jit(solution)/shard_map/ppermute | solution.py:45
  161.1 6.6 %collective-permute-start.19 = (bf16[128,768]{1,0:T(8,128)(2,1)}, bf16[128,768]{1,0:T(8,128)(2,1)}, u32[]{:S(2)}, u32[]{:S(2)}) collective-permute-start(bf16[128,768]{1,0:T(8,128)(2,1)} %convert_element_type.261), channel_id=1, source_target_pairs={{0,8},{4,12},{8,0},{12,4},{16,24},{20,28},{24,16},{28,20},{1,9},{5... | collective-permute-start | bytes 589832 | tf_op jit(solution)/shard_map/ppermute | solution.py:45
  162.9 9.0 %collective-permute-start.18 = (bf16[128,768]{1,0:T(8,128)(2,1)}, bf16[128,768]{1,0:T(8,128)(2,1)}, u32[]{:S(2)}, u32[]{:S(2)}) collective-permute-start(bf16[128,768]{1,0:T(8,128)(2,1)} %convert_element_type.261), channel_id=1, source_target_pairs={{0,4},{4,0},{8,12},{12,8},{16,20},{20,16},{24,28},{28,24},{1,5},{5... | collective-permute-start | bytes 589832 | tf_op jit(solution)/shard_map/ppermute | solution.py:45
  167.7 4.2 %collective-permute-start.20 = (bf16[128,768]{1,0:T(8,128)(2,1)}, bf16[128,768]{1,0:T(8,128)(2,1)}, u32[]{:S(2)}, u32[]{:S(2)}) collective-permute-start(bf16[128,768]{1,0:T(8,128)(2,1)} %collective-permute-done.19), channel_id=1, source_target_pairs={{0,4},{4,0},{8,12},{12,8},{16,20},{20,16},{24,28},{28,24},{1,5},{5... | collective-permute-start | bytes 589832 | tf_op jit(solution)/shard_map/ppermute | solution.py:45
  177.6 8.2 %collective-permute-start.21 = (bf16[2,128,768]{2,1,0:T(8,128)(2,1)S(1)}, bf16[2,128,768]{2,1,0:T(8,128)(2,1)S(1)}, u32[]{:S(2)}, u32[]{:S(2)}) collective-permute-start(bf16[2,128,768]{2,1,0:T(8,128)(2,1)S(1)} %pad_maximum_fusion.7), channel_id=1, source_target_pairs={{0,4},{4,0},{8,12},{12,8},{16,20},{20,16},{24,28},{28,24},{1,5},{5... | collective-permute-start | bytes 1179656 | tf_op jit(solution)/shard_map/ppermute | solution.py:45
  180.9 17.6 %collective-permute-start.37 = (bf16[2,96,768]{2,1,0:T(8,128)(2,1)S(1)}, bf16[2,96,768]{2,1,0:T(8,128)(2,1)S(1)}, u32[]{:S(2)}, u32[]{:S(2)}) collective-permute-start(bf16[2,96,768]{2,1,0:T(8,128)(2,1)S(1)} %get-tuple-element.86), channel_id=1, source_target_pairs={{0,3},{1,2},{2,1},{3,0},{4,7},{5,6},{6,5},{7,4},{8,11},{9,10},{10,... | collective-permute-start | bytes 884744 | tf_op jit(solution)/shard_map/ppermute | solution.py:45
  182.4 16.7 %collective-permute-start.36 = (bf16[2,96,768]{2,1,0:T(8,128)(2,1)S(1)}, bf16[2,96,768]{2,1,0:T(8,128)(2,1)S(1)}, u32[]{:S(2)}, u32[]{:S(2)}) collective-permute-start(bf16[2,96,768]{2,1,0:T(8,128)(2,1)S(1)} %get-tuple-element.85), channel_id=1, source_target_pairs={{0,2},{1,3},{2,0},{3,1},{4,6},{5,7},{6,4},{7,5},{8,10},{9,11},{10,... | collective-permute-start | bytes 884744 | tf_op jit(solution)/shard_map/ppermute | solution.py:45
  183.5 17.0 %collective-permute-start.35 = (bf16[2,96,768]{2,1,0:T(8,128)(2,1)S(1)}, bf16[2,96,768]{2,1,0:T(8,128)(2,1)S(1)}, u32[]{:S(2)}, u32[]{:S(2)}) collective-permute-start(bf16[2,96,768]{2,1,0:T(8,128)(2,1)S(1)} %get-tuple-element.84), channel_id=1, source_target_pairs={{0,1},{1,0},{2,3},{3,2},{4,5},{5,4},{6,7},{7,6},{8,9},{9,8},{10,11... | collective-permute-start | bytes 884744 | tf_op jit(solution)/shard_map/ppermute | solution.py:45
  186.0 6.5 %collective-permute-start.22 = (bf16[128,768]{1,0:T(8,128)(2,1)S(1)}, bf16[128,768]{1,0:T(8,128)(2,1)S(1)}, u32[]{:S(2)}, u32[]{:S(2)}) collective-permute-start(bf16[128,768]{1,0:T(8,128)(2,1)S(1)} %fusion.32), channel_id=1, source_target_pairs={{0,8},{4,12},{8,0},{12,4},{16,24},{20,28},{24,16},{28,20},{1,9},{5... | collective-permute-start | bytes 589832 | tf_op jit(solution)/shard_map/ppermute | solution.py:45
  194.4 10.8 %collective-permute-start.34 = (bf16[8,24,768]{2,1,0:T(8,128)(2,1)S(1)}, bf16[8,24,768]{2,1,0:T(8,128)(2,1)S(1)}, u32[]{:S(2)}, u32[]{:S(2)}) collective-permute-start(bf16[8,24,768]{2,1,0:T(8,128)(2,1)S(1)} %get-tuple-element.88), channel_id=1, source_target_pairs={{0,3},{1,2},{2,1},{3,0},{4,7},{5,6},{6,5},{7,4},{8,11},{9,10},{10,... | collective-permute-start | bytes 884744 | tf_op jit(solution)/shard_map/ppermute | solution.py:45
  197.0 41.7 %collective-permute-start.23 = (bf16[8,24,1536]{2,1,0:T(8,128)(2,1)}, bf16[8,24,1536]{2,1,0:T(8,128)(2,1)}, u32[]{:S(2)}, u32[]{:S(2)}) collective-permute-start(bf16[8,24,1536]{2,1,0:T(8,128)(2,1)} %get-tuple-element.82), channel_id=1, source_target_pairs={{0,1},{1,0},{2,3},{3,2},{4,5},{5,4},{6,7},{7,6},{8,9},{9,8},{10,11... | collective-permute-start | bytes 1769480 | tf_op jit(solution)/shard_map/ppermute | solution.py:45
  198.5 40.2 %collective-permute-start.24 = (bf16[8,24,1536]{2,1,0:T(8,128)(2,1)}, bf16[8,24,1536]{2,1,0:T(8,128)(2,1)}, u32[]{:S(2)}, u32[]{:S(2)}) collective-permute-start(bf16[8,24,1536]{2,1,0:T(8,128)(2,1)} %get-tuple-element.83), channel_id=1, source_target_pairs={{0,2},{1,3},{2,0},{3,1},{4,6},{5,7},{6,4},{7,5},{8,10},{9,11},{10,... | collective-permute-start | bytes 1769480 | tf_op jit(solution)/shard_map/ppermute | solution.py:45
  199.1 39.7 %collective-permute-start.25 = (bf16[8,24,1536]{2,1,0:T(8,128)(2,1)}, bf16[8,24,1536]{2,1,0:T(8,128)(2,1)}, u32[]{:S(2)}, u32[]{:S(2)}) collective-permute-start(bf16[8,24,1536]{2,1,0:T(8,128)(2,1)} %get-tuple-element.81), channel_id=1, source_target_pairs={{0,3},{1,2},{2,1},{3,0},{4,7},{5,6},{6,5},{7,4},{8,11},{9,10},{10,... | collective-permute-start | bytes 1769480 | tf_op jit(solution)/shard_map/ppermute | solution.py:45
  201.5 34.1 %collective-permute-start.33 = (bf16[8,24,768]{2,1,0:T(8,128)(2,1)}, bf16[8,24,768]{2,1,0:T(8,128)(2,1)}, u32[]{:S(2)}, u32[]{:S(2)}) collective-permute-start(bf16[8,24,768]{2,1,0:T(8,128)(2,1)} %get-tuple-element.89), channel_id=1, source_target_pairs={{0,2},{1,3},{2,0},{3,1},{4,6},{5,7},{6,4},{7,5},{8,10},{9,11},{10,... | collective-permute-start | bytes 884744 | tf_op jit(solution)/shard_map/ppermute | solution.py:45
  205.3 32.2 %collective-permute-start.32 = (bf16[8,24,768]{2,1,0:T(8,128)(2,1)}, bf16[8,24,768]{2,1,0:T(8,128)(2,1)}, u32[]{:S(2)}, u32[]{:S(2)}) collective-permute-start(bf16[8,24,768]{2,1,0:T(8,128)(2,1)} %get-tuple-element.87), channel_id=1, source_target_pairs={{0,1},{1,0},{2,3},{3,2},{4,5},{5,4},{6,7},{7,6},{8,9},{9,8},{10,11... | collective-permute-start | bytes 884744 | tf_op jit(solution)/shard_map/ppermute | solution.py:45
  207.9 30.9 %all-to-all-start.3 = ((bf16[8,64,192]{2,1,0:T(8,128)(2,1)}), bf16[8,64,192]{2,1,0:T(8,128)(2,1)S(1)}, u32[]{:S(2)}, u32[]{:S(2)}) async-start(bf16[8,64,192]{2,1,0:T(8,128)(2,1)} %bitcast.53), calls=%async_computation.3 | async-start | bytes 524288 | tf_op jit(solution)/shard_map/all_to_all | solution.py:255
  213.3 37.0 %copy-start.30 = (f32[768]{0:T(1024)S(1)}, f32[768]{0:T(1024)}, u32[]{:S(2)}) copy-start(f32[768]{0:T(1024)} %get-tuple-element.66) | copy-start | bytes 9220
  235.6 47.8 %collective-permute-start.38 = (bf16[96,768]{1,0:T(8,128)(2,1)}, bf16[96,768]{1,0:T(8,128)(2,1)}, u32[]{:S(2)}, u32[]{:S(2)}) collective-permute-start(bf16[96,768]{1,0:T(8,128)(2,1)} %fusion.57), channel_id=1, source_target_pairs={{0,16},{4,20},{8,24},{12,28},{16,0},{20,4},{24,8},{28,12},{1,17},{... | collective-permute-start | bytes 442376 | tf_op jit(solution)/shard_map/ppermute | solution.py:45
  253.2 8.3 %collective-permute-start.29 = (bf16[4,64,768]{2,1,0:T(8,128)(2,1)}, bf16[4,64,768]{2,1,0:T(8,128)(2,1)}, u32[]{:S(2)}, u32[]{:S(2)}) collective-permute-start(bf16[4,64,768]{2,1,0:T(8,128)(2,1)} %dynamic-slice_bitcast_fusion.1), channel_id=1, source_target_pairs={{0,4},{4,0},{8,12},{12,8},{16,20},{20,16},{24,28},{28,24},{1,5},{5... | collective-permute-start | bytes 1179656 | tf_op jit(solution)/shard_map/ppermute | solution.py:45
  256.0 23.8 %all-to-all-start.5 = ((bf16[8,24,1536]{2,1,0:T(8,128)(2,1)}), bf16[8,24,1536]{2,1,0:T(8,128)(2,1)S(1)}, u32[]{:S(2)}, u32[]{:S(2)}) async-start(bf16[8,24,1536]{2,1,0:T(8,128)(2,1)} %add_convert_fusion.1), calls=%async_computation.5 | async-start | bytes 1179648 | tf_op jit(solution)/shard_map/all_to_all | solution.py:255
  262.6 13.8 %collective-permute-start.30 = (bf16[2,64,768]{2,1,0:T(8,128)(2,1)S(1)}, bf16[2,64,768]{2,1,0:T(8,128)(2,1)S(1)}, u32[]{:S(2)}, u32[]{:S(2)}) collective-permute-start(bf16[2,64,768]{2,1,0:T(8,128)(2,1)S(1)} %fusion.54), channel_id=1, source_target_pairs={{0,8},{4,12},{8,0},{12,4},{16,24},{20,28},{24,16},{28,20},{1,9},{5... | collective-permute-start | bytes 589832 | tf_op jit(solution)/shard_map/ppermute | solution.py:45
  264.7 11.7 %collective-permute-start.26 = (bf16[8,24,584]{2,1,0:T(8,128)(2,1)S(1)}, bf16[8,24,584]{2,1,0:T(8,128)(2,1)S(1)}, u32[]{:S(2)}, u32[]{:S(2)}) collective-permute-start(bf16[8,24,584]{2,1,0:T(8,128)(2,1)S(1)} %get-tuple-element.91), channel_id=1, source_target_pairs={{0,1},{1,0},{2,3},{3,2},{4,5},{5,4},{6,7},{7,6},{8,9},{9,8},{10,11... | collective-permute-start | bytes 672776 | tf_op jit(solution)/shard_map/ppermute | solution.py:45
  265.9 11.2 %collective-permute-start.27 = (bf16[8,24,584]{2,1,0:T(8,128)(2,1)S(1)}, bf16[8,24,584]{2,1,0:T(8,128)(2,1)S(1)}, u32[]{:S(2)}, u32[]{:S(2)}) collective-permute-start(bf16[8,24,584]{2,1,0:T(8,128)(2,1)S(1)} %get-tuple-element.92), channel_id=1, source_target_pairs={{0,2},{1,3},{2,0},{3,1},{4,6},{5,7},{6,4},{7,5},{8,10},{9,11},{10,... | collective-permute-start | bytes 672776 | tf_op jit(solution)/shard_map/ppermute | solution.py:45
  266.9 11.8 %collective-permute-start.28 = (bf16[8,24,584]{2,1,0:T(8,128)(2,1)S(1)}, bf16[8,24,584]{2,1,0:T(8,128)(2,1)S(1)}, u32[]{:S(2)}, u32[]{:S(2)}) collective-permute-start(bf16[8,24,584]{2,1,0:T(8,128)(2,1)S(1)} %get-tuple-element.90), channel_id=1, source_target_pairs={{0,3},{1,2},{2,1},{3,0},{4,7},{5,6},{6,5},{7,4},{8,11},{9,10},{10,... | collective-permute-start | bytes 672776 | tf_op jit(solution)/shard_map/ppermute | solution.py:45
  279.8 26.3 %all-to-all-start.4 = ((bf16[8,24,1352]{2,1,0:T(8,128)(2,1)}), bf16[8,24,1352]{2,1,0:T(8,128)(2,1)S(1)}, u32[]{:S(2)}, u32[]{:S(2)}) async-start(bf16[8,24,1352]{2,1,0:T(8,128)(2,1)} %pad_maximum_fusion.5), calls=%async_computation.4 | async-start | bytes 1081344 | tf_op jit(solution)/shard_map/all_to_all | solution.py:255
  285.1 18.2 %collective-permute-start.31 = (bf16[64,768]{1,0:T(8,128)(2,1)S(1)}, bf16[64,768]{1,0:T(8,128)(2,1)S(1)}, u32[]{:S(2)}, u32[]{:S(2)}) collective-permute-start(bf16[64,768]{1,0:T(8,128)(2,1)S(1)} %fusion.61), channel_id=1, source_target_pairs={{0,16},{4,20},{8,24},{12,28},{16,0},{20,4},{24,8},{28,12},{1,17},{... | collective-permute-start | bytes 294920 | tf_op jit(solution)/shard_map/ppermute | solution.py:45
  (44 other events, 304.3 us)
Sparse Core Ops, SparseCore 0:
  11.2 34.0 all-gather.5
  47.6 33.2 all-gather.3
where the time goes:
time: 319 us; the launch traced here: 317 us
  waiting for transfers between devices  121 us (38%)
  starting transfers between devices  69.2 us (22%)
  local copies, waits for them, and re-layouts  42.4 us (13%)
  other arithmetic  33.9 us (11%)
  matrix products  18.9 us (6%)
  Pallas kernels  16.4 us (5%)
  between operations  15.3 us (5%)
    ppermute x39, waiting for transfers between devices, swap(): return lax.ppermute(value, axis, [(i, i ^ mask) for i in range(size)])  97.7 us
    ppermute x39, starting transfers between devices, swap(): return lax.ppermute(value, axis, [(i, i ^ mask) for i in range(size)])  45.9 us
    all_to_all x6, starting transfers between devices, exchange(): return lax.all_to_all(value, 'seq', 0, 0)  23.1 us
    all_to_all x6, waiting for transfers between devices, exchange(): return lax.all_to_all(value, 'seq', 0, 0)  23.1 us
    pallas_call x1, Pallas kernels, attend_back(): pl.pallas_call(lambda *refs: attend_back_kernel(heads, width, *refs), out...  9.48 us
    pallas_call x1, Pallas kernels, attend(): pl.pallas_call(lambda *refs: attend_kernel(heads, width, *refs), out_shap...  6.89 us
    dynamic_update_slice x19, local copies, waits for them, and re-layouts, put(): lax.dynamic_update_slice(buffer, jnp.expand_dims(value, axis), starts)  6.78 us
    dot_general x4, matrix products, dot(): return jnp.dot(left, right, preferred_element_type=WIDE)  6.66 us
  transfers between devices with their start and end apart: 47, of which 15 were waited for; matrix products, arithmetic and copies ran while one was open for 19% of the time, Pallas kernels for 5%

commit v1 on v0

--- a/solution.py
+++ b/solution.py
@@ -372,7 +372,8 @@
     grad_activated = dot_t(grad_mlp_rows, down_own)
     grad_gate, grad_up = geglu_back(grad_activated)
     grad_gate_up_low = jnp.concatenate([grad_gate, grad_up], axis=-1).astype(LOW)
-    grad_hidden = grad_resid_two + group_scatter(dot_t(grad_gate_up_low, gate_up_own), seq_count)
+    grad_hidden = dot_t(grad_gate_up_low, gate_up_own)
+    grad_hidden = grad_resid_two + group_scatter(grad_hidden, seq_count)
     grad_down = dot_w(activated, grad_mlp_rows)
     grad_gate_up = dot_w(hidden_rows, grad_gate_up_low)
     grad_gate_up = grad_gate_up.reshape(seq_count, dp_count, wide_rows, 2 * hidden)
@@ -389,13 +390,12 @@
     grad_attended = dot_t(grad_attn_low, out_full).astype(LOW)
     grad_out_w = dot_w(attended, grad_attn_low)
     grad_out_w = grad_out_w.reshape(seq_count, dp_count, wide_rows, D)
-    grad_out_w = scatter_by_swaps(grad_out_w, "dp", dp_count, dp_at, 1).astype(LOW)
+    grad_out_w = scatter_swaps(grad_out_w, "dp", dp_count, dp_at, 1)
 
     spread = grad_attended.reshape(sequences, seq_rows, D)
     spread = jnp.pad(spread, ((0, 0), (0, 0), (0, padded * HD - D)))
     spread = spread.reshape(sequences, seq_rows, head_groups, width).transpose(0, 2, 1, 3)
     grad_blended = exchange(spread.reshape(seq_count, seq_rows, width))
-    grad_blended, grad_gate_up = together(grad_blended, grad_gate_up)
     grad_gate_up = add_up(grad_gate_up).astype(LOW)
     grad_blended = grad_blended.reshape(length, width)
     grad_proj, totals = attend_back(
@@ -435,8 +435,8 @@
         [grad_qkv.reshape(seq_count, dp_count, wide_rows, 3 * width), grad_small], axis=-1
     )
     late = scatter_swaps(late, "dp", dp_count, dp_at, 1)
-    late, grad_rows = together(late, grad_rows)
-    late = add_up(late).astype(LOW)
+    late, grad_out_w = together(late, grad_out_w)
+    late, grad_out_w = add_up(late).astype(LOW), add_up(grad_out_w).astype(LOW)
     grad_rows = sequence_swap(grad_rows, seq_count, seq_at, sequences)
     grad_tokens = grad_resid_one + grad_rows.reshape(rows, D)
     late = jnp.concatenate([late, grad_out_w], axis=-1)

time: 319 us -> 313 us (0.981)
  other arithmetic: 33.9 us -> 29.7 us
  waiting for transfers between devices: 121 us -> 125 us
  local copies, waits for them, and re-layouts: 42.4 us -> 38.9 us
    all_to_all x6, waiting for transfers between devices: 23.1 us -> 26.9 us  [exchange(): return lax.all_to_all(value, 'seq', 0, 0)]
  transfers between devices with their start and end apart: 47 -> 47, of which waited for: 15 -> 19; matrix products, arithmetic and copies ran while one was open for 19% -> 16% of each run, Pallas kernels for 5% -> 5%
where the time goes in v1:
time: 313 us; the launch traced here: 311 us
  waiting for transfers between devices  125 us (40%)
  starting transfers between devices  68.4 us (22%)
  local copies, waits for them, and re-layouts  38.9 us (12%)
  other arithmetic  29.7 us (9%)
  matrix products  17.9 us (6%)
  Pallas kernels  16.4 us (5%)
  between operations  15.3 us (5%)
    ppermute x39, waiting for transfers between devices, swap(): return lax.ppermute(value, axis, [(i, i ^ mask) for i in range(size)])  98 us
    ppermute x39, starting transfers between devices, swap(): return lax.ppermute(value, axis, [(i, i ^ mask) for i in range(size)])  45.2 us
    all_to_all x6, waiting for transfers between devices, exchange(): return lax.all_to_all(value, 'seq', 0, 0)  26.9 us
    all_to_all x6, starting transfers between devices, exchange(): return lax.all_to_all(value, 'seq', 0, 0)  23.1 us
    pallas_call x1, Pallas kernels, attend_back(): pl.pallas_call(lambda *refs: attend_back_kernel(heads, width, *refs), out...  9.49 us
    pallas_call x1, Pallas kernels, attend(): pl.pallas_call(lambda *refs: attend_kernel(heads, width, *refs), out_shap...  6.89 us
    dynamic_update_slice x19, local copies, waits for them, and re-layouts, put(): lax.dynamic_update_slice(buffer, jnp.expand_dims(value, axis), starts)  6.78 us
    dot_general x4, matrix products, dot(): return jnp.dot(left, right, preferred_element_type=WIDE)  6.67 us
  transfers between devices with their start and end apart: 47, of which 19 were waited for; matrix products, arithmetic and copies ran while one was open for 16% of the time, Pallas kernels for 5%

profile of v1, /device:TPU:0, one launch (start us, length us, event | category | flops | bytes accessed | tf_op | source)
XLA Modules:
  0.0 311.4 jit_solution(16067525723239781177)
XLA Ops:
  9.5 1.6 pad_maximum_fusion.9
  11.1 3.0 collective-permute-start.3
  14.1 1.5 collective-permute-start.4
  18.7 5.3 %all-to-all-start = ((bf16[8,24,584]{2,1,0:T(8,128)(2,1)}), bf16[8,24,584]{2,1,0:T(8,128)(2,1)S(1)}, u32[]{:S(2)}, u32[]{:S(2)}) async-start(bf16[8,24,584]{2,1,0:T(8,128)(2,1)} %pad_maximum_fusion.8), calls=%async_computation | async-start | bytes 491520 | tf_op jit(solution)/shard_map/all_to_all | solution.py:255
  25.6 14.8 %all-to-all-done = bf16[8,24,584]{2,1,0:T(8,128)(2,1)S(1)} async-done(((bf16[8,24,584]{2,1,0:T(8,128)(2,1)}), bf16[8,24,584]{2,1,0:T(8,128)(2,1)S(1)}, u32[]{:S(2)}, u32[]{:S(2)}) %all-to-all-start) | async-done | bytes 224288 | tf_op jit(solution)/shard_map/all_to_all | solution.py:255
  45.4 3.5 %all-to-all-start.2 = ((bf16[8,24,1536]{2,1,0:T(8,128)(2,1)}), bf16[8,24,1536]{2,1,0:T(8,128)(2,1)S(1)}, u32[]{:S(2)}, u32[]{:S(2)}) async-start(bf16[8,24,1536]{2,1,0:T(8,128)(2,1)} %bitcast.21), calls=%async_computation.2 | async-start | bytes 1179648 | tf_op jit(solution)/shard_map/all_to_all | solution.py:255
  49.0 2.8 collective-permute-start.9
  52.8 28.7 %collective-permute-done.9 = bf16[96,768]{1,0:T(8,128)(2,1)S(1)} collective-permute-done((bf16[96,768]{1,0:T(8,128)(2,1)}, bf16[96,768]{1,0:T(8,128)(2,1)S(1)}, u32[]{:S(2)}, u32[]{:S(2)}) %collective-permute-start.9) | collective-permute-done | bytes 147488 | tf_op jit(solution)/shard_map/ppermute | solution.py:45
  81.5 1.5 collective-permute-start.10
  87.2 2.4 collective-permute-start.8
  92.4 1.6 fusion.7.refs_1_
  95.5 6.9 %attend.1 = (bf16[512,192]{1,0:T(8,128)(2,1)}, f32[512,3]{1,0:T(8,128)}) custom-call(f32[3]{0:T(128)} %dynamic_slice.96.refs_0_, bf16[512,576]{1,0:T(8,128)(2,1)} %fusion.7.refs_1_, f32[512,2]{1,0:T(8,128)} %copy.133.refs_2_.refs_4_, f32[2,512]{1,0:T(2,128)} %get-tuple-element.104.refs_3_.refs_5_), custom_call_target="tpu_custom_call" | custom-call | tf_op jit(solution)/shard_map/attend/pallas_call | solution.py:207
  102.4 3.4 %all-to-all-start.1 = ((bf16[8,64,192]{2,1,0:T(8,128)(2,1)}), bf16[8,64,192]{2,1,0:T(8,128)(2,1)S(1)}, u32[]{:S(2)}, u32[]{:S(2)}) async-start(bf16[8,64,192]{2,1,0:T(8,128)(2,1)} %bitcast.314), calls=%async_computation.1 | async-start | bytes 524288 | tf_op jit(solution)/shard_map/all_to_all | solution.py:255
  107.2 8.3 %all-to-all-done.1 = bf16[8,64,192]{2,1,0:T(8,128)(2,1)S(1)} async-done(((bf16[8,64,192]{2,1,0:T(8,128)(2,1)}), bf16[8,64,192]{2,1,0:T(8,128)(2,1)S(1)}, u32[]{:S(2)}, u32[]{:S(2)}) %all-to-all-start.1) | async-done | bytes 196640 | tf_op jit(solution)/shard_map/all_to_all | solution.py:255
  116.0 1.6 fusion.8
  117.6 5.0 %collective-permute-done.12 = bf16[2,96,768]{2,1,0:T(8,128)(2,1)S(1)} collective-permute-done((bf16[2,96,768]{2,1,0:T(8,128)(2,1)S(1)}, bf16[2,96,768]{2,1,0:T(8,128)(2,1)S(1)}, u32[]{:S(2)}, u32[]{:S(2)}) %collective-permute-start.12) | collective-permute-done | bytes 294944 | tf_op jit(solution)/shard_map/ppermute | solution.py:45
  132.7 4.3 %multiply_convert_fusion.1 = (bf16[512,768]{1,0:T(8,128)(2,1)S(1)}, f32[512,768]{1,0:T(8,128)}) fusion(f32[512,1536]{1,0:T(8,128)S(1)} %fusion.60), kind=kLoop, calls=%fused_computation.13 | loop fusion | flops 25952256 | bytes 5505024 | tf_op jit(solution)/shard_map/convert_element_type | solution.py:357
  137.0 2.0 fusion.84
  142.8 1.7 fusion.43
  146.5 1.7 fusion.37
  148.2 1.9 collective-permute-start.17
  152.0 3.7 %collective-permute-done.17 = bf16[128,768]{1,0:T(8,128)(2,1)} collective-permute-done((bf16[128,768]{1,0:T(8,128)(2,1)}, bf16[128,768]{1,0:T(8,128)(2,1)}, u32[]{:S(2)}, u32[]{:S(2)}) %collective-permute-start.17) | collective-permute-done | bytes 196640 | tf_op jit(solution)/shard_map/ppermute | solution.py:45
  161.1 1.7 collective-permute-start.19
  162.8 4.9 %collective-permute-done.19 = bf16[128,768]{1,0:T(8,128)(2,1)} collective-permute-done((bf16[128,768]{1,0:T(8,128)(2,1)}, bf16[128,768]{1,0:T(8,128)(2,1)}, u32[]{:S(2)}, u32[]{:S(2)}) %collective-permute-start.19) | collective-permute-done | bytes 196640 | tf_op jit(solution)/shard_map/ppermute | solution.py:45
  167.7 2.3 copy.147
  170.0 1.7 copy.153
  171.9 2.5 fusion.59
  178.7 2.0 fusion.58
  180.8 1.5 collective-permute-start.37
  186.1 1.5 collective-permute-start.34
  187.6 4.1 %collective-permute-done.37 = bf16[2,96,768]{2,1,0:T(8,128)(2,1)S(1)} collective-permute-done((bf16[2,96,768]{2,1,0:T(8,128)(2,1)S(1)}, bf16[2,96,768]{2,1,0:T(8,128)(2,1)S(1)}, u32[]{:S(2)}, u32[]{:S(2)}) %collective-permute-start.37) | collective-permute-done | bytes 294944 | tf_op jit(solution)/shard_map/ppermute | solution.py:45
  193.2 4.9 %collective-permute-done.36 = bf16[2,96,768]{2,1,0:T(8,128)(2,1)S(1)} collective-permute-done((bf16[2,96,768]{2,1,0:T(8,128)(2,1)S(1)}, bf16[2,96,768]{2,1,0:T(8,128)(2,1)S(1)}, u32[]{:S(2)}, u32[]{:S(2)}) %collective-permute-start.36) | collective-permute-done | bytes 294944 | tf_op jit(solution)/shard_map/ppermute | solution.py:45
  199.4 1.9 collective-permute-start.38
  201.9 7.0 %collective-permute-done.38 = bf16[96,768]{1,0:T(8,128)(2,1)S(1)} collective-permute-done((bf16[96,768]{1,0:T(8,128)(2,1)S(1)}, bf16[96,768]{1,0:T(8,128)(2,1)S(1)}, u32[]{:S(2)}, u32[]{:S(2)}) %collective-permute-start.38) | collective-permute-done | bytes 147488 | tf_op jit(solution)/shard_map/ppermute | solution.py:45
  210.7 12.1 %collective-permute-done.33 = bf16[8,24,1536]{2,1,0:T(8,128)(2,1)S(1)} collective-permute-done((bf16[8,24,1536]{2,1,0:T(8,128)(2,1)S(1)}, bf16[8,24,1536]{2,1,0:T(8,128)(2,1)S(1)}, u32[]{:S(2)}, u32[]{:S(2)}) %collective-permute-start.33) | collective-permute-done | bytes 589856 | tf_op jit(solution)/shard_map/ppermute | solution.py:45
  226.9 3.4 %all-to-all-start.3 = ((bf16[8,64,192]{2,1,0:T(8,128)(2,1)}), bf16[8,64,192]{2,1,0:T(8,128)(2,1)S(1)}, u32[]{:S(2)}, u32[]{:S(2)}) async-start(bf16[8,64,192]{2,1,0:T(8,128)(2,1)} %bitcast.51), calls=%async_computation.3 | async-start | bytes 524288 | tf_op jit(solution)/shard_map/all_to_all | solution.py:255
  233.7 1.5 collective-permute-start.31
  236.1 3.8 %all-to-all-done.3 = bf16[8,64,192]{2,1,0:T(8,128)(2,1)S(1)} async-done(((bf16[8,64,192]{2,1,0:T(8,128)(2,1)}), bf16[8,64,192]{2,1,0:T(8,128)(2,1)S(1)}, u32[]{:S(2)}, u32[]{:S(2)}) %all-to-all-start.3) | async-done | bytes 196640 | tf_op jit(solution)/shard_map/all_to_all | solution.py:255
  239.9 3.8 %all-to-all-start.5 = ((bf16[8,24,1536]{2,1,0:T(8,128)(2,1)}), bf16[8,24,1536]{2,1,0:T(8,128)(2,1)S(1)}, u32[]{:S(2)}, u32[]{:S(2)}) async-start(bf16[8,24,1536]{2,1,0:T(8,128)(2,1)} %fusion.11), calls=%async_computation.5 | async-start | bytes 1179648 | tf_op jit(solution)/shard_map/all_to_all | solution.py:255
  243.7 9.5 %attend_back.1 = (bf16[512,576]{1,0:T(8,128)(2,1)}, f32[8,192]{1,0:T(8,128)}) custom-call(f32[3]{0:T(128)} %dynamic_slice.96.refs_0_, bf16[512,576]{1,0:T(8,128)(2,1)} %fusion.7.refs_1_, bf16[512,192]{1,0:T(8,128)(2,1)} %bitcast.300, f32[512,3]{1,0:T(8,128)} %get-tuple-element.45.refs_3_, f32[512,2]{1,0:T(8,128)} %copy.133.refs_2_.refs_4_, ...), custom_call_target="tpu_custom_call" | custom-call | tf_op jit(solution)/shard_map/attend_back/pallas_call | solution.py:222
  254.9 2.0 fusion.14
  259.9 1.5 collective-permute-start.28
  261.7 5.1 %collective-permute-done.26 = bf16[8,24,584]{2,1,0:T(8,128)(2,1)S(1)} collective-permute-done((bf16[8,24,584]{2,1,0:T(8,128)(2,1)S(1)}, bf16[8,24,584]{2,1,0:T(8,128)(2,1)S(1)}, u32[]{:S(2)}, u32[]{:S(2)}) %collective-permute-start.26) | collective-permute-done | bytes 224288 | tf_op jit(solution)/shard_map/ppermute | solution.py:45
  267.5 4.5 %collective-permute-done.28 = bf16[8,24,584]{2,1,0:T(8,128)(2,1)S(1)} collective-permute-done((bf16[8,24,584]{2,1,0:T(8,128)(2,1)S(1)}, bf16[8,24,584]{2,1,0:T(8,128)(2,1)S(1)}, u32[]{:S(2)}, u32[]{:S(2)}) %collective-permute-start.28) | collective-permute-done | bytes 224288 | tf_op jit(solution)/shard_map/ppermute | solution.py:45
  273.5 1.7 collective-permute-start.24
  276.1 3.7 %all-to-all-start.4 = ((bf16[8,24,1352]{2,1,0:T(8,128)(2,1)}), bf16[8,24,1352]{2,1,0:T(8,128)(2,1)S(1)}, u32[]{:S(2)}, u32[]{:S(2)}) async-start(bf16[8,24,1352]{2,1,0:T(8,128)(2,1)} %pad_maximum_fusion.5), calls=%async_computation.4 | async-start | bytes 1081344 | tf_op jit(solution)/shard_map/all_to_all | solution.py:255
  279.9 3.0 collective-permute-start.25
  284.9 14.8 %collective-permute-done.25 = bf16[64,768]{1,0:T(8,128)(2,1)S(1)} collective-permute-done((bf16[64,768]{1,0:T(8,128)(2,1)S(1)}, bf16[64,768]{1,0:T(8,128)(2,1)S(1)}, u32[]{:S(2)}, u32[]{:S(2)}) %collective-permute-start.25) | collective-permute-done | bytes 98336 | tf_op jit(solution)/shard_map/ppermute | solution.py:45
  (312 shorter events, 81.9 us)
Async XLA Ops:
  7.2 82.4 %all-gather.6.cloned.1.call-start = ((), (), s32[]{:S(2)}) async-start(), calls=%async_computation.7 | async-start | bytes 1880064 | tf_op jit(solution)/shard_map/all_gather | solution.py:301
  11.1 13.7 %collective-permute-start.3 = (bf16[24,768]{1,0:T(8,128)(2,1)}, bf16[24,768]{1,0:T(8,128)(2,1)S(1)}, u32[]{:S(2)}, u32[]{:S(2)}) collective-permute-start(bf16[24,768]{1,0:T(8,128)(2,1)} %param.15), channel_id=1, source_target_pairs={{0,1},{1,0},{2,3},{3,2},{4,5},{5,4},{6,7},{7,6},{8,9},{9,8},{10,11... | collective-permute-start | bytes 110600 | tf_op jit(solution)/shard_map/ppermute | solution.py:45
  14.1 10.7 %collective-permute-start.4 = (bf16[24,768]{1,0:T(8,128)(2,1)}, bf16[24,768]{1,0:T(8,128)(2,1)S(1)}, u32[]{:S(2)}, u32[]{:S(2)}) collective-permute-start(bf16[24,768]{1,0:T(8,128)(2,1)} %param.15), channel_id=1, source_target_pairs={{0,2},{1,3},{2,0},{3,1},{4,6},{5,7},{6,4},{7,5},{8,10},{9,11},{10,... | collective-permute-start | bytes 110600 | tf_op jit(solution)/shard_map/ppermute | solution.py:45
  15.7 9.2 %collective-permute-start.5 = (bf16[24,768]{1,0:T(8,128)(2,1)}, bf16[24,768]{1,0:T(8,128)(2,1)S(1)}, u32[]{:S(2)}, u32[]{:S(2)}) collective-permute-start(bf16[24,768]{1,0:T(8,128)(2,1)} %param.15), channel_id=1, source_target_pairs={{0,3},{1,2},{2,1},{3,0},{4,7},{5,6},{6,5},{7,4},{8,11},{9,10},{10,... | collective-permute-start | bytes 110600 | tf_op jit(solution)/shard_map/ppermute | solution.py:45
  17.9 26.0 %copy-start.22 = (bf16[24,6144]{1,0:T(8,128)(2,1)S(1)}, bf16[24,6144]{1,0:T(8,128)(2,1)}, u32[]{:S(2)}) copy-start(bf16[24,6144]{1,0:T(8,128)(2,1)} %param.16) | copy-start | bytes 884740
  18.7 21.6 %all-to-all-start = ((bf16[8,24,584]{2,1,0:T(8,128)(2,1)}), bf16[8,24,584]{2,1,0:T(8,128)(2,1)S(1)}, u32[]{:S(2)}, u32[]{:S(2)}) async-start(bf16[8,24,584]{2,1,0:T(8,128)(2,1)} %pad_maximum_fusion.8), calls=%async_computation | async-start | bytes 491520 | tf_op jit(solution)/shard_map/all_to_all | solution.py:255
  24.0 91.9 %all-gather.4.cloned.1.call-start = ((), (), s32[]{:S(2)}) async-start(), calls=%async_computation.6 | async-start | bytes 1327104 | tf_op jit(solution)/shard_map/all_gather | solution.py:311
  40.3 44.2 %collective-permute-start = (bf16[8,24,584]{2,1,0:T(8,128)(2,1)S(1)}, bf16[8,24,584]{2,1,0:T(8,128)(2,1)S(1)}, u32[]{:S(2)}, u32[]{:S(2)}) collective-permute-start(bf16[8,24,584]{2,1,0:T(8,128)(2,1)S(1)} %all-to-all-done), channel_id=1, source_target_pairs={{0,1},{1,0},{2,3},{3,2},{4,5},{5,4},{6,7},{7,6},{8,9},{9,8},{10,11... | collective-permute-start | bytes 672776 | tf_op jit(solution)/shard_map/ppermute | solution.py:45
  41.8 42.8 %collective-permute-start.1 = (bf16[8,24,584]{2,1,0:T(8,128)(2,1)S(1)}, bf16[8,24,584]{2,1,0:T(8,128)(2,1)S(1)}, u32[]{:S(2)}, u32[]{:S(2)}) collective-permute-start(bf16[8,24,584]{2,1,0:T(8,128)(2,1)S(1)} %all-to-all-done), channel_id=1, source_target_pairs={{0,2},{1,3},{2,0},{3,1},{4,6},{5,7},{6,4},{7,5},{8,10},{9,11},{10,... | collective-permute-start | bytes 672776 | tf_op jit(solution)/shard_map/ppermute | solution.py:45
  43.3 41.4 %collective-permute-start.2 = (bf16[8,24,584]{2,1,0:T(8,128)(2,1)S(1)}, bf16[8,24,584]{2,1,0:T(8,128)(2,1)S(1)}, u32[]{:S(2)}, u32[]{:S(2)}) collective-permute-start(bf16[8,24,584]{2,1,0:T(8,128)(2,1)S(1)} %all-to-all-done), channel_id=1, source_target_pairs={{0,3},{1,2},{2,1},{3,0},{4,7},{5,6},{6,5},{7,4},{8,11},{9,10},{10,... | collective-permute-start | bytes 672776 | tf_op jit(solution)/shard_map/ppermute | solution.py:45
  45.4 40.6 %all-to-all-start.2 = ((bf16[8,24,1536]{2,1,0:T(8,128)(2,1)}), bf16[8,24,1536]{2,1,0:T(8,128)(2,1)S(1)}, u32[]{:S(2)}, u32[]{:S(2)}) async-start(bf16[8,24,1536]{2,1,0:T(8,128)(2,1)} %bitcast.21), calls=%async_computation.2 | async-start | bytes 1179648 | tf_op jit(solution)/shard_map/all_to_all | solution.py:255
  49.0 32.5 %collective-permute-start.9 = (bf16[96,768]{1,0:T(8,128)(2,1)}, bf16[96,768]{1,0:T(8,128)(2,1)S(1)}, u32[]{:S(2)}, u32[]{:S(2)}) collective-permute-start(bf16[96,768]{1,0:T(8,128)(2,1)} %param.17), channel_id=1, source_target_pairs={{0,16},{4,20},{8,24},{12,28},{16,0},{20,4},{24,8},{28,12},{1,17},{... | collective-permute-start | bytes 442376 | tf_op jit(solution)/shard_map/ppermute | solution.py:45
  81.5 24.4 %collective-permute-start.10 = (bf16[2,96,768]{2,1,0:T(8,128)(2,1)S(1)}, bf16[2,96,768]{2,1,0:T(8,128)(2,1)}, u32[]{:S(2)}, u32[]{:S(2)}) collective-permute-start(bf16[2,96,768]{2,1,0:T(8,128)(2,1)S(1)} %bitcast_dynamic-update-slice_fusion.12), channel_id=1, source_target_pairs={{0,1},{1,0},{2,3},{3,2},{4,5},{5,4},{6,7},{7,6},{8,9},{9,8},{10,11... | collective-permute-start | bytes 884744 | tf_op jit(solution)/shard_map/ppermute | solution.py:45
  83.0 34.6 %collective-permute-start.11 = (bf16[2,96,768]{2,1,0:T(8,128)(2,1)S(1)}, bf16[2,96,768]{2,1,0:T(8,128)(2,1)}, u32[]{:S(2)}, u32[]{:S(2)}) collective-permute-start(bf16[2,96,768]{2,1,0:T(8,128)(2,1)S(1)} %bitcast_dynamic-update-slice_fusion.12), channel_id=1, source_target_pairs={{0,2},{1,3},{2,0},{3,1},{4,6},{5,7},{6,4},{7,5},{8,10},{9,11},{10,... | collective-permute-start | bytes 884744 | tf_op jit(solution)/shard_map/ppermute | solution.py:45
  86.1 36.6 %collective-permute-start.6 = (bf16[8,24,1536]{2,1,0:T(8,128)(2,1)S(1)}, bf16[8,24,1536]{2,1,0:T(8,128)(2,1)}, u32[]{:S(2)}, u32[]{:S(2)}) collective-permute-start(bf16[8,24,1536]{2,1,0:T(8,128)(2,1)S(1)} %all-to-all-done.2), channel_id=1, source_target_pairs={{0,1},{1,0},{2,3},{3,2},{4,5},{5,4},{6,7},{7,6},{8,9},{9,8},{10,11... | collective-permute-start | bytes 1769480 | tf_op jit(solution)/shard_map/ppermute | solution.py:45
  86.6 36.3 %collective-permute-start.7 = (bf16[8,24,1536]{2,1,0:T(8,128)(2,1)S(1)}, bf16[8,24,1536]{2,1,0:T(8,128)(2,1)}, u32[]{:S(2)}, u32[]{:S(2)}) collective-permute-start(bf16[8,24,1536]{2,1,0:T(8,128)(2,1)S(1)} %all-to-all-done.2), channel_id=1, source_target_pairs={{0,2},{1,3},{2,0},{3,1},{4,6},{5,7},{6,4},{7,5},{8,10},{9,11},{10,... | collective-permute-start | bytes 1769480 | tf_op jit(solution)/shard_map/ppermute | solution.py:45
  87.2 35.8 %collective-permute-start.8 = (bf16[8,24,1536]{2,1,0:T(8,128)(2,1)S(1)}, bf16[8,24,1536]{2,1,0:T(8,128)(2,1)}, u32[]{:S(2)}, u32[]{:S(2)}) collective-permute-start(bf16[8,24,1536]{2,1,0:T(8,128)(2,1)S(1)} %all-to-all-done.2), channel_id=1, source_target_pairs={{0,3},{1,2},{2,1},{3,0},{4,7},{5,6},{6,5},{7,4},{8,11},{9,10},{10,... | collective-permute-start | bytes 1769480 | tf_op jit(solution)/shard_map/ppermute | solution.py:45
  102.4 13.1 %all-to-all-start.1 = ((bf16[8,64,192]{2,1,0:T(8,128)(2,1)}), bf16[8,64,192]{2,1,0:T(8,128)(2,1)S(1)}, u32[]{:S(2)}, u32[]{:S(2)}) async-start(bf16[8,64,192]{2,1,0:T(8,128)(2,1)} %bitcast.314), calls=%async_computation.1 | async-start | bytes 524288 | tf_op jit(solution)/shard_map/all_to_all | solution.py:255
  105.9 16.7 %collective-permute-start.12 = (bf16[2,96,768]{2,1,0:T(8,128)(2,1)S(1)}, bf16[2,96,768]{2,1,0:T(8,128)(2,1)S(1)}, u32[]{:S(2)}, u32[]{:S(2)}) collective-permute-start(bf16[2,96,768]{2,1,0:T(8,128)(2,1)S(1)} %bitcast_dynamic-update-slice_fusion.12), channel_id=1, source_target_pairs={{0,3},{1,2},{2,1},{3,0},{4,7},{5,6},{6,5},{7,4},{8,11},{9,10},{10,... | collective-permute-start | bytes 884744 | tf_op jit(solution)/shard_map/ppermute | solution.py:45
  123.4 6.2 %collective-permute-start.14 = (bf16[128,768]{1,0:T(8,128)(2,1)S(1)}, bf16[128,768]{1,0:T(8,128)(2,1)S(1)}, u32[]{:S(2)}, u32[]{:S(2)}) collective-permute-start(bf16[128,768]{1,0:T(8,128)(2,1)S(1)} %fusion.44), channel_id=1, source_target_pairs={{0,8},{4,12},{8,0},{12,4},{16,24},{20,28},{24,16},{28,20},{1,9},{5... | collective-permute-start | bytes 589832 | tf_op jit(solution)/shard_map/ppermute | solution.py:45
  123.5 6.7 %collective-permute-start.13 = (bf16[128,768]{1,0:T(8,128)(2,1)S(1)}, bf16[128,768]{1,0:T(8,128)(2,1)S(1)}, u32[]{:S(2)}, u32[]{:S(2)}) collective-permute-start(bf16[128,768]{1,0:T(8,128)(2,1)S(1)} %fusion.44), channel_id=1, source_target_pairs={{0,4},{4,0},{8,12},{12,8},{16,20},{20,16},{24,28},{28,24},{1,5},{5... | collective-permute-start | bytes 589832 | tf_op jit(solution)/shard_map/ppermute | solution.py:45
  129.6 1.6 collective-permute-start.15
  139.8 4.7 %collective-permute-start.16 = (bf16[2,128,768]{2,1,0:T(8,128)(2,1)}, bf16[2,128,768]{2,1,0:T(8,128)(2,1)}, u32[]{:S(2)}, u32[]{:S(2)}) collective-permute-start(bf16[2,128,768]{2,1,0:T(8,128)(2,1)} %pad_maximum_fusion.6), channel_id=1, source_target_pairs={{0,4},{4,0},{8,12},{12,8},{16,20},{20,16},{24,28},{28,24},{1,5},{5... | collective-permute-start | bytes 1179656 | tf_op jit(solution)/shard_map/ppermute | solution.py:45
  148.2 7.5 %collective-permute-start.17 = (bf16[128,768]{1,0:T(8,128)(2,1)}, bf16[128,768]{1,0:T(8,128)(2,1)}, u32[]{:S(2)}, u32[]{:S(2)}) collective-permute-start(bf16[128,768]{1,0:T(8,128)(2,1)} %fusion.37), channel_id=1, source_target_pairs={{0,8},{4,12},{8,0},{12,4},{16,24},{20,28},{24,16},{28,20},{1,9},{5... | collective-permute-start | bytes 589832 | tf_op jit(solution)/shard_map/ppermute | solution.py:45
  161.1 6.6 %collective-permute-start.19 = (bf16[128,768]{1,0:T(8,128)(2,1)}, bf16[128,768]{1,0:T(8,128)(2,1)}, u32[]{:S(2)}, u32[]{:S(2)}) collective-permute-start(bf16[128,768]{1,0:T(8,128)(2,1)} %convert_element_type.261), channel_id=1, source_target_pairs={{0,8},{4,12},{8,0},{12,4},{16,24},{20,28},{24,16},{28,20},{1,9},{5... | collective-permute-start | bytes 589832 | tf_op jit(solution)/shard_map/ppermute | solution.py:45
  162.8 9.0 %collective-permute-start.18 = (bf16[128,768]{1,0:T(8,128)(2,1)}, bf16[128,768]{1,0:T(8,128)(2,1)}, u32[]{:S(2)}, u32[]{:S(2)}) collective-permute-start(bf16[128,768]{1,0:T(8,128)(2,1)} %convert_element_type.261), channel_id=1, source_target_pairs={{0,4},{4,0},{8,12},{12,8},{16,20},{20,16},{24,28},{28,24},{1,5},{5... | collective-permute-start | bytes 589832 | tf_op jit(solution)/shard_map/ppermute | solution.py:45
  167.7 4.2 %collective-permute-start.20 = (bf16[128,768]{1,0:T(8,128)(2,1)}, bf16[128,768]{1,0:T(8,128)(2,1)}, u32[]{:S(2)}, u32[]{:S(2)}) collective-permute-start(bf16[128,768]{1,0:T(8,128)(2,1)} %collective-permute-done.19), channel_id=1, source_target_pairs={{0,4},{4,0},{8,12},{12,8},{16,20},{20,16},{24,28},{28,24},{1,5},{5... | collective-permute-start | bytes 589832 | tf_op jit(solution)/shard_map/ppermute | solution.py:45
  177.6 23.6 %collective-permute-start.21 = (bf16[2,128,768]{2,1,0:T(8,128)(2,1)S(1)}, bf16[2,128,768]{2,1,0:T(8,128)(2,1)S(1)}, u32[]{:S(2)}, u32[]{:S(2)}) collective-permute-start(bf16[2,128,768]{2,1,0:T(8,128)(2,1)S(1)} %pad_maximum_fusion.7), channel_id=1, source_target_pairs={{0,4},{4,0},{8,12},{12,8},{16,20},{20,16},{24,28},{28,24},{1,5},{5... | collective-permute-start | bytes 1179656 | tf_op jit(solution)/shard_map/ppermute | solution.py:45
  180.8 10.9 %collective-permute-start.37 = (bf16[2,96,768]{2,1,0:T(8,128)(2,1)S(1)}, bf16[2,96,768]{2,1,0:T(8,128)(2,1)S(1)}, u32[]{:S(2)}, u32[]{:S(2)}) collective-permute-start(bf16[2,96,768]{2,1,0:T(8,128)(2,1)S(1)} %get-tuple-element.82), channel_id=1, source_target_pairs={{0,3},{1,2},{2,1},{3,0},{4,7},{5,6},{6,5},{7,4},{8,11},{9,10},{10,... | collective-permute-start | bytes 884744 | tf_op jit(solution)/shard_map/ppermute | solution.py:45
  182.4 15.7 %collective-permute-start.36 = (bf16[2,96,768]{2,1,0:T(8,128)(2,1)S(1)}, bf16[2,96,768]{2,1,0:T(8,128)(2,1)S(1)}, u32[]{:S(2)}, u32[]{:S(2)}) collective-permute-start(bf16[2,96,768]{2,1,0:T(8,128)(2,1)S(1)} %get-tuple-element.81), channel_id=1, source_target_pairs={{0,2},{1,3},{2,0},{3,1},{4,6},{5,7},{6,4},{7,5},{8,10},{9,11},{10,... | collective-permute-start | bytes 884744 | tf_op jit(solution)/shard_map/ppermute | solution.py:45
  183.5 15.7 %collective-permute-start.35 = (bf16[2,96,768]{2,1,0:T(8,128)(2,1)S(1)}, bf16[2,96,768]{2,1,0:T(8,128)(2,1)S(1)}, u32[]{:S(2)}, u32[]{:S(2)}) collective-permute-start(bf16[2,96,768]{2,1,0:T(8,128)(2,1)S(1)} %get-tuple-element.80), channel_id=1, source_target_pairs={{0,1},{1,0},{2,3},{3,2},{4,5},{5,4},{6,7},{7,6},{8,9},{9,8},{10,11... | collective-permute-start | bytes 884744 | tf_op jit(solution)/shard_map/ppermute | solution.py:45
  186.1 24.7 %collective-permute-start.34 = (bf16[8,24,1536]{2,1,0:T(8,128)(2,1)S(1)}, bf16[8,24,1536]{2,1,0:T(8,128)(2,1)S(1)}, u32[]{:S(2)}, u32[]{:S(2)}) collective-permute-start(bf16[8,24,1536]{2,1,0:T(8,128)(2,1)S(1)} %get-tuple-element.78), channel_id=1, source_target_pairs={{0,3},{1,2},{2,1},{3,0},{4,7},{5,6},{6,5},{7,4},{8,11},{9,10},{10,... | collective-permute-start | bytes 1769480 | tf_op jit(solution)/shard_map/ppermute | solution.py:45
  191.7 31.1 %collective-permute-start.33 = (bf16[8,24,1536]{2,1,0:T(8,128)(2,1)S(1)}, bf16[8,24,1536]{2,1,0:T(8,128)(2,1)S(1)}, u32[]{:S(2)}, u32[]{:S(2)}) collective-permute-start(bf16[8,24,1536]{2,1,0:T(8,128)(2,1)S(1)} %get-tuple-element.79), channel_id=1, source_target_pairs={{0,2},{1,3},{2,0},{3,1},{4,6},{5,7},{6,4},{7,5},{8,10},{9,11},{10,... | collective-permute-start | bytes 1769480 | tf_op jit(solution)/shard_map/ppermute | solution.py:45
  198.1 24.8 %collective-permute-start.32 = (bf16[8,24,1536]{2,1,0:T(8,128)(2,1)S(1)}, bf16[8,24,1536]{2,1,0:T(8,128)(2,1)S(1)}, u32[]{:S(2)}, u32[]{:S(2)}) collective-permute-start(bf16[8,24,1536]{2,1,0:T(8,128)(2,1)S(1)} %get-tuple-element.77), channel_id=1, source_target_pairs={{0,1},{1,0},{2,3},{3,2},{4,5},{5,4},{6,7},{7,6},{8,9},{9,8},{10,11... | collective-permute-start | bytes 1769480 | tf_op jit(solution)/shard_map/ppermute | solution.py:45
  199.4 9.5 %collective-permute-start.38 = (bf16[96,768]{1,0:T(8,128)(2,1)S(1)}, bf16[96,768]{1,0:T(8,128)(2,1)S(1)}, u32[]{:S(2)}, u32[]{:S(2)}) collective-permute-start(bf16[96,768]{1,0:T(8,128)(2,1)S(1)} %fusion.57), channel_id=1, source_target_pairs={{0,16},{4,20},{8,24},{12,28},{16,0},{20,4},{24,8},{28,12},{1,17},{... | collective-permute-start | bytes 442376 | tf_op jit(solution)/shard_map/ppermute | solution.py:45
  201.3 22.7 %collective-permute-start.22 = (bf16[128,768]{1,0:T(8,128)(2,1)S(1)}, bf16[128,768]{1,0:T(8,128)(2,1)S(1)}, u32[]{:S(2)}, u32[]{:S(2)}) collective-permute-start(bf16[128,768]{1,0:T(8,128)(2,1)S(1)} %fusion.32), channel_id=1, source_target_pairs={{0,8},{4,12},{8,0},{12,4},{16,24},{20,28},{24,16},{28,20},{1,9},{5... | collective-permute-start | bytes 589832 | tf_op jit(solution)/shard_map/ppermute | solution.py:45
  226.9 13.1 %all-to-all-start.3 = ((bf16[8,64,192]{2,1,0:T(8,128)(2,1)}), bf16[8,64,192]{2,1,0:T(8,128)(2,1)S(1)}, u32[]{:S(2)}, u32[]{:S(2)}) async-start(bf16[8,64,192]{2,1,0:T(8,128)(2,1)} %bitcast.51), calls=%async_computation.3 | async-start | bytes 524288 | tf_op jit(solution)/shard_map/all_to_all | solution.py:255
  231.8 28.1 %collective-permute-start.29 = (bf16[8,24,768]{2,1,0:T(8,128)(2,1)}, bf16[8,24,768]{2,1,0:T(8,128)(2,1)S(1)}, u32[]{:S(2)}, u32[]{:S(2)}) collective-permute-start(bf16[8,24,768]{2,1,0:T(8,128)(2,1)} %get-tuple-element.84), channel_id=1, source_target_pairs={{0,1},{1,0},{2,3},{3,2},{4,5},{5,4},{6,7},{7,6},{8,9},{9,8},{10,11... | collective-permute-start | bytes 884744 | tf_op jit(solution)/shard_map/ppermute | solution.py:45
  232.8 28.8 %collective-permute-start.30 = (bf16[8,24,768]{2,1,0:T(8,128)(2,1)}, bf16[8,24,768]{2,1,0:T(8,128)(2,1)}, u32[]{:S(2)}, u32[]{:S(2)}) collective-permute-start(bf16[8,24,768]{2,1,0:T(8,128)(2,1)} %get-tuple-element.85), channel_id=1, source_target_pairs={{0,2},{1,3},{2,0},{3,1},{4,6},{5,7},{6,4},{7,5},{8,10},{9,11},{10,... | collective-permute-start | bytes 884744 | tf_op jit(solution)/shard_map/ppermute | solution.py:45
  233.7 28.0 %collective-permute-start.31 = (bf16[8,24,768]{2,1,0:T(8,128)(2,1)}, bf16[8,24,768]{2,1,0:T(8,128)(2,1)}, u32[]{:S(2)}, u32[]{:S(2)}) collective-permute-start(bf16[8,24,768]{2,1,0:T(8,128)(2,1)} %get-tuple-element.83), channel_id=1, source_target_pairs={{0,3},{1,2},{2,1},{3,0},{4,7},{5,6},{6,5},{7,4},{8,11},{9,10},{10,... | collective-permute-start | bytes 884744 | tf_op jit(solution)/shard_map/ppermute | solution.py:45
  239.9 36.2 %all-to-all-start.5 = ((bf16[8,24,1536]{2,1,0:T(8,128)(2,1)}), bf16[8,24,1536]{2,1,0:T(8,128)(2,1)S(1)}, u32[]{:S(2)}, u32[]{:S(2)}) async-start(bf16[8,24,1536]{2,1,0:T(8,128)(2,1)} %fusion.11), calls=%async_computation.5 | async-start | bytes 1179648 | tf_op jit(solution)/shard_map/all_to_all | solution.py:255
  257.9 8.9 %collective-permute-start.26 = (bf16[8,24,584]{2,1,0:T(8,128)(2,1)S(1)}, bf16[8,24,584]{2,1,0:T(8,128)(2,1)S(1)}, u32[]{:S(2)}, u32[]{:S(2)}) collective-permute-start(bf16[8,24,584]{2,1,0:T(8,128)(2,1)S(1)} %get-tuple-element.87), channel_id=1, source_target_pairs={{0,1},{1,0},{2,3},{3,2},{4,5},{5,4},{6,7},{7,6},{8,9},{9,8},{10,11... | collective-permute-start | bytes 672776 | tf_op jit(solution)/shard_map/ppermute | solution.py:45
  259.0 8.5 %collective-permute-start.27 = (bf16[8,24,584]{2,1,0:T(8,128)(2,1)S(1)}, bf16[8,24,584]{2,1,0:T(8,128)(2,1)S(1)}, u32[]{:S(2)}, u32[]{:S(2)}) collective-permute-start(bf16[8,24,584]{2,1,0:T(8,128)(2,1)S(1)} %get-tuple-element.88), channel_id=1, source_target_pairs={{0,2},{1,3},{2,0},{3,1},{4,6},{5,7},{6,4},{7,5},{8,10},{9,11},{10,... | collective-permute-start | bytes 672776 | tf_op jit(solution)/shard_map/ppermute | solution.py:45
  259.9 12.1 %collective-permute-start.28 = (bf16[8,24,584]{2,1,0:T(8,128)(2,1)S(1)}, bf16[8,24,584]{2,1,0:T(8,128)(2,1)S(1)}, u32[]{:S(2)}, u32[]{:S(2)}) collective-permute-start(bf16[8,24,584]{2,1,0:T(8,128)(2,1)S(1)} %get-tuple-element.86), channel_id=1, source_target_pairs={{0,3},{1,2},{2,1},{3,0},{4,7},{5,6},{6,5},{7,4},{8,11},{9,10},{10,... | collective-permute-start | bytes 672776 | tf_op jit(solution)/shard_map/ppermute | solution.py:45
  261.6 11.7 %collective-permute-start.23 = (bf16[4,64,768]{2,1,0:T(8,128)(2,1)S(1)}, bf16[4,64,768]{2,1,0:T(8,128)(2,1)S(1)}, u32[]{:S(2)}, u32[]{:S(2)}) collective-permute-start(bf16[4,64,768]{2,1,0:T(8,128)(2,1)S(1)} %dynamic-slice_bitcast_fusion.1), channel_id=1, source_target_pairs={{0,4},{4,0},{8,12},{12,8},{16,20},{20,16},{24,28},{28,24},{1,5},{5... | collective-permute-start | bytes 1179656 | tf_op jit(solution)/shard_map/ppermute | solution.py:45
  273.5 6.4 %collective-permute-start.24 = (bf16[2,64,768]{2,1,0:T(8,128)(2,1)S(1)}, bf16[2,64,768]{2,1,0:T(8,128)(2,1)S(1)}, u32[]{:S(2)}, u32[]{:S(2)}) collective-permute-start(bf16[2,64,768]{2,1,0:T(8,128)(2,1)S(1)} %fusion.54), channel_id=1, source_target_pairs={{0,8},{4,12},{8,0},{12,4},{16,24},{20,28},{24,16},{28,20},{1,9},{5... | collective-permute-start | bytes 589832 | tf_op jit(solution)/shard_map/ppermute | solution.py:45
  276.1 24.4 %all-to-all-start.4 = ((bf16[8,24,1352]{2,1,0:T(8,128)(2,1)}), bf16[8,24,1352]{2,1,0:T(8,128)(2,1)S(1)}, u32[]{:S(2)}, u32[]{:S(2)}) async-start(bf16[8,24,1352]{2,1,0:T(8,128)(2,1)} %pad_maximum_fusion.5), calls=%async_computation.4 | async-start | bytes 1081344 | tf_op jit(solution)/shard_map/all_to_all | solution.py:255
  279.9 19.8 %collective-permute-start.25 = (bf16[64,768]{1,0:T(8,128)(2,1)S(1)}, bf16[64,768]{1,0:T(8,128)(2,1)S(1)}, u32[]{:S(2)}, u32[]{:S(2)}) collective-permute-start(bf16[64,768]{1,0:T(8,128)(2,1)S(1)} %fusion.61), channel_id=1, source_target_pairs={{0,16},{4,20},{8,24},{12,28},{16,0},{20,4},{24,8},{28,12},{1,17},{... | collective-permute-start | bytes 294920 | tf_op jit(solution)/shard_map/ppermute | solution.py:45
  (43 other events, 290.5 us)
Sparse Core Ops, SparseCore 0:
  11.2 34.0 all-gather.5
  47.6 33.2 all-gather.3

commit v2 on v1

--- a/solution.py
+++ b/solution.py
@@ -96,13 +96,10 @@
     return jnp.concatenate([rows, partner, across, corner], axis=0)
 
 
-def group_scatter(partial, seq_count):
-    rows = partial.shape[0] // GROUP
-    blocks = partial.reshape(GROUP, rows, partial.shape[1])
-    sent = jnp.stack([blocks[1], blocks[3]]).astype(LOW)
+def group_scatter(kept, sent, seq_count):
     came = swap(sent, "seq", seq_count, 1).astype(WIDE)
-    across = swap((blocks[2] + came[1]).astype(LOW), "seq", seq_count, 2).astype(WIDE)
-    return blocks[0] + came[0] + across
+    across = swap((kept[1] + came[1]).astype(LOW), "seq", seq_count, 2).astype(WIDE)
+    return kept[0] + came[0] + across
 
 
 def sequence_reduce(blocks, seq_count, seq_at, sequences):
@@ -247,8 +244,71 @@
     return inverse * (scaled - first_mean - normed * second_mean)
 
 
-def geglu(gate_in, up_in):
-    return jax.nn.gelu(gate_in, approximate=False) * up_in
+def split_store(kept, sent, block, value):
+    if block % 2:
+        sent[block // 2] = value.astype(LOW)
+    else:
+        kept[block // 2] = value
+
+
+def mlp_kernel(hidden, rows, gate_up_own, down_own, kept, sent, activated, through_gate, through_up):
+    for block in range(GROUP):
+        here = pl.ds(block * (rows.shape[0] // GROUP), rows.shape[0] // GROUP)
+        gate_up = dot(rows[here, :], gate_up_own[...])
+        gate, up = gate_up[:, :hidden], gate_up[:, hidden:]
+        below = 0.5 * (1.0 + lax.erf(gate * math.sqrt(0.5)))
+        density = jnp.exp(-0.5 * gate * gate) * (1.0 / math.sqrt(2.0 * math.pi))
+        gelu = gate * below
+        low = (gelu * up).astype(LOW)
+        activated[here, :] = low
+        through_gate[here, :] = up * (below + gate * density)
+        through_up[here, :] = gelu
+        split_store(kept, sent, block, dot(low, down_own[...]))
+
+
+def mlp_back_kernel(
+    hidden, grads, through_gate, through_up, gate_up_own, down_own, kept, sent, grad_gate_up
+):
+    grad_activated = dot_t(grads[...], down_own[...])
+    grad_gate_up[:, :hidden] = (grad_activated * through_gate[...]).astype(LOW)
+    grad_gate_up[:, hidden:] = (grad_activated * through_up[...]).astype(LOW)
+    partial = dot_t(grad_gate_up[...], gate_up_own[...])
+    count = grads.shape[0] // GROUP
+    for block in range(GROUP):
+        split_store(kept, sent, block, partial[block * count : (block + 1) * count])
+
+
+def in_vmem(kernel, out_shape, *arrays):
+    return pl.pallas_call(
+        kernel,
+        out_shape=out_shape,
+        in_specs=[pl.BlockSpec(memory_space=pltpu.VMEM)] * len(arrays),
+        out_specs=jax.tree.map(lambda _: pl.BlockSpec(memory_space=pltpu.VMEM), out_shape),
+    )(*arrays)
+
+
+def split_shapes(count):
+    half = (GROUP // 2, count // GROUP, D)
+    return jax.ShapeDtypeStruct(half, WIDE), jax.ShapeDtypeStruct(half, LOW)
+
+
+def mlp_forward(rows, gate_up_own, down_own):
+    count, hidden = rows.shape[0], down_own.shape[0]
+    out_shape = split_shapes(count) + (
+        jax.ShapeDtypeStruct((count, hidden), LOW),
+        jax.ShapeDtypeStruct((count, hidden), WIDE),
+        jax.ShapeDtypeStruct((count, hidden), WIDE),
+    )
+    kernel = lambda *refs: mlp_kernel(hidden, *refs)
+    return in_vmem(kernel, out_shape, rows, gate_up_own, down_own)
+
+
+def mlp_backward(grads, through_gate, through_up, gate_up_own, down_own):
+    count, hidden = grads.shape[0], down_own.shape[0]
+    out_shape = split_shapes(count) + (jax.ShapeDtypeStruct((count, 2 * hidden), LOW),)
+    kernel = lambda *refs: mlp_back_kernel(hidden, *refs)
+    arrays = (grads, through_gate, through_up, gate_up_own, down_own)
+    return in_vmem(kernel, out_shape, *arrays)
 
 
 def exchange(value):
@@ -343,22 +403,25 @@
         return arrived[:, :, :D].reshape(rows, -1)
 
     attended = to_rows(blended)
+    attended, bias_parts, gain_parts = together(
+        attended, jnp.split(bias_vector, 6), jnp.split(gain_vector, 2)
+    )
     token_wide = tokens_flat.astype(WIDE)
-    resid_one = token_wide + (dot(attended, out_full) + bias_vector[2 * D : 3 * D])
+    resid_one = token_wide + (dot(attended, out_full) + bias_parts[2])
     resid_one, gate_up_pieces, down_pieces = together(resid_one, gate_up_pieces, down_pieces)
     gate_up_own = in_order(gate_up_pieces, dp_at, 1).reshape(D, 2 * hidden)
     down_own = in_order(down_pieces, dp_at, 1).reshape(hidden, D)
     hidden_one, normed_one, inverse_one = norm_forward(
-        resid_one, gain_vector[0:D], bias_vector[4 * D : 5 * D]
+        resid_one, gain_parts[0], bias_parts[4]
     )
     hidden_rows = group_gather(hidden_one.astype(LOW), seq_count)
-    gate_up = dot(hidden_rows, gate_up_own)
-    activated_wide, geglu_back = jax.vjp(geglu, gate_up[:, :hidden], gate_up[:, hidden:])
-    activated = activated_wide.astype(LOW)
-    mlp_out = group_scatter(dot(activated, down_own), seq_count)
-    resid_two = hidden_one + (mlp_out + bias_vector[3 * D : 4 * D])
+    kept, sent, activated, through_gate, through_up = mlp_forward(
+        hidden_rows, gate_up_own, down_own
+    )
+    mlp_out = group_scatter(kept, sent, seq_count)
+    resid_two = hidden_one + (mlp_out + bias_parts[3])
     normed_out, normed_two, inverse_two = norm_forward(
-        resid_two, gain_vector[D : 2 * D], bias_vector[5 * D : 6 * D]
+        resid_two, gain_parts[1], bias_parts[5]
     )
     valid_mask = padding.reshape(rows, 1).astype(WIDE)
     layer_out = (normed_out * valid_mask).astype(LOW)
@@ -366,14 +429,13 @@
     grad_final = cotangent.reshape(rows, D).astype(WIDE) * valid_mask
     grad_gain_two = jnp.sum(grad_final * normed_two, axis=0)
     grad_bias_two = jnp.sum(grad_final, axis=0)
-    grad_resid_two = norm_backward(grad_final, normed_two, inverse_two, gain_vector[D : 2 * D])
+    grad_resid_two = norm_backward(grad_final, normed_two, inverse_two, gain_parts[1])
     grad_bias_down = jnp.sum(grad_resid_two, axis=0)
     grad_mlp_rows = group_gather(grad_resid_two.astype(LOW), seq_count)
-    grad_activated = dot_t(grad_mlp_rows, down_own)
-    grad_gate, grad_up = geglu_back(grad_activated)
-    grad_gate_up_low = jnp.concatenate([grad_gate, grad_up], axis=-1).astype(LOW)
-    grad_hidden = dot_t(grad_gate_up_low, gate_up_own)
-    grad_hidden = grad_resid_two + group_scatter(grad_hidden, seq_count)
+    kept, sent, grad_gate_up_low = mlp_backward(
+        grad_mlp_rows, through_gate, through_up, gate_up_own, down_own
+    )
+    grad_hidden = grad_resid_two + group_scatter(kept, sent, seq_count)
     grad_down = dot_w(activated, grad_mlp_rows)
     grad_gate_up = dot_w(hidden_rows, grad_gate_up_low)
     grad_gate_up = grad_gate_up.reshape(seq_count, dp_count, wide_rows, 2 * hidden)
@@ -384,7 +446,7 @@
 
     grad_gain_one = jnp.sum(grad_hidden * normed_one, axis=0)
     grad_bias_one = jnp.sum(grad_hidden, axis=0)
-    grad_resid_one = norm_backward(grad_hidden, normed_one, inverse_one, gain_vector[0:D])
+    grad_resid_one = norm_backward(grad_hidden, normed_one, inverse_one, gain_parts[0])
     grad_bias_attn = jnp.sum(grad_resid_one, axis=0)
     grad_attn_low = grad_resid_one.astype(LOW)
     grad_attended = dot_t(grad_attn_low, out_full).astype(LOW)
@@ -426,8 +488,8 @@
             grad_bias_one,
             grad_bias_two,
         ]
-    ).reshape(seq_count, dp_count, bias_part)
-    grad_gains = jnp.concatenate([grad_gain_one, grad_gain_two])
+    ).astype(LOW).reshape(seq_count, dp_count, bias_part)
+    grad_gains = jnp.concatenate([grad_gain_one, grad_gain_two]).astype(LOW)
     grad_gains = grad_gains.reshape(seq_count, dp_count, gain_part)
     grad_small = jnp.concatenate([grad_biases, grad_gains], axis=-1)
     grad_small = grad_small.reshape(seq_count, dp_count, wide_rows, small_columns)

time: 313 us -> 287 us (0.917)
  waiting for transfers between devices: 125 us -> 99.4 us
  Pallas kernels: 16.4 us -> 30.3 us
  other arithmetic: 29.7 us -> 20.5 us
  matrix products: 17.9 us -> 12 us
    ppermute x39, waiting for transfers between devices: 98 us -> 56.4 us  [swap(): return lax.ppermute(value, axis, [(i, i ^ mask) for i in range(size)])]
    all_to_all x6, waiting for transfers between devices: 26.9 us -> 43 us  [exchange(): return lax.all_to_all(value, 'seq', 0, 0)]
    pallas_call x0 -> x2, Pallas kernels: none -> 13.9 us  [in_vmem(): pl.pallas_call(kernel, out_shape=out_shape, in_specs=[pl.BlockSpec(memory...]
    convert_element_type x3, other arithmetic: 6.09 us -> 0.17 us  [the longest x2 0.09 us: group_scatter(): (kept[1] + came[1]).astype(LOW)]
    dynamic_update_slice x19, local copies, waits for them, and re-layouts: 6.78 us -> 11.1 us  [put(): lax.dynamic_update_slice(buffer, jnp.expand_dims(value, axis), starts)]
    dot_general x4 -> x2, matrix products: 5.32 us -> 1.57 us  [dot_t(): lax.dot_general(left, right, (((1,), (1,)), ((), ())), preferred_element_...]
    slice x8 -> x0, local copies, waits for them, and re-layouts: 3.45 us -> none  [the longest x3 2.67 us: local(): gain_vector[D:2 * D]]
    dot_general x4 -> x2, matrix products: 6.67 us -> 4.48 us  [dot(): return jnp.dot(left, right, preferred_element_type=WIDE)]
  transfers between devices with their start and end apart: 47 -> 47, of which waited for: 19 -> 18; matrix products, arithmetic and copies ran while one was open for 16% -> 19% of each run, Pallas kernels for 5% -> 8%
where the time goes in v2:
time: 287 us; the launch traced here: 286 us
  waiting for transfers between devices  99.4 us (35%)
  starting transfers between devices  69.2 us (24%)
  local copies, waits for them, and re-layouts  39.1 us (14%)
  Pallas kernels  30.3 us (11%)
  other arithmetic  20.5 us (7%)
  between operations  15.2 us (5%)
  matrix products  12 us (4%)
    ppermute x39, waiting for transfers between devices, swap(): return lax.ppermute(value, axis, [(i, i ^ mask) for i in range(size)])  56.4 us
    ppermute x39, starting transfers between devices, swap(): return lax.ppermute(value, axis, [(i, i ^ mask) for i in range(size)])  44.5 us
    all_to_all x6, waiting for transfers between devices, exchange(): return lax.all_to_all(value, 'seq', 0, 0)  43 us
    all_to_all x6, starting transfers between devices, exchange(): return lax.all_to_all(value, 'seq', 0, 0)  24.6 us
    pallas_call x2, Pallas kernels, in_vmem(): pl.pallas_call(kernel, out_shape=out_shape, in_specs=[pl.BlockSpec(memory...  13.9 us
    dynamic_update_slice x19, local copies, waits for them, and re-layouts, put(): lax.dynamic_update_slice(buffer, jnp.expand_dims(value, axis), starts)  11.1 us
    pallas_call x1, Pallas kernels, attend_back(): pl.pallas_call(lambda *refs: attend_back_kernel(heads, width, *refs), out...  9.53 us
    pallas_call x1, Pallas kernels, attend(): pl.pallas_call(lambda *refs: attend_kernel(heads, width, *refs), out_shap...  6.89 us
  transfers between devices with their start and end apart: 47, of which 18 were waited for; matrix products, arithmetic and copies ran while one was open for 19% of the time, Pallas kernels for 8%

profile of v2, /device:TPU:0, one launch (start us, length us, event | category | flops | bytes accessed | tf_op | source)
XLA Modules:
  0.0 285.7 jit_solution(15631722276654162034)
XLA Ops:
  9.5 1.6 pad_maximum_fusion.4
  11.1 3.0 %collective-permute-start.3 = (bf16[24,768]{1,0:T(8,128)(2,1)}, bf16[24,768]{1,0:T(8,128)(2,1)S(1)}, u32[]{:S(2)}, u32[]{:S(2)}) collective-permute-start(bf16[24,768]{1,0:T(8,128)(2,1)} %param.15), channel_id=1, source_target_pairs={{0,1},{1,0},{2,3},{3,2},{4,5},{5,4},{6,7},{7,6},{8,9},{9,8},{10,11... | collective-permute-start | bytes 110600 | tf_op jit(solution)/shard_map/ppermute | solution.py:45
  14.2 1.5 collective-permute-start.4
  18.1 5.3 %all-to-all-start = ((bf16[8,24,584]{2,1,0:T(8,128)(2,1)}), bf16[8,24,584]{2,1,0:T(8,128)(2,1)S(1)}, u32[]{:S(2)}, u32[]{:S(2)}) async-start(bf16[8,24,584]{2,1,0:T(8,128)(2,1)} %pad_maximum_fusion.3), calls=%async_computation | async-start | bytes 491520 | tf_op jit(solution)/shard_map/all_to_all | solution.py:315
  24.9 14.9 %all-to-all-done = bf16[8,24,584]{2,1,0:T(8,128)(2,1)S(1)} async-done(((bf16[8,24,584]{2,1,0:T(8,128)(2,1)}), bf16[8,24,584]{2,1,0:T(8,128)(2,1)S(1)}, u32[]{:S(2)}, u32[]{:S(2)}) %all-to-all-start) | async-done | bytes 224288 | tf_op jit(solution)/shard_map/all_to_all | solution.py:315
  41.3 1.5 collective-permute-start.1
  45.0 4.2 %all-to-all-start.2 = ((bf16[8,24,1536]{2,1,0:T(8,128)(2,1)}), bf16[8,24,1536]{2,1,0:T(8,128)(2,1)S(1)}, u32[]{:S(2)}, u32[]{:S(2)}) async-start(bf16[8,24,1536]{2,1,0:T(8,128)(2,1)} %bitcast.21), calls=%async_computation.2 | async-start | bytes 1179648 | tf_op jit(solution)/shard_map/all_to_all | solution.py:315
  53.3 1.6 collective-permute-start.11
  57.4 17.6 %all-to-all-done.2 = bf16[8,24,1536]{2,1,0:T(8,128)(2,1)S(1)} async-done(((bf16[8,24,1536]{2,1,0:T(8,128)(2,1)}), bf16[8,24,1536]{2,1,0:T(8,128)(2,1)S(1)}, u32[]{:S(2)}, u32[]{:S(2)}) %all-to-all-start.2) | async-done | bytes 589856 | tf_op jit(solution)/shard_map/all_to_all | solution.py:315
  75.0 1.5 collective-permute-start.6
  76.5 1.5 collective-permute-start.7
  78.5 1.5 slice.114
  81.3 2.8 fusion.refs_1_
  85.6 6.9 %attend.1 = (bf16[512,192]{1,0:T(8,128)(2,1)}, f32[512,3]{1,0:T(8,128)}) custom-call(f32[3]{0:T(128)} %dynamic_slice.96.refs_0_, bf16[512,576]{1,0:T(8,128)(2,1)} %fusion.refs_1_, f32[512,2]{1,0:T(8,128)} %copy.172.refs_2_.refs_4_, f32[2,512]{1,0:T(2,128)} %get-tuple-element.126.refs_3_.refs_5_), custom_call_target="tpu_custom_call" | custom-call | tf_op jit(solution)/shard_map/attend/pallas_call | solution.py:204
  92.5 3.6 %all-to-all-start.1 = ((bf16[8,64,192]{2,1,0:T(8,128)(2,1)}), bf16[8,64,192]{2,1,0:T(8,128)(2,1)S(1)}, u32[]{:S(2)}, u32[]{:S(2)}) async-start(bf16[8,64,192]{2,1,0:T(8,128)(2,1)} %bitcast.288), calls=%async_computation.1 | async-start | bytes 524288 | tf_op jit(solution)/shard_map/all_to_all | solution.py:315
  96.2 2.5 collective-permute-start.12
  98.8 6.7 %all-to-all-done.1 = bf16[8,64,192]{2,1,0:T(8,128)(2,1)S(1)} async-done(((bf16[8,64,192]{2,1,0:T(8,128)(2,1)}), bf16[8,64,192]{2,1,0:T(8,128)(2,1)S(1)}, u32[]{:S(2)}, u32[]{:S(2)}) %all-to-all-start.1) | async-done | bytes 196640 | tf_op jit(solution)/shard_map/all_to_all | solution.py:315
  106.1 1.6 fusion.1
  110.6 1.7 bitcast_dynamic-update-slice_fusion.6
  112.3 1.8 bitcast_dynamic-update-slice_fusion.5
  117.8 1.9 bitcast_dynamic-update-slice_fusion.4
  122.3 6.6 %shard_map.170 = (f32[2,128,768]{2,1,0:T(8,128)}, bf16[2,128,768]{2,1,0:T(8,128)(2,1)}, bf16[512,768]{1,0:T(8,128)(2,1)}, f32[512,768]{1,0:T(8,128)}, f32[512,768]{1,0:T(8,128)}) custom-call(bf16[512,768]{1,0:T(8,128)(2,1)} %pad_maximum_fusion.refs_0_, bf16[768,1536]{1,0:T(8,128)(2,1)} %bitcast.255, bf16[768,768]{1,0:T(8,128)(2,1)} %bitcast.39.refs_2_.refs_4_), custom_call_target="tpu_custom_call" | custom-call | tf_op jit(solution)/shard_map/pallas_call | solution.py:282
  130.1 1.7 fusion.32
  131.9 2.0 collective-permute-start.17
  134.0 5.2 %collective-permute-done.17 = bf16[128,768]{1,0:T(8,128)(2,1)S(1)} collective-permute-done((bf16[128,768]{1,0:T(8,128)(2,1)S(1)}, bf16[128,768]{1,0:T(8,128)(2,1)S(1)}, u32[]{:S(2)}, u32[]{:S(2)}) %collective-permute-start.17) | collective-permute-done | bytes 196640 | tf_op jit(solution)/shard_map/ppermute | solution.py:45
  139.9 1.5 fusion.58
  141.5 1.8 collective-permute-start.19
  143.3 4.6 %collective-permute-done.19 = bf16[128,768]{1,0:T(8,128)(2,1)S(1)} collective-permute-done((bf16[128,768]{1,0:T(8,128)(2,1)S(1)}, bf16[128,768]{1,0:T(8,128)(2,1)S(1)}, u32[]{:S(2)}, u32[]{:S(2)}) %collective-permute-start.19) | collective-permute-done | bytes 196640 | tf_op jit(solution)/shard_map/ppermute | solution.py:45
  153.6 1.6 collective-permute-start.37
  156.2 7.3 %shard_map.171 = (f32[2,128,768]{2,1,0:T(8,128)}, bf16[2,128,768]{2,1,0:T(8,128)(2,1)}, bf16[512,1536]{1,0:T(8,128)(2,1)}) custom-call(bf16[512,768]{1,0:T(8,128)(2,1)} %pad_maximum_fusion.1.refs_0_, f32[512,768]{1,0:T(8,128)} %get-tuple-element.69.refs_1_, f32[512,768]{1,0:T(8,128)} %get-tuple-element.70.refs_2_, bf16[768,1536]{1,0:T(8,128)(2,1)} %bitcast.256, ...), custom_call_target="tpu_custom_call" | custom-call | tf_op jit(solution)/shard_map/pallas_call | solution.py:282
  163.5 2.8 fusion.57
  168.6 1.6 collective-permute-start.34
  171.4 3.0 %collective-permute-start.38 = (bf16[96,768]{1,0:T(8,128)(2,1)S(1)}, bf16[96,768]{1,0:T(8,128)(2,1)S(1)}, u32[]{:S(2)}, u32[]{:S(2)}) collective-permute-start(bf16[96,768]{1,0:T(8,128)(2,1)S(1)} %fusion.46), channel_id=1, source_target_pairs={{0,16},{4,20},{8,24},{12,28},{16,0},{20,4},{24,8},{28,12},{1,17},{... | collective-permute-start | bytes 442376 | tf_op jit(solution)/shard_map/ppermute | solution.py:45
  175.1 6.3 %collective-permute-done.38 = bf16[96,768]{1,0:T(8,128)(2,1)S(1)} collective-permute-done((bf16[96,768]{1,0:T(8,128)(2,1)S(1)}, bf16[96,768]{1,0:T(8,128)(2,1)S(1)}, u32[]{:S(2)}, u32[]{:S(2)}) %collective-permute-start.38) | collective-permute-done | bytes 147488 | tf_op jit(solution)/shard_map/ppermute | solution.py:45
  183.6 12.3 %collective-permute-done.34 = bf16[8,24,1536]{2,1,0:T(8,128)(2,1)S(1)} collective-permute-done((bf16[8,24,1536]{2,1,0:T(8,128)(2,1)S(1)}, bf16[8,24,1536]{2,1,0:T(8,128)(2,1)S(1)}, u32[]{:S(2)}, u32[]{:S(2)}) %collective-permute-start.34) | collective-permute-done | bytes 589856 | tf_op jit(solution)/shard_map/ppermute | solution.py:45
  200.1 4.3 %all-to-all-start.3 = ((bf16[8,64,192]{2,1,0:T(8,128)(2,1)}), bf16[8,64,192]{2,1,0:T(8,128)(2,1)S(1)}, u32[]{:S(2)}, u32[]{:S(2)}) async-start(bf16[8,64,192]{2,1,0:T(8,128)(2,1)} %bitcast.47), calls=%async_computation.3 | async-start | bytes 524288 | tf_op jit(solution)/shard_map/all_to_all | solution.py:315
  206.6 1.5 collective-permute-start.30
  210.3 3.8 %all-to-all-done.3 = bf16[8,64,192]{2,1,0:T(8,128)(2,1)S(1)} async-done(((bf16[8,64,192]{2,1,0:T(8,128)(2,1)}), bf16[8,64,192]{2,1,0:T(8,128)(2,1)S(1)}, u32[]{:S(2)}, u32[]{:S(2)}) %all-to-all-start.3) | async-done | bytes 196640 | tf_op jit(solution)/shard_map/all_to_all | solution.py:315
  214.1 3.5 %all-to-all-start.5 = ((bf16[8,24,1536]{2,1,0:T(8,128)(2,1)}), bf16[8,24,1536]{2,1,0:T(8,128)(2,1)S(1)}, u32[]{:S(2)}, u32[]{:S(2)}) async-start(bf16[8,24,1536]{2,1,0:T(8,128)(2,1)} %fusion.4), calls=%async_computation.5 | async-start | bytes 1179648 | tf_op jit(solution)/shard_map/all_to_all | solution.py:315
  217.7 9.5 %attend_back.1 = (bf16[512,576]{1,0:T(8,128)(2,1)}, f32[8,192]{1,0:T(8,128)}) custom-call(f32[3]{0:T(128)} %dynamic_slice.96.refs_0_, bf16[512,576]{1,0:T(8,128)(2,1)} %fusion.refs_1_, bf16[512,192]{1,0:T(8,128)(2,1)} %bitcast.275, f32[512,3]{1,0:T(8,128)} %get-tuple-element.73.refs_3_, f32[512,2]{1,0:T(8,128)} %copy.172.refs_2_.refs_4_, ...), custom_call_target="tpu_custom_call" | custom-call | tf_op jit(solution)/shard_map/attend_back/pallas_call | solution.py:219
  230.0 1.9 fusion.5
  232.9 1.5 collective-permute-start.27
  236.8 4.2 %collective-permute-done.26 = bf16[8,24,584]{2,1,0:T(8,128)(2,1)S(1)} collective-permute-done((bf16[8,24,584]{2,1,0:T(8,128)(2,1)S(1)}, bf16[8,24,584]{2,1,0:T(8,128)(2,1)S(1)}, u32[]{:S(2)}, u32[]{:S(2)}) %collective-permute-start.26) | collective-permute-done | bytes 224288 | tf_op jit(solution)/shard_map/ppermute | solution.py:45
  240.9 5.2 %collective-permute-done.27 = bf16[8,24,584]{2,1,0:T(8,128)(2,1)S(1)} collective-permute-done((bf16[8,24,584]{2,1,0:T(8,128)(2,1)S(1)}, bf16[8,24,584]{2,1,0:T(8,128)(2,1)S(1)}, u32[]{:S(2)}, u32[]{:S(2)}) %collective-permute-start.27) | collective-permute-done | bytes 224288 | tf_op jit(solution)/shard_map/ppermute | solution.py:45
  247.7 1.7 collective-permute-start.24
  250.4 3.7 %all-to-all-start.4 = ((bf16[8,24,1352]{2,1,0:T(8,128)(2,1)}), bf16[8,24,1352]{2,1,0:T(8,128)(2,1)S(1)}, u32[]{:S(2)}, u32[]{:S(2)}) async-start(bf16[8,24,1352]{2,1,0:T(8,128)(2,1)} %pad_maximum_fusion.2), calls=%async_computation.4 | async-start | bytes 1081344 | tf_op jit(solution)/shard_map/all_to_all | solution.py:315
  254.2 3.0 %collective-permute-start.25 = (bf16[64,768]{1,0:T(8,128)(2,1)S(1)}, bf16[64,768]{1,0:T(8,128)(2,1)S(1)}, u32[]{:S(2)}, u32[]{:S(2)}) collective-permute-start(bf16[64,768]{1,0:T(8,128)(2,1)S(1)} %fusion.47), channel_id=1, source_target_pairs={{0,16},{4,20},{8,24},{12,28},{16,0},{20,4},{24,8},{28,12},{1,17},{... | collective-permute-start | bytes 294920 | tf_op jit(solution)/shard_map/ppermute | solution.py:45
  259.2 14.8 %collective-permute-done.25 = bf16[64,768]{1,0:T(8,128)(2,1)S(1)} collective-permute-done((bf16[64,768]{1,0:T(8,128)(2,1)S(1)}, bf16[64,768]{1,0:T(8,128)(2,1)S(1)}, u32[]{:S(2)}, u32[]{:S(2)}) %collective-permute-start.25) | collective-permute-done | bytes 98336 | tf_op jit(solution)/shard_map/ppermute | solution.py:45
  (308 shorter events, 68.3 us)
Async XLA Ops:
  7.2 71.3 %all-gather.6.cloned.1.call-start = ((), (), s32[]{:S(2)}) async-start(), calls=%async_computation.7 | async-start | bytes 1880064 | tf_op jit(solution)/shard_map/all_gather | solution.py:361
  11.1 13.0 %collective-permute-start.3 = (bf16[24,768]{1,0:T(8,128)(2,1)}, bf16[24,768]{1,0:T(8,128)(2,1)S(1)}, u32[]{:S(2)}, u32[]{:S(2)}) collective-permute-start(bf16[24,768]{1,0:T(8,128)(2,1)} %param.15), channel_id=1, source_target_pairs={{0,1},{1,0},{2,3},{3,2},{4,5},{5,4},{6,7},{7,6},{8,9},{9,8},{10,11... | collective-permute-start | bytes 110600 | tf_op jit(solution)/shard_map/ppermute | solution.py:45
  14.2 10.0 %collective-permute-start.4 = (bf16[24,768]{1,0:T(8,128)(2,1)}, bf16[24,768]{1,0:T(8,128)(2,1)S(1)}, u32[]{:S(2)}, u32[]{:S(2)}) collective-permute-start(bf16[24,768]{1,0:T(8,128)(2,1)} %param.15), channel_id=1, source_target_pairs={{0,2},{1,3},{2,0},{3,1},{4,6},{5,7},{6,4},{7,5},{8,10},{9,11},{10,... | collective-permute-start | bytes 110600 | tf_op jit(solution)/shard_map/ppermute | solution.py:45
  15.7 8.5 %collective-permute-start.5 = (bf16[24,768]{1,0:T(8,128)(2,1)}, bf16[24,768]{1,0:T(8,128)(2,1)S(1)}, u32[]{:S(2)}, u32[]{:S(2)}) collective-permute-start(bf16[24,768]{1,0:T(8,128)(2,1)} %param.15), channel_id=1, source_target_pairs={{0,3},{1,2},{2,1},{3,0},{4,7},{5,6},{6,5},{7,4},{8,11},{9,10},{10,... | collective-permute-start | bytes 110600 | tf_op jit(solution)/shard_map/ppermute | solution.py:45
  17.3 26.3 %copy-start.19 = (bf16[24,6144]{1,0:T(8,128)(2,1)S(1)}, bf16[24,6144]{1,0:T(8,128)(2,1)}, u32[]{:S(2)}) copy-start(bf16[24,6144]{1,0:T(8,128)(2,1)} %param.16) | copy-start | bytes 884740
  18.1 21.8 %all-to-all-start = ((bf16[8,24,584]{2,1,0:T(8,128)(2,1)}), bf16[8,24,584]{2,1,0:T(8,128)(2,1)S(1)}, u32[]{:S(2)}, u32[]{:S(2)}) async-start(bf16[8,24,584]{2,1,0:T(8,128)(2,1)} %pad_maximum_fusion.3), calls=%async_computation | async-start | bytes 491520 | tf_op jit(solution)/shard_map/all_to_all | solution.py:315
  23.4 82.6 %all-gather.4.cloned.1.call-start = ((), (), s32[]{:S(2)}) async-start(), calls=%async_computation.6 | async-start | bytes 1327104 | tf_op jit(solution)/shard_map/all_gather | solution.py:371
  39.8 15.1 %collective-permute-start = (bf16[8,24,584]{2,1,0:T(8,128)(2,1)S(1)}, bf16[8,24,584]{2,1,0:T(8,128)(2,1)S(1)}, u32[]{:S(2)}, u32[]{:S(2)}) collective-permute-start(bf16[8,24,584]{2,1,0:T(8,128)(2,1)S(1)} %all-to-all-done), channel_id=1, source_target_pairs={{0,1},{1,0},{2,3},{3,2},{4,5},{5,4},{6,7},{7,6},{8,9},{9,8},{10,11... | collective-permute-start | bytes 672776 | tf_op jit(solution)/shard_map/ppermute | solution.py:45
  41.3 13.6 %collective-permute-start.1 = (bf16[8,24,584]{2,1,0:T(8,128)(2,1)S(1)}, bf16[8,24,584]{2,1,0:T(8,128)(2,1)S(1)}, u32[]{:S(2)}, u32[]{:S(2)}) collective-permute-start(bf16[8,24,584]{2,1,0:T(8,128)(2,1)S(1)} %all-to-all-done), channel_id=1, source_target_pairs={{0,2},{1,3},{2,0},{3,1},{4,6},{5,7},{6,4},{7,5},{8,10},{9,11},{10,... | collective-permute-start | bytes 672776 | tf_op jit(solution)/shard_map/ppermute | solution.py:45
  42.8 12.2 %collective-permute-start.2 = (bf16[8,24,584]{2,1,0:T(8,128)(2,1)S(1)}, bf16[8,24,584]{2,1,0:T(8,128)(2,1)S(1)}, u32[]{:S(2)}, u32[]{:S(2)}) collective-permute-start(bf16[8,24,584]{2,1,0:T(8,128)(2,1)S(1)} %all-to-all-done), channel_id=1, source_target_pairs={{0,3},{1,2},{2,1},{3,0},{4,7},{5,6},{6,5},{7,4},{8,11},{9,10},{10,... | collective-permute-start | bytes 672776 | tf_op jit(solution)/shard_map/ppermute | solution.py:45
  43.5 7.8 %collective-permute-start.9 = (bf16[96,768]{1,0:T(8,128)(2,1)S(1)}, bf16[96,768]{1,0:T(8,128)(2,1)S(1)}, u32[]{:S(2)}, u32[]{:S(2)}) collective-permute-start(bf16[96,768]{1,0:T(8,128)(2,1)S(1)} %copy-done.28), channel_id=1, source_target_pairs={{0,16},{4,20},{8,24},{12,28},{16,0},{20,4},{24,8},{28,12},{1,17},{... | collective-permute-start | bytes 442376 | tf_op jit(solution)/shard_map/ppermute | solution.py:45
  45.0 30.0 %all-to-all-start.2 = ((bf16[8,24,1536]{2,1,0:T(8,128)(2,1)}), bf16[8,24,1536]{2,1,0:T(8,128)(2,1)S(1)}, u32[]{:S(2)}, u32[]{:S(2)}) async-start(bf16[8,24,1536]{2,1,0:T(8,128)(2,1)} %bitcast.21), calls=%async_computation.2 | async-start | bytes 1179648 | tf_op jit(solution)/shard_map/all_to_all | solution.py:315
  51.9 44.3 %collective-permute-start.10 = (bf16[2,96,768]{2,1,0:T(8,128)(2,1)}, bf16[2,96,768]{2,1,0:T(8,128)(2,1)}, u32[]{:S(2)}, u32[]{:S(2)}) collective-permute-start(bf16[2,96,768]{2,1,0:T(8,128)(2,1)} %bitcast_dynamic-update-slice_fusion.12), channel_id=1, source_target_pairs={{0,1},{1,0},{2,3},{3,2},{4,5},{5,4},{6,7},{7,6},{8,9},{9,8},{10,11... | collective-permute-start | bytes 884744 | tf_op jit(solution)/shard_map/ppermute | solution.py:45
  53.3 54.4 %collective-permute-start.11 = (bf16[2,96,768]{2,1,0:T(8,128)(2,1)}, bf16[2,96,768]{2,1,0:T(8,128)(2,1)}, u32[]{:S(2)}, u32[]{:S(2)}) collective-permute-start(bf16[2,96,768]{2,1,0:T(8,128)(2,1)} %bitcast_dynamic-update-slice_fusion.12), channel_id=1, source_target_pairs={{0,2},{1,3},{2,0},{3,1},{4,6},{5,7},{6,4},{7,5},{8,10},{9,11},{10,... | collective-permute-start | bytes 884744 | tf_op jit(solution)/shard_map/ppermute | solution.py:45
  75.0 33.6 %collective-permute-start.6 = (bf16[8,24,1536]{2,1,0:T(8,128)(2,1)S(1)}, bf16[8,24,1536]{2,1,0:T(8,128)(2,1)}, u32[]{:S(2)}, u32[]{:S(2)}) collective-permute-start(bf16[8,24,1536]{2,1,0:T(8,128)(2,1)S(1)} %all-to-all-done.2), channel_id=1, source_target_pairs={{0,1},{1,0},{2,3},{3,2},{4,5},{5,4},{6,7},{7,6},{8,9},{9,8},{10,11... | collective-permute-start | bytes 1769480 | tf_op jit(solution)/shard_map/ppermute | solution.py:45
  76.5 32.3 %collective-permute-start.7 = (bf16[8,24,1536]{2,1,0:T(8,128)(2,1)S(1)}, bf16[8,24,1536]{2,1,0:T(8,128)(2,1)}, u32[]{:S(2)}, u32[]{:S(2)}) collective-permute-start(bf16[8,24,1536]{2,1,0:T(8,128)(2,1)S(1)} %all-to-all-done.2), channel_id=1, source_target_pairs={{0,2},{1,3},{2,0},{3,1},{4,6},{5,7},{6,4},{7,5},{8,10},{9,11},{10,... | collective-permute-start | bytes 1769480 | tf_op jit(solution)/shard_map/ppermute | solution.py:45
  78.0 30.8 %collective-permute-start.8 = (bf16[8,24,1536]{2,1,0:T(8,128)(2,1)S(1)}, bf16[8,24,1536]{2,1,0:T(8,128)(2,1)}, u32[]{:S(2)}, u32[]{:S(2)}) collective-permute-start(bf16[8,24,1536]{2,1,0:T(8,128)(2,1)S(1)} %all-to-all-done.2), channel_id=1, source_target_pairs={{0,3},{1,2},{2,1},{3,0},{4,7},{5,6},{6,5},{7,4},{8,11},{9,10},{10,... | collective-permute-start | bytes 1769480 | tf_op jit(solution)/shard_map/ppermute | solution.py:45
  92.5 13.1 %all-to-all-start.1 = ((bf16[8,64,192]{2,1,0:T(8,128)(2,1)}), bf16[8,64,192]{2,1,0:T(8,128)(2,1)S(1)}, u32[]{:S(2)}, u32[]{:S(2)}) async-start(bf16[8,64,192]{2,1,0:T(8,128)(2,1)} %bitcast.288), calls=%async_computation.1 | async-start | bytes 524288 | tf_op jit(solution)/shard_map/all_to_all | solution.py:315
  96.2 12.4 %collective-permute-start.12 = (bf16[2,96,768]{2,1,0:T(8,128)(2,1)}, bf16[2,96,768]{2,1,0:T(8,128)(2,1)S(1)}, u32[]{:S(2)}, u32[]{:S(2)}) collective-permute-start(bf16[2,96,768]{2,1,0:T(8,128)(2,1)} %bitcast_dynamic-update-slice_fusion.12), channel_id=1, source_target_pairs={{0,3},{1,2},{2,1},{3,0},{4,7},{5,6},{6,5},{7,4},{8,11},{9,10},{10,... | collective-permute-start | bytes 884744 | tf_op jit(solution)/shard_map/ppermute | solution.py:45
  109.3 10.4 %collective-permute-start.14 = (bf16[128,768]{1,0:T(8,128)(2,1)S(1)}, bf16[128,768]{1,0:T(8,128)(2,1)S(1)}, u32[]{:S(2)}, u32[]{:S(2)}) collective-permute-start(bf16[128,768]{1,0:T(8,128)(2,1)S(1)} %fusion.33), channel_id=1, source_target_pairs={{0,8},{4,12},{8,0},{12,4},{16,24},{20,28},{24,16},{28,20},{1,9},{5... | collective-permute-start | bytes 589832 | tf_op jit(solution)/shard_map/ppermute | solution.py:45
  109.5 11.5 %collective-permute-start.13 = (bf16[128,768]{1,0:T(8,128)(2,1)S(1)}, bf16[128,768]{1,0:T(8,128)(2,1)S(1)}, u32[]{:S(2)}, u32[]{:S(2)}) collective-permute-start(bf16[128,768]{1,0:T(8,128)(2,1)S(1)} %fusion.33), channel_id=1, source_target_pairs={{0,4},{4,0},{8,12},{12,8},{16,20},{20,16},{24,28},{28,24},{1,5},{5... | collective-permute-start | bytes 589832 | tf_op jit(solution)/shard_map/ppermute | solution.py:45
  119.7 1.6 collective-permute-start.15
  128.9 2.9 %collective-permute-start.16 = (bf16[2,128,768]{2,1,0:T(8,128)(2,1)}, bf16[2,128,768]{2,1,0:T(8,128)(2,1)S(1)}, u32[]{:S(2)}, u32[]{:S(2)}) collective-permute-start(bf16[2,128,768]{2,1,0:T(8,128)(2,1)} %get-tuple-element.65), channel_id=1, source_target_pairs={{0,4},{4,0},{8,12},{12,8},{16,20},{20,16},{24,28},{28,24},{1,5},{5... | collective-permute-start | bytes 1179656 | tf_op jit(solution)/shard_map/ppermute | solution.py:45
  131.9 7.3 %collective-permute-start.17 = (bf16[128,768]{1,0:T(8,128)(2,1)S(1)}, bf16[128,768]{1,0:T(8,128)(2,1)S(1)}, u32[]{:S(2)}, u32[]{:S(2)}) collective-permute-start(bf16[128,768]{1,0:T(8,128)(2,1)S(1)} %fusion.44), channel_id=1, source_target_pairs={{0,8},{4,12},{8,0},{12,4},{16,24},{20,28},{24,16},{28,20},{1,9},{5... | collective-permute-start | bytes 589832 | tf_op jit(solution)/shard_map/ppermute | solution.py:45
  141.5 6.4 %collective-permute-start.19 = (bf16[128,768]{1,0:T(8,128)(2,1)S(1)}, bf16[128,768]{1,0:T(8,128)(2,1)S(1)}, u32[]{:S(2)}, u32[]{:S(2)}) collective-permute-start(bf16[128,768]{1,0:T(8,128)(2,1)S(1)} %convert_element_type.274), channel_id=1, source_target_pairs={{0,8},{4,12},{8,0},{12,4},{16,24},{20,28},{24,16},{28,20},{1,9},{5... | collective-permute-start | bytes 589832 | tf_op jit(solution)/shard_map/ppermute | solution.py:45
  143.3 5.9 %collective-permute-start.18 = (bf16[128,768]{1,0:T(8,128)(2,1)S(1)}, bf16[128,768]{1,0:T(8,128)(2,1)S(1)}, u32[]{:S(2)}, u32[]{:S(2)}) collective-permute-start(bf16[128,768]{1,0:T(8,128)(2,1)S(1)} %convert_element_type.274), channel_id=1, source_target_pairs={{0,4},{4,0},{8,12},{12,8},{16,20},{20,16},{24,28},{28,24},{1,5},{5... | collective-permute-start | bytes 589832 | tf_op jit(solution)/shard_map/ppermute | solution.py:45
  147.9 1.4 collective-permute-start.20
  151.7 16.1 %collective-permute-start.35 = (bf16[2,96,768]{2,1,0:T(8,128)(2,1)S(1)}, bf16[2,96,768]{2,1,0:T(8,128)(2,1)S(1)}, u32[]{:S(2)}, u32[]{:S(2)}) collective-permute-start(bf16[2,96,768]{2,1,0:T(8,128)(2,1)S(1)} %get-tuple-element.106), channel_id=1, source_target_pairs={{0,1},{1,0},{2,3},{3,2},{4,5},{5,4},{6,7},{7,6},{8,9},{9,8},{10,11... | collective-permute-start | bytes 884744 | tf_op jit(solution)/shard_map/ppermute | solution.py:45
  152.9 15.7 %collective-permute-start.36 = (bf16[2,96,768]{2,1,0:T(8,128)(2,1)S(1)}, bf16[2,96,768]{2,1,0:T(8,128)(2,1)S(1)}, u32[]{:S(2)}, u32[]{:S(2)}) collective-permute-start(bf16[2,96,768]{2,1,0:T(8,128)(2,1)S(1)} %get-tuple-element.107), channel_id=1, source_target_pairs={{0,2},{1,3},{2,0},{3,1},{4,6},{5,7},{6,4},{7,5},{8,10},{9,11},{10,... | collective-permute-start | bytes 884744 | tf_op jit(solution)/shard_map/ppermute | solution.py:45
  153.6 16.5 %collective-permute-start.37 = (bf16[2,96,768]{2,1,0:T(8,128)(2,1)S(1)}, bf16[2,96,768]{2,1,0:T(8,128)(2,1)S(1)}, u32[]{:S(2)}, u32[]{:S(2)}) collective-permute-start(bf16[2,96,768]{2,1,0:T(8,128)(2,1)S(1)} %get-tuple-element.108), channel_id=1, source_target_pairs={{0,3},{1,2},{2,1},{3,0},{4,7},{5,6},{6,5},{7,4},{8,11},{9,10},{10,... | collective-permute-start | bytes 884744 | tf_op jit(solution)/shard_map/ppermute | solution.py:45
  163.5 10.9 %collective-permute-start.21 = (bf16[2,128,768]{2,1,0:T(8,128)(2,1)}, bf16[2,128,768]{2,1,0:T(8,128)(2,1)S(1)}, u32[]{:S(2)}, u32[]{:S(2)}) collective-permute-start(bf16[2,128,768]{2,1,0:T(8,128)(2,1)} %get-tuple-element.72), channel_id=1, source_target_pairs={{0,4},{4,0},{8,12},{12,8},{16,20},{20,16},{24,28},{28,24},{1,5},{5... | collective-permute-start | bytes 1179656 | tf_op jit(solution)/shard_map/ppermute | solution.py:45
  166.6 16.3 %collective-permute-start.32 = (bf16[8,24,1536]{2,1,0:T(8,128)(2,1)S(1)}, bf16[8,24,1536]{2,1,0:T(8,128)(2,1)S(1)}, u32[]{:S(2)}, u32[]{:S(2)}) collective-permute-start(bf16[8,24,1536]{2,1,0:T(8,128)(2,1)S(1)} %get-tuple-element.103), channel_id=1, source_target_pairs={{0,1},{1,0},{2,3},{3,2},{4,5},{5,4},{6,7},{7,6},{8,9},{9,8},{10,11... | collective-permute-start | bytes 1769480 | tf_op jit(solution)/shard_map/ppermute | solution.py:45
  167.8 15.8 %collective-permute-start.33 = (bf16[8,24,1536]{2,1,0:T(8,128)(2,1)S(1)}, bf16[8,24,1536]{2,1,0:T(8,128)(2,1)S(1)}, u32[]{:S(2)}, u32[]{:S(2)}) collective-permute-start(bf16[8,24,1536]{2,1,0:T(8,128)(2,1)S(1)} %get-tuple-element.105), channel_id=1, source_target_pairs={{0,2},{1,3},{2,0},{3,1},{4,6},{5,7},{6,4},{7,5},{8,10},{9,11},{10,... | collective-permute-start | bytes 1769480 | tf_op jit(solution)/shard_map/ppermute | solution.py:45
  168.6 27.4 %collective-permute-start.34 = (bf16[8,24,1536]{2,1,0:T(8,128)(2,1)S(1)}, bf16[8,24,1536]{2,1,0:T(8,128)(2,1)S(1)}, u32[]{:S(2)}, u32[]{:S(2)}) collective-permute-start(bf16[8,24,1536]{2,1,0:T(8,128)(2,1)S(1)} %get-tuple-element.104), channel_id=1, source_target_pairs={{0,3},{1,2},{2,1},{3,0},{4,7},{5,6},{6,5},{7,4},{8,11},{9,10},{10,... | collective-permute-start | bytes 1769480 | tf_op jit(solution)/shard_map/ppermute | solution.py:45
  171.4 10.0 %collective-permute-start.38 = (bf16[96,768]{1,0:T(8,128)(2,1)S(1)}, bf16[96,768]{1,0:T(8,128)(2,1)S(1)}, u32[]{:S(2)}, u32[]{:S(2)}) collective-permute-start(bf16[96,768]{1,0:T(8,128)(2,1)S(1)} %fusion.46), channel_id=1, source_target_pairs={{0,16},{4,20},{8,24},{12,28},{16,0},{20,4},{24,8},{28,12},{1,17},{... | collective-permute-start | bytes 442376 | tf_op jit(solution)/shard_map/ppermute | solution.py:45
  174.5 22.6 %collective-permute-start.22 = (bf16[128,768]{1,0:T(8,128)(2,1)S(1)}, bf16[128,768]{1,0:T(8,128)(2,1)S(1)}, u32[]{:S(2)}, u32[]{:S(2)}) collective-permute-start(bf16[128,768]{1,0:T(8,128)(2,1)S(1)} %fusion.45), channel_id=1, source_target_pairs={{0,8},{4,12},{8,0},{12,4},{16,24},{20,28},{24,16},{28,20},{1,9},{5... | collective-permute-start | bytes 589832 | tf_op jit(solution)/shard_map/ppermute | solution.py:45
  200.1 14.0 %all-to-all-start.3 = ((bf16[8,64,192]{2,1,0:T(8,128)(2,1)}), bf16[8,64,192]{2,1,0:T(8,128)(2,1)S(1)}, u32[]{:S(2)}, u32[]{:S(2)}) async-start(bf16[8,64,192]{2,1,0:T(8,128)(2,1)} %bitcast.47), calls=%async_computation.3 | async-start | bytes 524288 | tf_op jit(solution)/shard_map/all_to_all | solution.py:315
  205.8 29.5 %collective-permute-start.29 = (bf16[8,24,768]{2,1,0:T(8,128)(2,1)}, bf16[8,24,768]{2,1,0:T(8,128)(2,1)}, u32[]{:S(2)}, u32[]{:S(2)}) collective-permute-start(bf16[8,24,768]{2,1,0:T(8,128)(2,1)} %get-tuple-element.111), channel_id=1, source_target_pairs={{0,1},{1,0},{2,3},{3,2},{4,5},{5,4},{6,7},{7,6},{8,9},{9,8},{10,11... | collective-permute-start | bytes 884744 | tf_op jit(solution)/shard_map/ppermute | solution.py:45
  206.6 30.0 %collective-permute-start.30 = (bf16[8,24,768]{2,1,0:T(8,128)(2,1)}, bf16[8,24,768]{2,1,0:T(8,128)(2,1)}, u32[]{:S(2)}, u32[]{:S(2)}) collective-permute-start(bf16[8,24,768]{2,1,0:T(8,128)(2,1)} %get-tuple-element.110), channel_id=1, source_target_pairs={{0,2},{1,3},{2,0},{3,1},{4,6},{5,7},{6,4},{7,5},{8,10},{9,11},{10,... | collective-permute-start | bytes 884744 | tf_op jit(solution)/shard_map/ppermute | solution.py:45
  208.2 28.6 %collective-permute-start.31 = (bf16[8,24,768]{2,1,0:T(8,128)(2,1)}, bf16[8,24,768]{2,1,0:T(8,128)(2,1)}, u32[]{:S(2)}, u32[]{:S(2)}) collective-permute-start(bf16[8,24,768]{2,1,0:T(8,128)(2,1)} %get-tuple-element.109), channel_id=1, source_target_pairs={{0,3},{1,2},{2,1},{3,0},{4,7},{5,6},{6,5},{7,4},{8,11},{9,10},{10,... | collective-permute-start | bytes 884744 | tf_op jit(solution)/shard_map/ppermute | solution.py:45
  214.1 36.3 %all-to-all-start.5 = ((bf16[8,24,1536]{2,1,0:T(8,128)(2,1)}), bf16[8,24,1536]{2,1,0:T(8,128)(2,1)S(1)}, u32[]{:S(2)}, u32[]{:S(2)}) async-start(bf16[8,24,1536]{2,1,0:T(8,128)(2,1)} %fusion.4), calls=%async_computation.5 | async-start | bytes 1179648 | tf_op jit(solution)/shard_map/all_to_all | solution.py:315
  232.1 8.9 %collective-permute-start.26 = (bf16[8,24,584]{2,1,0:T(8,128)(2,1)S(1)}, bf16[8,24,584]{2,1,0:T(8,128)(2,1)S(1)}, u32[]{:S(2)}, u32[]{:S(2)}) collective-permute-start(bf16[8,24,584]{2,1,0:T(8,128)(2,1)S(1)} %get-tuple-element.113), channel_id=1, source_target_pairs={{0,1},{1,0},{2,3},{3,2},{4,5},{5,4},{6,7},{7,6},{8,9},{9,8},{10,11... | collective-permute-start | bytes 672776 | tf_op jit(solution)/shard_map/ppermute | solution.py:45
  232.9 13.2 %collective-permute-start.27 = (bf16[8,24,584]{2,1,0:T(8,128)(2,1)S(1)}, bf16[8,24,584]{2,1,0:T(8,128)(2,1)S(1)}, u32[]{:S(2)}, u32[]{:S(2)}) collective-permute-start(bf16[8,24,584]{2,1,0:T(8,128)(2,1)S(1)} %get-tuple-element.114), channel_id=1, source_target_pairs={{0,2},{1,3},{2,0},{3,1},{4,6},{5,7},{6,4},{7,5},{8,10},{9,11},{10,... | collective-permute-start | bytes 672776 | tf_op jit(solution)/shard_map/ppermute | solution.py:45
  235.3 10.8 %collective-permute-start.28 = (bf16[8,24,584]{2,1,0:T(8,128)(2,1)S(1)}, bf16[8,24,584]{2,1,0:T(8,128)(2,1)S(1)}, u32[]{:S(2)}, u32[]{:S(2)}) collective-permute-start(bf16[8,24,584]{2,1,0:T(8,128)(2,1)S(1)} %get-tuple-element.112), channel_id=1, source_target_pairs={{0,3},{1,2},{2,1},{3,0},{4,7},{5,6},{6,5},{7,4},{8,11},{9,10},{10,... | collective-permute-start | bytes 672776 | tf_op jit(solution)/shard_map/ppermute | solution.py:45
  236.7 10.9 %collective-permute-start.23 = (bf16[4,64,768]{2,1,0:T(8,128)(2,1)S(1)}, bf16[4,64,768]{2,1,0:T(8,128)(2,1)S(1)}, u32[]{:S(2)}, u32[]{:S(2)}) collective-permute-start(bf16[4,64,768]{2,1,0:T(8,128)(2,1)S(1)} %dynamic-slice_bitcast_fusion.1), channel_id=1, source_target_pairs={{0,4},{4,0},{8,12},{12,8},{16,20},{20,16},{24,28},{28,24},{1,5},{5... | collective-permute-start | bytes 1179656 | tf_op jit(solution)/shard_map/ppermute | solution.py:45
  247.7 6.4 %collective-permute-start.24 = (bf16[2,64,768]{2,1,0:T(8,128)(2,1)S(1)}, bf16[2,64,768]{2,1,0:T(8,128)(2,1)S(1)}, u32[]{:S(2)}, u32[]{:S(2)}) collective-permute-start(bf16[2,64,768]{2,1,0:T(8,128)(2,1)S(1)} %fusion.43), channel_id=1, source_target_pairs={{0,8},{4,12},{8,0},{12,4},{16,24},{20,28},{24,16},{28,20},{1,9},{5... | collective-permute-start | bytes 589832 | tf_op jit(solution)/shard_map/ppermute | solution.py:45
  250.4 24.4 %all-to-all-start.4 = ((bf16[8,24,1352]{2,1,0:T(8,128)(2,1)}), bf16[8,24,1352]{2,1,0:T(8,128)(2,1)S(1)}, u32[]{:S(2)}, u32[]{:S(2)}) async-start(bf16[8,24,1352]{2,1,0:T(8,128)(2,1)} %pad_maximum_fusion.2), calls=%async_computation.4 | async-start | bytes 1081344 | tf_op jit(solution)/shard_map/all_to_all | solution.py:315
  254.2 19.8 %collective-permute-start.25 = (bf16[64,768]{1,0:T(8,128)(2,1)S(1)}, bf16[64,768]{1,0:T(8,128)(2,1)S(1)}, u32[]{:S(2)}, u32[]{:S(2)}) collective-permute-start(bf16[64,768]{1,0:T(8,128)(2,1)S(1)} %fusion.47), channel_id=1, source_target_pairs={{0,16},{4,20},{8,24},{12,28},{16,0},{20,4},{24,8},{28,12},{1,17},{... | collective-permute-start | bytes 294920 | tf_op jit(solution)/shard_map/ppermute | solution.py:45
  (43 other events, 362.0 us)
Sparse Core Ops, SparseCore 0:
  11.2 33.8 all-gather.5
  47.3 29.5 all-gather.3

commit v3 on v2

--- a/solution.py
+++ b/solution.py
@@ -76,6 +76,16 @@
         part = lax.dynamic_index_in_dim(value, place ^ mask, axis, False).astype(LOW)
         pieces.append(swap(part, name, total, mask * step))
     return tuple(pieces)
+
+
+def line_gather(blocks, reach, seq_count, seq_at):
+    while reach:
+        came = swap(blocks, "seq", seq_count, reach)
+        upper = (seq_at // reach) % 2 == 1
+        pair = (jnp.where(upper, came, blocks), jnp.where(upper, blocks, came))
+        blocks = jnp.stack(pair, axis=1).reshape((2 * blocks.shape[0],) + blocks.shape[1:])
+        reach = reach // 2
+    return blocks
 
 
 def add_up(pieces):
@@ -354,21 +364,25 @@
     qkv_rows, gate_up_in, down_in = together(qkv_rows, w_gate_up, w_down)
     qkv_own = gather_by_swaps(qkv_rows, "dp", dp_count, dp_at, 1)
 
-    marks = jnp.concatenate([segments.reshape(-1), padding.reshape(-1)]).astype(LOW)
-    extra_rows = -(-marks.shape[0] // (8 * D)) * 8
-    marks = jnp.pad(marks, (0, extra_rows * D - marks.shape[0])).reshape(extra_rows, D)
-    packed = jnp.concatenate([tokens_flat, marks], axis=0)
-    line = lax.all_gather(packed, "seq", axis=0, tiled=False)
-    token_rows = lax.dynamic_slice_in_dim(line[:, :rows], own_seq * seq_rows, seq_rows, 1)
-    token_rows = token_rows.reshape(length, D)
-    mark_line = line[:, rows:].reshape(seq_count, extra_rows * D)[:, : 2 * rows]
-    mark_line = mark_line.reshape(seq_count, 2, sequences, seq_rows)
-    mark_line = lax.dynamic_index_in_dim(mark_line, own_seq, 2, False).astype(WIDE)
+    marks = jnp.concatenate([segments, padding], axis=1).astype(LOW)
+    extra_rows = -(-marks.shape[1] // (8 * D)) * 8
+    marks = jnp.pad(marks, ((0, 0), (0, extra_rows * D - marks.shape[1])))
+    packed = jnp.concatenate([tokens, marks.reshape(sequences, extra_rows, D)], axis=1)
+    line = put(
+        jnp.zeros_like(packed), lax.dynamic_index_in_dim(packed, own_seq, 0, False), own_seq, 0
+    )
+    for mask in range(1, sequences):
+        sent = lax.dynamic_index_in_dim(packed, own_seq ^ mask, 0, False)
+        line = put(line, swap(sent, "seq", seq_count, mask * head_groups), own_seq ^ mask, 0)
+    line = line_gather(line, head_groups // 2, seq_count, seq_at)
+    token_rows = line[:, :seq_rows].reshape(length, D)
+    mark_line = line[:, seq_rows:].reshape(seq_count, extra_rows * D)[:, : 2 * seq_rows]
+    mark_line = mark_line.reshape(seq_count, 2, seq_rows).astype(WIDE)
     marks_row = jnp.stack([mark_line[:, 0].reshape(length), mark_line[:, 1].reshape(length)])
     marks_column = marks_row.T
 
     out_part = gather_by_swaps(w_out, "dp", dp_count, dp_at, 0).reshape(-1, D)
-    out_full = lax.all_gather(out_part, "seq", axis=0, tiled=True)
+    out_full = line_gather(out_part[None], seq_count // 2, seq_count, seq_at).reshape(-1, D)
 
     columns = gate_up_in.reshape(wide_rows, 2, halves, GROUP, run).transpose(3, 0, 1, 2, 4)
     columns = columns.reshape(1, GROUP, wide_rows, 2 * halves * run)
@@ -395,6 +409,8 @@
     slopes = jnp.pad(jnp.asarray(slope_table(H)), (0, padded - H))
     slopes = lax.dynamic_slice_in_dim(slopes, own_heads * heads, heads, 0)
     blended, log_sums = attend(heads, width, slopes, qkv, marks_column, marks_row)
+    blended, down_pieces = together(blended, down_pieces)
+    down_own = in_order(down_pieces, dp_at, 1).reshape(hidden, D)
     blended = blended.reshape(seq_count, seq_rows, width)
 
     def to_rows(by_head):
@@ -408,9 +424,8 @@
     )
     token_wide = tokens_flat.astype(WIDE)
     resid_one = token_wide + (dot(attended, out_full) + bias_parts[2])
-    resid_one, gate_up_pieces, down_pieces = together(resid_one, gate_up_pieces, down_pieces)
+    resid_one, gate_up_pieces = together(resid_one, gate_up_pieces)
     gate_up_own = in_order(gate_up_pieces, dp_at, 1).reshape(D, 2 * hidden)
-    down_own = in_order(down_pieces, dp_at, 1).reshape(hidden, D)
     hidden_one, normed_one, inverse_one = norm_forward(
         resid_one, gain_parts[0], bias_parts[4]
     )

time: 287 us -> 301 us (1.049)
  waiting for transfers between devices: 99.4 us -> 119 us
  between operations: 15.2 us -> 1.91 us
  starting transfers between devices: 69.2 us -> 75.3 us
    ppermute x39 -> x45, waiting for transfers between devices: 56.4 us -> 110 us  [swap(): return lax.ppermute(value, axis, [(i, i ^ mask) for i in range(size)])]
    all_to_all x6, waiting for transfers between devices: 43 us -> 9.3 us  [exchange(): return lax.all_to_all(value, 'seq', 0, 0)]
    ppermute x39 -> x45, starting transfers between devices: 44.5 us -> 50.2 us  [swap(): return lax.ppermute(value, axis, [(i, i ^ mask) for i in range(size)])]
    dynamic_update_slice x19 -> x20, local copies, waits for them, and re-layouts: 11.1 us -> 14.6 us  [put(): lax.dynamic_update_slice(buffer, jnp.expand_dims(value, axis), starts)]
  transfers between devices with their start and end apart: 47 -> 51, of which waited for: 18 -> 19; matrix products, arithmetic and copies ran while one was open for 19% -> 19% of each run, Pallas kernels for 8% -> 8%
where the time goes in v3:
time: 301 us; the launch traced here: 299 us
  waiting for transfers between devices  119 us (40%)
  starting transfers between devices  75.3 us (25%)
  local copies, waits for them, and re-layouts  40.5 us (13%)
  Pallas kernels  30.3 us (10%)
  other arithmetic  21.9 us (7%)
  matrix products  10.3 us (3%)
    ppermute x45, waiting for transfers between devices, swap(): return lax.ppermute(value, axis, [(i, i ^ mask) for i in range(size)])  110 us
    ppermute x45, starting transfers between devices, swap(): return lax.ppermute(value, axis, [(i, i ^ mask) for i in range(size)])  50.2 us
    all_to_all x6, starting transfers between devices, exchange(): return lax.all_to_all(value, 'seq', 0, 0)  25.1 us
    dynamic_update_slice x20, local copies, waits for them, and re-layouts, put(): lax.dynamic_update_slice(buffer, jnp.expand_dims(value, axis), starts)  14.6 us
    pallas_call x2, Pallas kernels, in_vmem(): pl.pallas_call(kernel, out_shape=out_shape, in_specs=[pl.BlockSpec(memory...  13.9 us
    pallas_call x1, Pallas kernels, attend_back(): pl.pallas_call(lambda *refs: attend_back_kernel(heads, width, *refs), out...  9.51 us
    all_to_all x6, waiting for transfers between devices, exchange(): return lax.all_to_all(value, 'seq', 0, 0)  9.3 us
    pallas_call x1, Pallas kernels, attend(): pl.pallas_call(lambda *refs: attend_kernel(heads, width, *refs), out_shap...  6.89 us
  transfers between devices with their start and end apart: 51, of which 19 were waited for; matrix products, arithmetic and copies ran while one was open for 19% of the time, Pallas kernels for 8%

profile of v3, /device:TPU:0, one launch (start us, length us, event | category | flops | bytes accessed | tf_op | source)
XLA Modules:
  0.0 299.3 jit_solution(14487873471355237714)
XLA Ops:
  0.7 3.0 %collective-permute-start.10 = (bf16[24,768]{1,0:T(8,128)(2,1)}, bf16[24,768]{1,0:T(8,128)(2,1)S(1)}, u32[]{:S(2)}, u32[]{:S(2)}) collective-permute-start(bf16[24,768]{1,0:T(8,128)(2,1)} %param.15), channel_id=1, source_target_pairs={{0,1},{1,0},{2,3},{3,2},{4,5},{5,4},{6,7},{7,6},{8,9},{9,8},{10,11... | collective-permute-start | bytes 110600 | tf_op jit(solution)/shard_map/ppermute | solution.py:45
  8.3 5.3 %all-to-all-start = ((bf16[8,24,584]{2,1,0:T(8,128)(2,1)}), bf16[8,24,584]{2,1,0:T(8,128)(2,1)S(1)}, u32[]{:S(2)}, u32[]{:S(2)}) async-start(bf16[8,24,584]{2,1,0:T(8,128)(2,1)} %pad_maximum_fusion.7), calls=%async_computation | async-start | bytes 491520 | tf_op jit(solution)/shard_map/all_to_all | solution.py:325
  14.4 3.0 collective-permute-start
  18.2 13.2 %collective-permute-done = bf16[72,768]{1,0:T(8,128)(2,1)S(1)} collective-permute-done((bf16[72,768]{1,0:T(8,128)(2,1)S(1)}, bf16[72,768]{1,0:T(8,128)(2,1)S(1)}, u32[]{:S(2)}, u32[]{:S(2)}) %collective-permute-start) | collective-permute-done | bytes 110624 | tf_op jit(solution)/shard_map/ppermute | solution.py:45
  31.5 2.6 collective-permute-done.13
  34.9 4.9 %collective-permute-done.1 = bf16[2,72,768]{2,1,0:T(8,128)(2,1)S(1)} collective-permute-done((bf16[2,72,768]{2,1,0:T(8,128)(2,1)S(1)}, bf16[2,72,768]{2,1,0:T(8,128)(2,1)S(1)}, u32[]{:S(2)}, u32[]{:S(2)}) %collective-permute-start.1) | collective-permute-done | bytes 221216 | tf_op jit(solution)/shard_map/ppermute | solution.py:45
  40.0 1.6 collective-permute-start.3
  45.0 3.5 %all-to-all-start.2 = ((bf16[8,24,1536]{2,1,0:T(8,128)(2,1)}), bf16[8,24,1536]{2,1,0:T(8,128)(2,1)S(1)}, u32[]{:S(2)}, u32[]{:S(2)}) async-start(bf16[8,24,1536]{2,1,0:T(8,128)(2,1)} %bitcast.40), calls=%async_computation.2 | async-start | bytes 1179648 | tf_op jit(solution)/shard_map/all_to_all | solution.py:325
  49.3 1.6 bitcast_dynamic-update-slice_fusion.13
  51.0 2.9 collective-permute-start.6
  55.0 16.5 %collective-permute-done.6 = bf16[96,768]{1,0:T(8,128)(2,1)S(1)} collective-permute-done((bf16[96,768]{1,0:T(8,128)(2,1)}, bf16[96,768]{1,0:T(8,128)(2,1)S(1)}, u32[]{:S(2)}, u32[]{:S(2)}) %collective-permute-start.6) | collective-permute-done | bytes 147488 | tf_op jit(solution)/shard_map/ppermute | solution.py:45
  74.7 1.6 collective-permute-start.8
  81.9 1.6 fusion.refs_1_
  85.0 6.9 %attend.1 = (bf16[512,192]{1,0:T(8,128)(2,1)}, f32[512,3]{1,0:T(8,128)}) custom-call(f32[3]{0:T(128)} %dynamic_slice.96.refs_0_, bf16[512,576]{1,0:T(8,128)(2,1)} %fusion.refs_1_, f32[512,2]{1,0:T(8,128)} %copy.190.refs_2_.refs_4_, f32[2,512]{1,0:T(2,128)} %get-tuple-element.140.refs_3_.refs_5_), custom_call_target="tpu_custom_call" | custom-call | tf_op jit(solution)/shard_map/attend/pallas_call | solution.py:214
  93.0 1.7 bitcast_dynamic-update-slice_fusion.6
  94.7 1.7 bitcast_dynamic-update-slice_fusion.5
  96.4 1.7 bitcast_dynamic-update-slice_fusion.4
  98.1 1.7 bitcast_dynamic-update-slice_fusion.7
  99.9 4.2 %all-to-all-start.1 = ((bf16[8,64,192]{2,1,0:T(8,128)(2,1)}), bf16[8,64,192]{2,1,0:T(8,128)(2,1)}, u32[]{:S(2)}, u32[]{:S(2)}) async-start(bf16[8,64,192]{2,1,0:T(8,128)(2,1)} %bitcast.21), calls=%async_computation.1 | async-start | bytes 524288 | tf_op jit(solution)/shard_map/all_to_all | solution.py:325
  104.1 1.6 collective-permute-start.16
  109.0 4.6 %all-to-all-done.1 = bf16[8,64,192]{2,1,0:T(8,128)(2,1)} async-done(((bf16[8,64,192]{2,1,0:T(8,128)(2,1)}), bf16[8,64,192]{2,1,0:T(8,128)(2,1)}, u32[]{:S(2)}, u32[]{:S(2)}) %all-to-all-start.1) | async-done | bytes 196640 | tf_op jit(solution)/shard_map/all_to_all | solution.py:325
  116.4 4.1 %collective-permute-done.16 = bf16[8,24,1536]{2,1,0:T(8,128)(2,1)} collective-permute-done((bf16[8,24,1536]{2,1,0:T(8,128)(2,1)S(1)}, bf16[8,24,1536]{2,1,0:T(8,128)(2,1)}, u32[]{:S(2)}, u32[]{:S(2)}) %collective-permute-start.16) | collective-permute-done | bytes 589856 | tf_op jit(solution)/shard_map/ppermute | solution.py:45
  120.5 13.0 %collective-permute-done.17 = bf16[8,24,1536]{2,1,0:T(8,128)(2,1)} collective-permute-done((bf16[8,24,1536]{2,1,0:T(8,128)(2,1)S(1)}, bf16[8,24,1536]{2,1,0:T(8,128)(2,1)}, u32[]{:S(2)}, u32[]{:S(2)}) %collective-permute-start.17) | collective-permute-done | bytes 589856 | tf_op jit(solution)/shard_map/ppermute | solution.py:45
  134.0 1.7 collective-permute-start.20
  138.3 1.7 collective-permute-done.20
  142.9 6.5 %shard_map.170 = (f32[2,128,768]{2,1,0:T(8,128)}, bf16[2,128,768]{2,1,0:T(8,128)(2,1)}, bf16[512,768]{1,0:T(8,128)(2,1)}, f32[512,768]{1,0:T(8,128)}, f32[512,768]{1,0:T(8,128)}) custom-call(bf16[512,768]{1,0:T(8,128)(2,1)} %pad_maximum_fusion.2.refs_0_, bf16[768,1536]{1,0:T(8,128)(2,1)} %bitcast.302, bf16[768,768]{1,0:T(8,128)(2,1)} %bitcast.56.refs_2_.refs_4_), custom_call_target="tpu_custom_call" | custom-call | tf_op jit(solution)/shard_map/pallas_call | solution.py:292
  150.7 1.7 fusion.32
  152.6 1.7 collective-permute-start.23
  154.4 5.2 %collective-permute-done.23 = bf16[128,768]{1,0:T(8,128)(2,1)S(1)} collective-permute-done((bf16[128,768]{1,0:T(8,128)(2,1)S(1)}, bf16[128,768]{1,0:T(8,128)(2,1)S(1)}, u32[]{:S(2)}, u32[]{:S(2)}) %collective-permute-start.23) | collective-permute-done | bytes 196640 | tf_op jit(solution)/shard_map/ppermute | solution.py:45
  161.9 1.7 collective-permute-start.25
  163.6 4.4 %collective-permute-done.25 = bf16[128,768]{1,0:T(8,128)(2,1)S(1)} collective-permute-done((bf16[128,768]{1,0:T(8,128)(2,1)S(1)}, bf16[128,768]{1,0:T(8,128)(2,1)S(1)}, u32[]{:S(2)}, u32[]{:S(2)}) %collective-permute-start.25) | collective-permute-done | bytes 196640 | tf_op jit(solution)/shard_map/ppermute | solution.py:45
  176.3 7.3 %shard_map.171 = (f32[2,128,768]{2,1,0:T(8,128)}, bf16[2,128,768]{2,1,0:T(8,128)(2,1)}, bf16[512,1536]{1,0:T(8,128)(2,1)}) custom-call(bf16[512,768]{1,0:T(8,128)(2,1)} %pad_maximum_fusion.3.refs_0_, f32[512,768]{1,0:T(8,128)} %get-tuple-element.71.refs_1_, f32[512,768]{1,0:T(8,128)} %get-tuple-element.72.refs_2_, bf16[768,1536]{1,0:T(8,128)(2,1)} %bitcast.303, ...), custom_call_target="tpu_custom_call" | custom-call | tf_op jit(solution)/shard_map/pallas_call | solution.py:292
  183.7 2.8 fusion.56
  191.5 2.6 collective-permute-start.44
  195.8 5.3 %collective-permute-done.44 = bf16[96,768]{1,0:T(8,128)(2,1)S(1)} collective-permute-done((bf16[96,768]{1,0:T(8,128)(2,1)S(1)}, bf16[96,768]{1,0:T(8,128)(2,1)S(1)}, u32[]{:S(2)}, u32[]{:S(2)}) %collective-permute-start.44) | collective-permute-done | bytes 147488 | tf_op jit(solution)/shard_map/ppermute | solution.py:45
  203.0 13.4 %collective-permute-done.39 = bf16[8,24,1536]{2,1,0:T(8,128)(2,1)S(1)} collective-permute-done((bf16[8,24,1536]{2,1,0:T(8,128)(2,1)S(1)}, bf16[8,24,1536]{2,1,0:T(8,128)(2,1)S(1)}, u32[]{:S(2)}, u32[]{:S(2)}) %collective-permute-start.39) | collective-permute-done | bytes 589856 | tf_op jit(solution)/shard_map/ppermute | solution.py:45
  220.3 4.7 %all-to-all-start.3 = ((bf16[8,64,192]{2,1,0:T(8,128)(2,1)}), bf16[8,64,192]{2,1,0:T(8,128)(2,1)}, u32[]{:S(2)}, u32[]{:S(2)}) async-start(bf16[8,64,192]{2,1,0:T(8,128)(2,1)} %bitcast.64), calls=%async_computation.3 | async-start | bytes 524288 | tf_op jit(solution)/shard_map/all_to_all | solution.py:325
  230.1 4.7 %all-to-all-done.3 = bf16[8,64,192]{2,1,0:T(8,128)(2,1)} async-done(((bf16[8,64,192]{2,1,0:T(8,128)(2,1)}), bf16[8,64,192]{2,1,0:T(8,128)(2,1)}, u32[]{:S(2)}, u32[]{:S(2)}) %all-to-all-start.3) | async-done | bytes 196640 | tf_op jit(solution)/shard_map/all_to_all | solution.py:325
  234.8 3.5 %all-to-all-start.5 = ((bf16[8,24,1536]{2,1,0:T(8,128)(2,1)}), bf16[8,24,1536]{2,1,0:T(8,128)(2,1)S(1)}, u32[]{:S(2)}, u32[]{:S(2)}) async-start(bf16[8,24,1536]{2,1,0:T(8,128)(2,1)} %fusion.4), calls=%async_computation.5 | async-start | bytes 1179648 | tf_op jit(solution)/shard_map/all_to_all | solution.py:325
  238.4 9.5 %attend_back.1 = (bf16[512,576]{1,0:T(8,128)(2,1)}, f32[8,192]{1,0:T(8,128)}) custom-call(f32[3]{0:T(128)} %dynamic_slice.96.refs_0_, bf16[512,576]{1,0:T(8,128)(2,1)} %fusion.refs_1_, bf16[512,192]{1,0:T(8,128)(2,1)} %bitcast.65.refs_2_, f32[512,3]{1,0:T(8,128)} %get-tuple-element.75.refs_3_, f32[512,2]{1,0:T(8,128)} %copy.190.refs_2_.refs_4_, ...), custom_call_target="tpu_custom_call" | custom-call | tf_op jit(solution)/shard_map/attend_back/pallas_call | solution.py:229
  250.7 1.9 fusion.5
  255.7 1.5 collective-permute-start.34
  257.4 4.2 %collective-permute-done.32 = bf16[8,24,584]{2,1,0:T(8,128)(2,1)S(1)} collective-permute-done((bf16[8,24,584]{2,1,0:T(8,128)(2,1)S(1)}, bf16[8,24,584]{2,1,0:T(8,128)(2,1)S(1)}, u32[]{:S(2)}, u32[]{:S(2)}) %collective-permute-start.32) | collective-permute-done | bytes 224288 | tf_op jit(solution)/shard_map/ppermute | solution.py:45
  261.6 5.0 %collective-permute-done.33 = bf16[8,24,584]{2,1,0:T(8,128)(2,1)S(1)} collective-permute-done((bf16[8,24,584]{2,1,0:T(8,128)(2,1)S(1)}, bf16[8,24,584]{2,1,0:T(8,128)(2,1)S(1)}, u32[]{:S(2)}, u32[]{:S(2)}) %collective-permute-start.33) | collective-permute-done | bytes 224288 | tf_op jit(solution)/shard_map/ppermute | solution.py:45
  268.2 1.7 collective-permute-start.30
  270.8 3.7 %all-to-all-start.4 = ((bf16[8,24,1352]{2,1,0:T(8,128)(2,1)}), bf16[8,24,1352]{2,1,0:T(8,128)(2,1)S(1)}, u32[]{:S(2)}, u32[]{:S(2)}) async-start(bf16[8,24,1352]{2,1,0:T(8,128)(2,1)} %pad_maximum_fusion.5), calls=%async_computation.4 | async-start | bytes 1081344 | tf_op jit(solution)/shard_map/all_to_all | solution.py:325
  274.6 3.0 collective-permute-start.31
  279.6 14.8 %collective-permute-done.31 = bf16[64,768]{1,0:T(8,128)(2,1)S(1)} collective-permute-done((bf16[64,768]{1,0:T(8,128)(2,1)S(1)}, bf16[64,768]{1,0:T(8,128)(2,1)S(1)}, u32[]{:S(2)}, u32[]{:S(2)}) %collective-permute-start.31) | collective-permute-done | bytes 98336 | tf_op jit(solution)/shard_map/ppermute | solution.py:45
  (317 shorter events, 80.5 us)
Async XLA Ops:
  0.7 17.4 %collective-permute-start.10 = (bf16[24,768]{1,0:T(8,128)(2,1)}, bf16[24,768]{1,0:T(8,128)(2,1)S(1)}, u32[]{:S(2)}, u32[]{:S(2)}) collective-permute-start(bf16[24,768]{1,0:T(8,128)(2,1)} %param.15), channel_id=1, source_target_pairs={{0,1},{1,0},{2,3},{3,2},{4,5},{5,4},{6,7},{7,6},{8,9},{9,8},{10,11... | collective-permute-start | bytes 110600 | tf_op jit(solution)/shard_map/ppermute | solution.py:45
  3.7 14.4 %collective-permute-start.11 = (bf16[24,768]{1,0:T(8,128)(2,1)}, bf16[24,768]{1,0:T(8,128)(2,1)S(1)}, u32[]{:S(2)}, u32[]{:S(2)}) collective-permute-start(bf16[24,768]{1,0:T(8,128)(2,1)} %param.15), channel_id=1, source_target_pairs={{0,2},{1,3},{2,0},{3,1},{4,6},{5,7},{6,4},{7,5},{8,10},{9,11},{10,... | collective-permute-start | bytes 110600 | tf_op jit(solution)/shard_map/ppermute | solution.py:45
  5.2 12.9 %collective-permute-start.12 = (bf16[24,768]{1,0:T(8,128)(2,1)}, bf16[24,768]{1,0:T(8,128)(2,1)S(1)}, u32[]{:S(2)}, u32[]{:S(2)}) collective-permute-start(bf16[24,768]{1,0:T(8,128)(2,1)} %param.15), channel_id=1, source_target_pairs={{0,3},{1,2},{2,1},{3,0},{4,7},{5,6},{6,5},{7,4},{8,11},{9,10},{10,... | collective-permute-start | bytes 110600 | tf_op jit(solution)/shard_map/ppermute | solution.py:45
  8.3 31.7 %all-to-all-start = ((bf16[8,24,584]{2,1,0:T(8,128)(2,1)}), bf16[8,24,584]{2,1,0:T(8,128)(2,1)S(1)}, u32[]{:S(2)}, u32[]{:S(2)}) async-start(bf16[8,24,584]{2,1,0:T(8,128)(2,1)} %pad_maximum_fusion.7), calls=%async_computation | async-start | bytes 491520 | tf_op jit(solution)/shard_map/all_to_all | solution.py:325
  14.4 17.1 %collective-permute-start = (bf16[72,768]{1,0:T(8,128)(2,1)S(1)}, bf16[72,768]{1,0:T(8,128)(2,1)S(1)}, u32[]{:S(2)}, u32[]{:S(2)}) collective-permute-start(bf16[72,768]{1,0:T(8,128)(2,1)S(1)} %get-tuple-element.128), channel_id=1, source_target_pairs={{0,16},{4,20},{8,24},{12,28},{16,0},{20,4},{24,8},{28,12},{1,17},{... | collective-permute-start | bytes 331784 | tf_op jit(solution)/shard_map/ppermute | solution.py:45
  18.1 16.0 %collective-permute-start.13 = (bf16[1,96,768]{2,1,0:T(8,128)(2,1)S(1)}, bf16[1,96,768]{2,1,0:T(8,128)(2,1)S(1)}, u32[]{:S(2)}, u32[]{:S(2)}) collective-permute-start(bf16[1,96,768]{2,1,0:T(8,128)(2,1)S(1)} %bitcast.334), channel_id=1, source_target_pairs={{0,16},{4,20},{8,24},{12,28},{16,0},{20,4},{24,8},{28,12},{1,17},{... | collective-permute-start | bytes 442376 | tf_op jit(solution)/shard_map/ppermute | solution.py:45
  31.4 8.4 %collective-permute-start.1 = (bf16[2,72,768]{2,1,0:T(8,128)(2,1)S(1)}, bf16[2,72,768]{2,1,0:T(8,128)(2,1)S(1)}, u32[]{:S(2)}, u32[]{:S(2)}) collective-permute-start(bf16[2,72,768]{2,1,0:T(8,128)(2,1)S(1)} %bitcast_dynamic-update-slice_fusion.14), channel_id=1, source_target_pairs={{0,8},{4,12},{8,0},{12,4},{16,24},{20,28},{24,16},{28,20},{1,9},{5... | collective-permute-start | bytes 663560 | tf_op jit(solution)/shard_map/ppermute | solution.py:45
  34.9 16.2 %collective-permute-start.14 = (bf16[2,96,768]{2,1,0:T(8,128)(2,1)}, bf16[2,96,768]{2,1,0:T(8,128)(2,1)}, u32[]{:S(2)}, u32[]{:S(2)}) collective-permute-start(bf16[2,96,768]{2,1,0:T(8,128)(2,1)} %maximum_bitcast_fusion), channel_id=1, source_target_pairs={{0,8},{4,12},{8,0},{12,4},{16,24},{20,28},{24,16},{28,20},{1,9},{5... | collective-permute-start | bytes 884744 | tf_op jit(solution)/shard_map/ppermute | solution.py:45
  39.9 40.6 %collective-permute-start.2 = (bf16[4,72,768]{2,1,0:T(8,128)(2,1)S(1)}, bf16[4,72,768]{2,1,0:T(8,128)(2,1)S(1)}, u32[]{:S(2)}, u32[]{:S(2)}) collective-permute-start(bf16[4,72,768]{2,1,0:T(8,128)(2,1)S(1)} %bitcast.321), channel_id=1, source_target_pairs={{0,4},{4,0},{8,12},{12,8},{16,20},{20,16},{24,28},{28,24},{1,5},{5... | collective-permute-start | bytes 1327112 | tf_op jit(solution)/shard_map/ppermute | solution.py:45
  40.0 32.3 %collective-permute-start.3 = (bf16[8,24,584]{2,1,0:T(8,128)(2,1)S(1)}, bf16[8,24,584]{2,1,0:T(8,128)(2,1)}, u32[]{:S(2)}, u32[]{:S(2)}) collective-permute-start(bf16[8,24,584]{2,1,0:T(8,128)(2,1)S(1)} %all-to-all-done), channel_id=1, source_target_pairs={{0,1},{1,0},{2,3},{3,2},{4,5},{5,4},{6,7},{7,6},{8,9},{9,8},{10,11... | collective-permute-start | bytes 672776 | tf_op jit(solution)/shard_map/ppermute | solution.py:45
  41.5 33.2 %collective-permute-start.4 = (bf16[8,24,584]{2,1,0:T(8,128)(2,1)S(1)}, bf16[8,24,584]{2,1,0:T(8,128)(2,1)}, u32[]{:S(2)}, u32[]{:S(2)}) collective-permute-start(bf16[8,24,584]{2,1,0:T(8,128)(2,1)S(1)} %all-to-all-done), channel_id=1, source_target_pairs={{0,2},{1,3},{2,0},{3,1},{4,6},{5,7},{6,4},{7,5},{8,10},{9,11},{10,... | collective-permute-start | bytes 672776 | tf_op jit(solution)/shard_map/ppermute | solution.py:45
  43.1 34.2 %collective-permute-start.5 = (bf16[8,24,584]{2,1,0:T(8,128)(2,1)S(1)}, bf16[8,24,584]{2,1,0:T(8,128)(2,1)S(1)}, u32[]{:S(2)}, u32[]{:S(2)}) collective-permute-start(bf16[8,24,584]{2,1,0:T(8,128)(2,1)S(1)} %all-to-all-done), channel_id=1, source_target_pairs={{0,3},{1,2},{2,1},{3,0},{4,7},{5,6},{6,5},{7,4},{8,11},{9,10},{10,... | collective-permute-start | bytes 672776 | tf_op jit(solution)/shard_map/ppermute | solution.py:45
  45.0 54.8 %all-to-all-start.2 = ((bf16[8,24,1536]{2,1,0:T(8,128)(2,1)}), bf16[8,24,1536]{2,1,0:T(8,128)(2,1)S(1)}, u32[]{:S(2)}, u32[]{:S(2)}) async-start(bf16[8,24,1536]{2,1,0:T(8,128)(2,1)} %bitcast.40), calls=%async_computation.2 | async-start | bytes 1179648 | tf_op jit(solution)/shard_map/all_to_all | solution.py:325
  51.0 20.5 %collective-permute-start.6 = (bf16[96,768]{1,0:T(8,128)(2,1)}, bf16[96,768]{1,0:T(8,128)(2,1)S(1)}, u32[]{:S(2)}, u32[]{:S(2)}) collective-permute-start(bf16[96,768]{1,0:T(8,128)(2,1)} %param.17), channel_id=1, source_target_pairs={{0,16},{4,20},{8,24},{12,28},{16,0},{20,4},{24,8},{28,12},{1,17},{... | collective-permute-start | bytes 442376 | tf_op jit(solution)/shard_map/ppermute | solution.py:45
  71.6 36.1 %collective-permute-start.15 = (bf16[4,96,768]{2,1,0:T(8,128)(2,1)S(1)}, bf16[4,96,768]{2,1,0:T(8,128)(2,1)}, u32[]{:S(2)}, u32[]{:S(2)}) collective-permute-start(bf16[4,96,768]{2,1,0:T(8,128)(2,1)S(1)} %bitcast.316), channel_id=1, source_target_pairs={{0,4},{4,0},{8,12},{12,8},{16,20},{20,16},{24,28},{28,24},{1,5},{5... | collective-permute-start | bytes 1769480 | tf_op jit(solution)/shard_map/ppermute | solution.py:45
  72.2 19.7 %collective-permute-start.7 = (bf16[2,96,768]{2,1,0:T(8,128)(2,1)}, bf16[2,96,768]{2,1,0:T(8,128)(2,1)}, u32[]{:S(2)}, u32[]{:S(2)}) collective-permute-start(bf16[2,96,768]{2,1,0:T(8,128)(2,1)} %bitcast_dynamic-update-slice_fusion.12), channel_id=1, source_target_pairs={{0,1},{1,0},{2,3},{3,2},{4,5},{5,4},{6,7},{7,6},{8,9},{9,8},{10,11... | collective-permute-start | bytes 884744 | tf_op jit(solution)/shard_map/ppermute | solution.py:45
  74.7 17.2 %collective-permute-start.8 = (bf16[2,96,768]{2,1,0:T(8,128)(2,1)}, bf16[2,96,768]{2,1,0:T(8,128)(2,1)}, u32[]{:S(2)}, u32[]{:S(2)}) collective-permute-start(bf16[2,96,768]{2,1,0:T(8,128)(2,1)} %bitcast_dynamic-update-slice_fusion.12), channel_id=1, source_target_pairs={{0,2},{1,3},{2,0},{3,1},{4,6},{5,7},{6,4},{7,5},{8,10},{9,11},{10,... | collective-permute-start | bytes 884744 | tf_op jit(solution)/shard_map/ppermute | solution.py:45
  77.3 14.6 %collective-permute-start.9 = (bf16[2,96,768]{2,1,0:T(8,128)(2,1)}, bf16[2,96,768]{2,1,0:T(8,128)(2,1)}, u32[]{:S(2)}, u32[]{:S(2)}) collective-permute-start(bf16[2,96,768]{2,1,0:T(8,128)(2,1)} %bitcast_dynamic-update-slice_fusion.12), channel_id=1, source_target_pairs={{0,3},{1,2},{2,1},{3,0},{4,7},{5,6},{6,5},{7,4},{8,11},{9,10},{10,... | collective-permute-start | bytes 884744 | tf_op jit(solution)/shard_map/ppermute | solution.py:45
  99.9 13.8 %all-to-all-start.1 = ((bf16[8,64,192]{2,1,0:T(8,128)(2,1)}), bf16[8,64,192]{2,1,0:T(8,128)(2,1)}, u32[]{:S(2)}, u32[]{:S(2)}) async-start(bf16[8,64,192]{2,1,0:T(8,128)(2,1)} %bitcast.21), calls=%async_computation.1 | async-start | bytes 524288 | tf_op jit(solution)/shard_map/all_to_all | solution.py:325
  104.1 16.4 %collective-permute-start.16 = (bf16[8,24,1536]{2,1,0:T(8,128)(2,1)S(1)}, bf16[8,24,1536]{2,1,0:T(8,128)(2,1)}, u32[]{:S(2)}, u32[]{:S(2)}) collective-permute-start(bf16[8,24,1536]{2,1,0:T(8,128)(2,1)S(1)} %all-to-all-done.2), channel_id=1, source_target_pairs={{0,1},{1,0},{2,3},{3,2},{4,5},{5,4},{6,7},{7,6},{8,9},{9,8},{10,11... | collective-permute-start | bytes 1769480 | tf_op jit(solution)/shard_map/ppermute | solution.py:45
  105.7 27.8 %collective-permute-start.17 = (bf16[8,24,1536]{2,1,0:T(8,128)(2,1)S(1)}, bf16[8,24,1536]{2,1,0:T(8,128)(2,1)}, u32[]{:S(2)}, u32[]{:S(2)}) collective-permute-start(bf16[8,24,1536]{2,1,0:T(8,128)(2,1)S(1)} %all-to-all-done.2), channel_id=1, source_target_pairs={{0,2},{1,3},{2,0},{3,1},{4,6},{5,7},{6,4},{7,5},{8,10},{9,11},{10,... | collective-permute-start | bytes 1769480 | tf_op jit(solution)/shard_map/ppermute | solution.py:45
  107.2 26.3 %collective-permute-start.18 = (bf16[8,24,1536]{2,1,0:T(8,128)(2,1)S(1)}, bf16[8,24,1536]{2,1,0:T(8,128)(2,1)}, u32[]{:S(2)}, u32[]{:S(2)}) collective-permute-start(bf16[8,24,1536]{2,1,0:T(8,128)(2,1)S(1)} %all-to-all-done.2), channel_id=1, source_target_pairs={{0,3},{1,2},{2,1},{3,0},{4,7},{5,6},{6,5},{7,4},{8,11},{9,10},{10,... | collective-permute-start | bytes 1769480 | tf_op jit(solution)/shard_map/ppermute | solution.py:45
  134.0 5.9 %collective-permute-start.20 = (bf16[128,768]{1,0:T(8,128)(2,1)S(1)}, bf16[128,768]{1,0:T(8,128)(2,1)S(1)}, u32[]{:S(2)}, u32[]{:S(2)}) collective-permute-start(bf16[128,768]{1,0:T(8,128)(2,1)S(1)} %fusion.33), channel_id=1, source_target_pairs={{0,8},{4,12},{8,0},{12,4},{16,24},{20,28},{24,16},{28,20},{1,9},{5... | collective-permute-start | bytes 589832 | tf_op jit(solution)/shard_map/ppermute | solution.py:45
  135.7 5.4 %collective-permute-start.19 = (bf16[128,768]{1,0:T(8,128)(2,1)S(1)}, bf16[128,768]{1,0:T(8,128)(2,1)S(1)}, u32[]{:S(2)}, u32[]{:S(2)}) collective-permute-start(bf16[128,768]{1,0:T(8,128)(2,1)S(1)} %fusion.33), channel_id=1, source_target_pairs={{0,4},{4,0},{8,12},{12,8},{16,20},{20,16},{24,28},{28,24},{1,5},{5... | collective-permute-start | bytes 589832 | tf_op jit(solution)/shard_map/ppermute | solution.py:45
  152.6 7.0 %collective-permute-start.23 = (bf16[128,768]{1,0:T(8,128)(2,1)S(1)}, bf16[128,768]{1,0:T(8,128)(2,1)S(1)}, u32[]{:S(2)}, u32[]{:S(2)}) collective-permute-start(bf16[128,768]{1,0:T(8,128)(2,1)S(1)} %fusion.44), channel_id=1, source_target_pairs={{0,8},{4,12},{8,0},{12,4},{16,24},{20,28},{24,16},{28,20},{1,9},{5... | collective-permute-start | bytes 589832 | tf_op jit(solution)/shard_map/ppermute | solution.py:45
  161.9 6.1 %collective-permute-start.25 = (bf16[128,768]{1,0:T(8,128)(2,1)S(1)}, bf16[128,768]{1,0:T(8,128)(2,1)S(1)}, u32[]{:S(2)}, u32[]{:S(2)}) collective-permute-start(bf16[128,768]{1,0:T(8,128)(2,1)S(1)} %convert_element_type.279), channel_id=1, source_target_pairs={{0,8},{4,12},{8,0},{12,4},{16,24},{20,28},{24,16},{28,20},{1,9},{5... | collective-permute-start | bytes 589832 | tf_op jit(solution)/shard_map/ppermute | solution.py:45
  163.6 5.7 %collective-permute-start.24 = (bf16[128,768]{1,0:T(8,128)(2,1)S(1)}, bf16[128,768]{1,0:T(8,128)(2,1)S(1)}, u32[]{:S(2)}, u32[]{:S(2)}) collective-permute-start(bf16[128,768]{1,0:T(8,128)(2,1)S(1)} %convert_element_type.279), channel_id=1, source_target_pairs={{0,4},{4,0},{8,12},{12,8},{16,20},{20,16},{24,28},{28,24},{1,5},{5... | collective-permute-start | bytes 589832 | tf_op jit(solution)/shard_map/ppermute | solution.py:45
  171.8 16.4 %collective-permute-start.41 = (bf16[2,96,768]{2,1,0:T(8,128)(2,1)S(1)}, bf16[2,96,768]{2,1,0:T(8,128)(2,1)S(1)}, u32[]{:S(2)}, u32[]{:S(2)}) collective-permute-start(bf16[2,96,768]{2,1,0:T(8,128)(2,1)S(1)} %get-tuple-element.108), channel_id=1, source_target_pairs={{0,1},{1,0},{2,3},{3,2},{4,5},{5,4},{6,7},{7,6},{8,9},{9,8},{10,11... | collective-permute-start | bytes 884744 | tf_op jit(solution)/shard_map/ppermute | solution.py:45
  173.3 15.5 %collective-permute-start.42 = (bf16[2,96,768]{2,1,0:T(8,128)(2,1)S(1)}, bf16[2,96,768]{2,1,0:T(8,128)(2,1)S(1)}, u32[]{:S(2)}, u32[]{:S(2)}) collective-permute-start(bf16[2,96,768]{2,1,0:T(8,128)(2,1)S(1)} %get-tuple-element.109), channel_id=1, source_target_pairs={{0,2},{1,3},{2,0},{3,1},{4,6},{5,7},{6,4},{7,5},{8,10},{9,11},{10,... | collective-permute-start | bytes 884744 | tf_op jit(solution)/shard_map/ppermute | solution.py:45
  173.9 16.4 %collective-permute-start.43 = (bf16[2,96,768]{2,1,0:T(8,128)(2,1)S(1)}, bf16[2,96,768]{2,1,0:T(8,128)(2,1)S(1)}, u32[]{:S(2)}, u32[]{:S(2)}) collective-permute-start(bf16[2,96,768]{2,1,0:T(8,128)(2,1)S(1)} %get-tuple-element.110), channel_id=1, source_target_pairs={{0,3},{1,2},{2,1},{3,0},{4,7},{5,6},{6,5},{7,4},{8,11},{9,10},{10,... | collective-permute-start | bytes 884744 | tf_op jit(solution)/shard_map/ppermute | solution.py:45
  183.6 10.5 %collective-permute-start.27 = (bf16[2,128,768]{2,1,0:T(8,128)(2,1)}, bf16[2,128,768]{2,1,0:T(8,128)(2,1)S(1)}, u32[]{:S(2)}, u32[]{:S(2)}) collective-permute-start(bf16[2,128,768]{2,1,0:T(8,128)(2,1)} %get-tuple-element.74), channel_id=1, source_target_pairs={{0,4},{4,0},{8,12},{12,8},{16,20},{20,16},{24,28},{28,24},{1,5},{5... | collective-permute-start | bytes 1179656 | tf_op jit(solution)/shard_map/ppermute | solution.py:45
  186.7 16.3 %collective-permute-start.38 = (bf16[8,24,1536]{2,1,0:T(8,128)(2,1)S(1)}, bf16[8,24,1536]{2,1,0:T(8,128)(2,1)S(1)}, u32[]{:S(2)}, u32[]{:S(2)}) collective-permute-start(bf16[8,24,1536]{2,1,0:T(8,128)(2,1)S(1)} %get-tuple-element.105), channel_id=1, source_target_pairs={{0,1},{1,0},{2,3},{3,2},{4,5},{5,4},{6,7},{7,6},{8,9},{9,8},{10,11... | collective-permute-start | bytes 1769480 | tf_op jit(solution)/shard_map/ppermute | solution.py:45
  188.2 28.1 %collective-permute-start.39 = (bf16[8,24,1536]{2,1,0:T(8,128)(2,1)S(1)}, bf16[8,24,1536]{2,1,0:T(8,128)(2,1)S(1)}, u32[]{:S(2)}, u32[]{:S(2)}) collective-permute-start(bf16[8,24,1536]{2,1,0:T(8,128)(2,1)S(1)} %get-tuple-element.107), channel_id=1, source_target_pairs={{0,2},{1,3},{2,0},{3,1},{4,6},{5,7},{6,4},{7,5},{8,10},{9,11},{10,... | collective-permute-start | bytes 1769480 | tf_op jit(solution)/shard_map/ppermute | solution.py:45
  188.8 27.5 %collective-permute-start.40 = (bf16[8,24,1536]{2,1,0:T(8,128)(2,1)S(1)}, bf16[8,24,1536]{2,1,0:T(8,128)(2,1)S(1)}, u32[]{:S(2)}, u32[]{:S(2)}) collective-permute-start(bf16[8,24,1536]{2,1,0:T(8,128)(2,1)S(1)} %get-tuple-element.106), channel_id=1, source_target_pairs={{0,3},{1,2},{2,1},{3,0},{4,7},{5,6},{6,5},{7,4},{8,11},{9,10},{10,... | collective-permute-start | bytes 1769480 | tf_op jit(solution)/shard_map/ppermute | solution.py:45
  191.5 9.6 %collective-permute-start.44 = (bf16[96,768]{1,0:T(8,128)(2,1)S(1)}, bf16[96,768]{1,0:T(8,128)(2,1)S(1)}, u32[]{:S(2)}, u32[]{:S(2)}) collective-permute-start(bf16[96,768]{1,0:T(8,128)(2,1)S(1)} %fusion.46), channel_id=1, source_target_pairs={{0,16},{4,20},{8,24},{12,28},{16,0},{20,4},{24,8},{28,12},{1,17},{... | collective-permute-start | bytes 442376 | tf_op jit(solution)/shard_map/ppermute | solution.py:45
  194.2 23.2 %collective-permute-start.28 = (bf16[128,768]{1,0:T(8,128)(2,1)S(1)}, bf16[128,768]{1,0:T(8,128)(2,1)S(1)}, u32[]{:S(2)}, u32[]{:S(2)}) collective-permute-start(bf16[128,768]{1,0:T(8,128)(2,1)S(1)} %fusion.45), channel_id=1, source_target_pairs={{0,8},{4,12},{8,0},{12,4},{16,24},{20,28},{24,16},{28,20},{1,9},{5... | collective-permute-start | bytes 589832 | tf_op jit(solution)/shard_map/ppermute | solution.py:45
  220.3 14.6 %all-to-all-start.3 = ((bf16[8,64,192]{2,1,0:T(8,128)(2,1)}), bf16[8,64,192]{2,1,0:T(8,128)(2,1)}, u32[]{:S(2)}, u32[]{:S(2)}) async-start(bf16[8,64,192]{2,1,0:T(8,128)(2,1)} %bitcast.64), calls=%async_computation.3 | async-start | bytes 524288 | tf_op jit(solution)/shard_map/all_to_all | solution.py:325
  226.5 29.2 %collective-permute-start.35 = (bf16[8,24,768]{2,1,0:T(8,128)(2,1)}, bf16[8,24,768]{2,1,0:T(8,128)(2,1)}, u32[]{:S(2)}, u32[]{:S(2)}) collective-permute-start(bf16[8,24,768]{2,1,0:T(8,128)(2,1)} %get-tuple-element.113), channel_id=1, source_target_pairs={{0,1},{1,0},{2,3},{3,2},{4,5},{5,4},{6,7},{7,6},{8,9},{9,8},{10,11... | collective-permute-start | bytes 884744 | tf_op jit(solution)/shard_map/ppermute | solution.py:45
  227.0 30.3 %collective-permute-start.36 = (bf16[8,24,768]{2,1,0:T(8,128)(2,1)}, bf16[8,24,768]{2,1,0:T(8,128)(2,1)}, u32[]{:S(2)}, u32[]{:S(2)}) collective-permute-start(bf16[8,24,768]{2,1,0:T(8,128)(2,1)} %get-tuple-element.112), channel_id=1, source_target_pairs={{0,2},{1,3},{2,0},{3,1},{4,6},{5,7},{6,4},{7,5},{8,10},{9,11},{10,... | collective-permute-start | bytes 884744 | tf_op jit(solution)/shard_map/ppermute | solution.py:45
  228.5 29.0 %collective-permute-start.37 = (bf16[8,24,768]{2,1,0:T(8,128)(2,1)}, bf16[8,24,768]{2,1,0:T(8,128)(2,1)}, u32[]{:S(2)}, u32[]{:S(2)}) collective-permute-start(bf16[8,24,768]{2,1,0:T(8,128)(2,1)} %get-tuple-element.111), channel_id=1, source_target_pairs={{0,3},{1,2},{2,1},{3,0},{4,7},{5,6},{6,5},{7,4},{8,11},{9,10},{10,... | collective-permute-start | bytes 884744 | tf_op jit(solution)/shard_map/ppermute | solution.py:45
  234.8 36.0 %all-to-all-start.5 = ((bf16[8,24,1536]{2,1,0:T(8,128)(2,1)}), bf16[8,24,1536]{2,1,0:T(8,128)(2,1)S(1)}, u32[]{:S(2)}, u32[]{:S(2)}) async-start(bf16[8,24,1536]{2,1,0:T(8,128)(2,1)} %fusion.4), calls=%async_computation.5 | async-start | bytes 1179648 | tf_op jit(solution)/shard_map/all_to_all | solution.py:325
  252.7 8.9 %collective-permute-start.32 = (bf16[8,24,584]{2,1,0:T(8,128)(2,1)S(1)}, bf16[8,24,584]{2,1,0:T(8,128)(2,1)S(1)}, u32[]{:S(2)}, u32[]{:S(2)}) collective-permute-start(bf16[8,24,584]{2,1,0:T(8,128)(2,1)S(1)} %get-tuple-element.115), channel_id=1, source_target_pairs={{0,1},{1,0},{2,3},{3,2},{4,5},{5,4},{6,7},{7,6},{8,9},{9,8},{10,11... | collective-permute-start | bytes 672776 | tf_op jit(solution)/shard_map/ppermute | solution.py:45
  253.4 13.2 %collective-permute-start.33 = (bf16[8,24,584]{2,1,0:T(8,128)(2,1)S(1)}, bf16[8,24,584]{2,1,0:T(8,128)(2,1)S(1)}, u32[]{:S(2)}, u32[]{:S(2)}) collective-permute-start(bf16[8,24,584]{2,1,0:T(8,128)(2,1)S(1)} %get-tuple-element.116), channel_id=1, source_target_pairs={{0,2},{1,3},{2,0},{3,1},{4,6},{5,7},{6,4},{7,5},{8,10},{9,11},{10,... | collective-permute-start | bytes 672776 | tf_op jit(solution)/shard_map/ppermute | solution.py:45
  255.7 10.9 %collective-permute-start.34 = (bf16[8,24,584]{2,1,0:T(8,128)(2,1)S(1)}, bf16[8,24,584]{2,1,0:T(8,128)(2,1)S(1)}, u32[]{:S(2)}, u32[]{:S(2)}) collective-permute-start(bf16[8,24,584]{2,1,0:T(8,128)(2,1)S(1)} %get-tuple-element.114), channel_id=1, source_target_pairs={{0,3},{1,2},{2,1},{3,0},{4,7},{5,6},{6,5},{7,4},{8,11},{9,10},{10,... | collective-permute-start | bytes 672776 | tf_op jit(solution)/shard_map/ppermute | solution.py:45
  257.3 10.7 %collective-permute-start.29 = (bf16[4,64,768]{2,1,0:T(8,128)(2,1)S(1)}, bf16[4,64,768]{2,1,0:T(8,128)(2,1)S(1)}, u32[]{:S(2)}, u32[]{:S(2)}) collective-permute-start(bf16[4,64,768]{2,1,0:T(8,128)(2,1)S(1)} %dynamic-slice_bitcast_fusion.1), channel_id=1, source_target_pairs={{0,4},{4,0},{8,12},{12,8},{16,20},{20,16},{24,28},{28,24},{1,5},{5... | collective-permute-start | bytes 1179656 | tf_op jit(solution)/shard_map/ppermute | solution.py:45
  268.2 6.4 %collective-permute-start.30 = (bf16[2,64,768]{2,1,0:T(8,128)(2,1)S(1)}, bf16[2,64,768]{2,1,0:T(8,128)(2,1)S(1)}, u32[]{:S(2)}, u32[]{:S(2)}) collective-permute-start(bf16[2,64,768]{2,1,0:T(8,128)(2,1)S(1)} %fusion.43), channel_id=1, source_target_pairs={{0,8},{4,12},{8,0},{12,4},{16,24},{20,28},{24,16},{28,20},{1,9},{5... | collective-permute-start | bytes 589832 | tf_op jit(solution)/shard_map/ppermute | solution.py:45
  270.8 24.4 %all-to-all-start.4 = ((bf16[8,24,1352]{2,1,0:T(8,128)(2,1)}), bf16[8,24,1352]{2,1,0:T(8,128)(2,1)S(1)}, u32[]{:S(2)}, u32[]{:S(2)}) async-start(bf16[8,24,1352]{2,1,0:T(8,128)(2,1)} %pad_maximum_fusion.5), calls=%async_computation.4 | async-start | bytes 1081344 | tf_op jit(solution)/shard_map/all_to_all | solution.py:325
  274.6 19.8 %collective-permute-start.31 = (bf16[64,768]{1,0:T(8,128)(2,1)S(1)}, bf16[64,768]{1,0:T(8,128)(2,1)S(1)}, u32[]{:S(2)}, u32[]{:S(2)}) collective-permute-start(bf16[64,768]{1,0:T(8,128)(2,1)S(1)} %fusion.47), channel_id=1, source_target_pairs={{0,16},{4,20},{8,24},{12,28},{16,0},{20,4},{24,8},{28,12},{1,17},{... | collective-permute-start | bytes 294920 | tf_op jit(solution)/shard_map/ppermute | solution.py:45
  (43 other events, 350.1 us)

commit v4 on v3

--- a/solution.py
+++ b/solution.py
@@ -16,6 +16,8 @@
 GROUP = 4
 QUERY_BLOCK = 128
 
+SEQ = "seq"
+DP = "dp"
 NEG_FILL = -1e30
 EPSILON = 1e-12
 LOW = jnp.bfloat16
@@ -80,7 +82,7 @@
 
 def line_gather(blocks, reach, seq_count, seq_at):
     while reach:
-        came = swap(blocks, "seq", seq_count, reach)
+        came = swap(blocks, SEQ, seq_count, reach)
         upper = (seq_at // reach) % 2 == 1
         pair = (jnp.where(upper, came, blocks), jnp.where(upper, blocks, came))
         blocks = jnp.stack(pair, axis=1).reshape((2 * blocks.shape[0],) + blocks.shape[1:])
@@ -100,15 +102,15 @@
 
 
 def group_gather(rows, seq_count):
-    partner = swap(rows, "seq", seq_count, 1)
-    across = swap(rows, "seq", seq_count, 2)
-    corner = swap(across, "seq", seq_count, 1)
+    partner = swap(rows, SEQ, seq_count, 1)
+    across = swap(rows, SEQ, seq_count, 2)
+    corner = swap(across, SEQ, seq_count, 1)
     return jnp.concatenate([rows, partner, across, corner], axis=0)
 
 
 def group_scatter(kept, sent, seq_count):
-    came = swap(sent, "seq", seq_count, 1).astype(WIDE)
-    across = swap((kept[1] + came[1]).astype(LOW), "seq", seq_count, 2).astype(WIDE)
+    came = swap(sent, SEQ, seq_count, 1).astype(WIDE)
+    across = swap((kept[1] + came[1]).astype(LOW), SEQ, seq_count, 2).astype(WIDE)
     return kept[0] + came[0] + across
 
 
@@ -119,7 +121,7 @@
         bit = (seq_at // step) % 2
         sent = lax.dynamic_index_in_dim(halves, 1 - bit, 1, False).astype(LOW)
         kept = lax.dynamic_index_in_dim(halves, bit, 1, False).astype(WIDE)
-        total = kept + swap(sent, "seq", seq_count, step).astype(WIDE)
+        total = kept + swap(sent, SEQ, seq_count, step).astype(WIDE)
         step *= 2
     return total
 
@@ -130,7 +132,7 @@
     result = put(jnp.zeros_like(total), lax.dynamic_index_in_dim(total, own, 0, False), own, 0)
     for mask in range(1, sequences):
         sent = lax.dynamic_index_in_dim(total, own ^ mask, 0, False).astype(LOW)
-        came = swap(sent, "seq", seq_count, mask * step).astype(WIDE)
+        came = swap(sent, SEQ, seq_count, mask * step).astype(WIDE)
         result = put(result, came, own ^ mask, 0)
     return result
 
@@ -220,7 +222,7 @@
         in_specs=[pl.BlockSpec(memory_space=pltpu.SMEM)]
         + [pl.BlockSpec(memory_space=pltpu.VMEM)] * 3,
         out_specs=[pl.BlockSpec(memory_space=pltpu.VMEM)] * 2,
-        name="attend",
+        name="at",
     )(slopes, qkv, marks_column, marks_row)
 
 
@@ -236,7 +238,7 @@
         + [pl.BlockSpec(memory_space=pltpu.VMEM)] * 5,
         out_specs=[pl.BlockSpec(memory_space=pltpu.VMEM)] * 2,
         scratch_shapes=[pltpu.VMEM((2, length, width), WIDE)],
-        name="attend_back",
+        name="ab",
     )(slopes, qkv, grad_out, sums, marks_column, marks_row)
 
 
@@ -322,7 +324,7 @@
 
 
 def exchange(value):
-    return lax.all_to_all(value, "seq", 0, 0)
+    return lax.all_to_all(value, SEQ, 0, 0)
 
 
 def together(*values):
@@ -333,8 +335,8 @@
     tokens, segments, padding, w_qkv, w_out, w_gate_up, w_down, biases, norm_gains, cotangent
 ):
     sequences, seq_rows = tokens.shape[:2]
-    seq_count, dp_count = lax.axis_size("seq"), lax.axis_size("dp")
-    seq_at, dp_at = lax.axis_index("seq"), lax.axis_index("dp")
+    seq_count, dp_count = lax.axis_size(SEQ), lax.axis_size(DP)
+    seq_at, dp_at = lax.axis_index(SEQ), lax.axis_index(DP)
     halves = seq_count // GROUP
     half_at = seq_at // GROUP
     rows = sequences * seq_rows
@@ -362,7 +364,7 @@
     small = jnp.broadcast_to(small, (seq_count, wide_rows, small_columns))
     qkv_rows = exchange(jnp.concatenate([by_heads, small], axis=-1))
     qkv_rows, gate_up_in, down_in = together(qkv_rows, w_gate_up, w_down)
-    qkv_own = gather_by_swaps(qkv_rows, "dp", dp_count, dp_at, 1)
+    qkv_own = gather_by_swaps(qkv_rows, DP, dp_count, dp_at, 1)
 
     marks = jnp.concatenate([segments, padding], axis=1).astype(LOW)
     extra_rows = -(-marks.shape[1] // (8 * D)) * 8
@@ -373,7 +375,7 @@
     )
     for mask in range(1, sequences):
         sent = lax.dynamic_index_in_dim(packed, own_seq ^ mask, 0, False)
-        line = put(line, swap(sent, "seq", seq_count, mask * head_groups), own_seq ^ mask, 0)
+        line = put(line, swap(sent, SEQ, seq_count, mask * head_groups), own_seq ^ mask, 0)
     line = line_gather(line, head_groups // 2, seq_count, seq_at)
     token_rows = line[:, :seq_rows].reshape(length, D)
     mark_line = line[:, seq_rows:].reshape(seq_count, extra_rows * D)[:, : 2 * seq_rows]
@@ -381,7 +383,7 @@
     marks_row = jnp.stack([mark_line[:, 0].reshape(length), mark_line[:, 1].reshape(length)])
     marks_column = marks_row.T
 
-    out_part = gather_by_swaps(w_out, "dp", dp_count, dp_at, 0).reshape(-1, D)
+    out_part = gather_by_swaps(w_out, DP, dp_count, dp_at, 0).reshape(-1, D)
     out_full = line_gather(out_part[None], seq_count // 2, seq_count, seq_at).reshape(-1, D)
 
     columns = gate_up_in.reshape(wide_rows, 2, halves, GROUP, run).transpose(3, 0, 1, 2, 4)
@@ -389,9 +391,9 @@
     columns = jnp.broadcast_to(columns, (halves,) + columns.shape[1:])
     hidden = halves * run
     gate_up_rows = exchange(columns.reshape(seq_count, wide_rows, 2 * hidden))
-    gate_up_pieces = swapped(gate_up_rows, "dp", dp_count)
-    down_part = gather_by_swaps(down_in, "seq", halves, half_at, 0, GROUP)
-    down_pieces = swapped(down_part, "dp", dp_count)
+    gate_up_pieces = swapped(gate_up_rows, DP, dp_count)
+    down_part = gather_by_swaps(down_in, SEQ, halves, half_at, 0, GROUP)
+    down_pieces = swapped(down_part, DP, dp_count)
 
     vectors = qkv_own[..., 3 * width :].reshape(seq_count, dp_count, bias_part + gain_part)
     bias_vector = vectors[:, :, :bias_part].reshape(6 * D).astype(WIDE)
@@ -454,10 +456,10 @@
     grad_down = dot_w(activated, grad_mlp_rows)
     grad_gate_up = dot_w(hidden_rows, grad_gate_up_low)
     grad_gate_up = grad_gate_up.reshape(seq_count, dp_count, wide_rows, 2 * hidden)
-    grad_gate_up = scatter_swaps(grad_gate_up, "dp", dp_count, dp_at, 1)
+    grad_gate_up = scatter_swaps(grad_gate_up, DP, dp_count, dp_at, 1)
     shard_down = grad_down.reshape(halves, dp_count, down_rows, D)
-    shard_down = scatter_by_swaps(shard_down, "dp", dp_count, dp_at, 1)
-    shard_down = scatter_by_swaps(shard_down, "seq", halves, half_at, 0, GROUP)
+    shard_down = scatter_by_swaps(shard_down, DP, dp_count, dp_at, 1)
+    shard_down = scatter_by_swaps(shard_down, SEQ, halves, half_at, 0, GROUP)
 
     grad_gain_one = jnp.sum(grad_hidden * normed_one, axis=0)
     grad_bias_one = jnp.sum(grad_hidden, axis=0)
@@ -467,7 +469,7 @@
     grad_attended = dot_t(grad_attn_low, out_full).astype(LOW)
     grad_out_w = dot_w(attended, grad_attn_low)
     grad_out_w = grad_out_w.reshape(seq_count, dp_count, wide_rows, D)
-    grad_out_w = scatter_swaps(grad_out_w, "dp", dp_count, dp_at, 1)
+    grad_out_w = scatter_swaps(grad_out_w, DP, dp_count, dp_at, 1)
 
     spread = grad_attended.reshape(sequences, seq_rows, D)
     spread = jnp.pad(spread, ((0, 0), (0, 0), (0, padded * HD - D)))
@@ -511,7 +513,7 @@
     late = jnp.concatenate(
         [grad_qkv.reshape(seq_count, dp_count, wide_rows, 3 * width), grad_small], axis=-1
     )
-    late = scatter_swaps(late, "dp", dp_count, dp_at, 1)
+    late = scatter_swaps(late, DP, dp_count, dp_at, 1)
     late, grad_out_w = together(late, grad_out_w)
     late, grad_out_w = add_up(late).astype(LOW), add_up(grad_out_w).astype(LOW)
     grad_rows = sequence_swap(grad_rows, seq_count, seq_at, sequences)
@@ -540,26 +542,26 @@
 
 def solution(mesh):
     in_specs = (
-        P("dp", "seq", None),
-        P("dp", "seq"),
-        P("dp", "seq"),
-        P(("seq", "dp"), None),
-        P(("seq", "dp"), None),
-        P(("seq", "dp"), None),
-        P(("seq", "dp"), None),
-        P(("seq", "dp")),
-        P(("seq", "dp")),
-        P("dp", "seq", None),
+        P(DP, SEQ, None),
+        P(DP, SEQ),
+        P(DP, SEQ),
+        P((SEQ, DP), None),
+        P((SEQ, DP), None),
+        P((SEQ, DP), None),
+        P((SEQ, DP), None),
+        P((SEQ, DP)),
+        P((SEQ, DP)),
+        P(DP, SEQ, None),
     )
     out_specs = (
-        P("dp", "seq", None),
-        P("dp", "seq", None),
-        P(("seq", "dp"), None),
-        P(("seq", "dp"), None),
-        P(("seq", "dp"), None),
-        P(("seq", "dp"), None),
-        P(("seq", "dp")),
-        P(("seq", "dp")),
+        P(DP, SEQ, None),
+        P(DP, SEQ, None),
+        P((SEQ, DP), None),
+        P((SEQ, DP), None),
+        P((SEQ, DP), None),
+        P((SEQ, DP), None),
+        P((SEQ, DP)),
+        P((SEQ, DP)),
     )
 
     return jax.shard_map(local, mesh=mesh, in_specs=in_specs, out_specs=out_specs, check_vma=False)

time: 301 us -> 301 us (level)
  no operation moved by 1% of the time
where the time goes in v4:
time: 301 us; the launch traced here: 299 us
  waiting for transfers between devices  119 us (40%)
  starting transfers between devices  75.3 us (25%)
  local copies, waits for them, and re-layouts  40.5 us (13%)
  Pallas kernels  30.3 us (10%)
  other arithmetic  21.9 us (7%)
  matrix products  10.3 us (3%)
    ppermute x45, waiting for transfers between devices, swap(): return lax.ppermute(value, axis, [(i, i ^ mask) for i in range(size)])  110 us
    ppermute x45, starting transfers between devices, swap(): return lax.ppermute(value, axis, [(i, i ^ mask) for i in range(size)])  50.2 us
    all_to_all x6, starting transfers between devices, exchange(): return lax.all_to_all(value, SEQ, 0, 0)  25.1 us
    dynamic_update_slice x20, local copies, waits for them, and re-layouts, put(): lax.dynamic_update_slice(buffer, jnp.expand_dims(value, axis), starts)  14.6 us
    pallas_call x2, Pallas kernels, in_vmem(): pl.pallas_call(kernel, out_shape=out_shape, in_specs=[pl.BlockSpec(memory...  13.9 us
    pallas_call x1, Pallas kernels, attend_back(): pl.pallas_call(lambda *refs: attend_back_kernel(heads, width, *refs), out...  9.51 us
    all_to_all x6, waiting for transfers between devices, exchange(): return lax.all_to_all(value, SEQ, 0, 0)  9.3 us
    pallas_call x1, Pallas kernels, attend(): pl.pallas_call(lambda *refs: attend_kernel(heads, width, *refs), out_shap...  6.89 us
  transfers between devices with their start and end apart: 51, of which 19 were waited for; matrix products, arithmetic and copies ran while one was open for 19% of the time, Pallas kernels for 8%

profile of v4, /device:TPU:0, one launch (start us, length us, event | category | flops | bytes accessed | tf_op | source)
XLA Modules:
  0.0 299.3 jit_solution(14487873471355237714)
XLA Ops:
  0.7 3.0 %collective-permute-start.10 = (bf16[24,768]{1,0:T(8,128)(2,1)}, bf16[24,768]{1,0:T(8,128)(2,1)S(1)}, u32[]{:S(2)}, u32[]{:S(2)}) collective-permute-start(bf16[24,768]{1,0:T(8,128)(2,1)} %param.15), channel_id=1, source_target_pairs={{0,1},{1,0},{2,3},{3,2},{4,5},{5,4},{6,7},{7,6},{8,9},{9,8},{10,11... | collective-permute-start | bytes 110600 | tf_op jit(solution)/shard_map/ppermute | solution.py:47
  8.3 5.3 %all-to-all-start = ((bf16[8,24,584]{2,1,0:T(8,128)(2,1)}), bf16[8,24,584]{2,1,0:T(8,128)(2,1)S(1)}, u32[]{:S(2)}, u32[]{:S(2)}) async-start(bf16[8,24,584]{2,1,0:T(8,128)(2,1)} %pad_maximum_fusion.7), calls=%async_computation | async-start | bytes 491520 | tf_op jit(solution)/shard_map/all_to_all | solution.py:327
  14.4 3.0 collective-permute-start
  18.2 13.2 %collective-permute-done = bf16[72,768]{1,0:T(8,128)(2,1)S(1)} collective-permute-done((bf16[72,768]{1,0:T(8,128)(2,1)S(1)}, bf16[72,768]{1,0:T(8,128)(2,1)S(1)}, u32[]{:S(2)}, u32[]{:S(2)}) %collective-permute-start) | collective-permute-done | bytes 110624 | tf_op jit(solution)/shard_map/ppermute | solution.py:47
  31.5 2.6 collective-permute-done.13
  34.9 4.9 %collective-permute-done.1 = bf16[2,72,768]{2,1,0:T(8,128)(2,1)S(1)} collective-permute-done((bf16[2,72,768]{2,1,0:T(8,128)(2,1)S(1)}, bf16[2,72,768]{2,1,0:T(8,128)(2,1)S(1)}, u32[]{:S(2)}, u32[]{:S(2)}) %collective-permute-start.1) | collective-permute-done | bytes 221216 | tf_op jit(solution)/shard_map/ppermute | solution.py:47
  40.0 1.6 collective-permute-start.3
  45.0 3.5 %all-to-all-start.2 = ((bf16[8,24,1536]{2,1,0:T(8,128)(2,1)}), bf16[8,24,1536]{2,1,0:T(8,128)(2,1)S(1)}, u32[]{:S(2)}, u32[]{:S(2)}) async-start(bf16[8,24,1536]{2,1,0:T(8,128)(2,1)} %bitcast.40), calls=%async_computation.2 | async-start | bytes 1179648 | tf_op jit(solution)/shard_map/all_to_all | solution.py:327
  49.3 1.6 bitcast_dynamic-update-slice_fusion.13
  51.0 2.9 collective-permute-start.6
  55.0 16.5 %collective-permute-done.6 = bf16[96,768]{1,0:T(8,128)(2,1)S(1)} collective-permute-done((bf16[96,768]{1,0:T(8,128)(2,1)}, bf16[96,768]{1,0:T(8,128)(2,1)S(1)}, u32[]{:S(2)}, u32[]{:S(2)}) %collective-permute-start.6) | collective-permute-done | bytes 147488 | tf_op jit(solution)/shard_map/ppermute | solution.py:47
  74.7 1.6 collective-permute-start.8
  81.9 1.6 fusion.refs_1_
  85.0 6.9 %at.1 = (bf16[512,192]{1,0:T(8,128)(2,1)}, f32[512,3]{1,0:T(8,128)}) custom-call(f32[3]{0:T(128)} %dynamic_slice.96.refs_0_, bf16[512,576]{1,0:T(8,128)(2,1)} %fusion.refs_1_, f32[512,2]{1,0:T(8,128)} %copy.190.refs_2_.refs_4_, f32[2,512]{1,0:T(2,128)} %get-tuple-element.140.refs_3_.refs_5_), custom_call_target="tpu_custom_call" | custom-call | tf_op jit(solution)/shard_map/at/pallas_call | solution.py:216
  93.0 1.7 bitcast_dynamic-update-slice_fusion.6
  94.7 1.7 bitcast_dynamic-update-slice_fusion.5
  96.4 1.7 bitcast_dynamic-update-slice_fusion.4
  98.1 1.7 bitcast_dynamic-update-slice_fusion.7
  99.9 4.2 %all-to-all-start.1 = ((bf16[8,64,192]{2,1,0:T(8,128)(2,1)}), bf16[8,64,192]{2,1,0:T(8,128)(2,1)}, u32[]{:S(2)}, u32[]{:S(2)}) async-start(bf16[8,64,192]{2,1,0:T(8,128)(2,1)} %bitcast.21), calls=%async_computation.1 | async-start | bytes 524288 | tf_op jit(solution)/shard_map/all_to_all | solution.py:327
  104.1 1.6 collective-permute-start.16
  109.0 4.6 %all-to-all-done.1 = bf16[8,64,192]{2,1,0:T(8,128)(2,1)} async-done(((bf16[8,64,192]{2,1,0:T(8,128)(2,1)}), bf16[8,64,192]{2,1,0:T(8,128)(2,1)}, u32[]{:S(2)}, u32[]{:S(2)}) %all-to-all-start.1) | async-done | bytes 196640 | tf_op jit(solution)/shard_map/all_to_all | solution.py:327
  116.4 4.1 %collective-permute-done.16 = bf16[8,24,1536]{2,1,0:T(8,128)(2,1)} collective-permute-done((bf16[8,24,1536]{2,1,0:T(8,128)(2,1)S(1)}, bf16[8,24,1536]{2,1,0:T(8,128)(2,1)}, u32[]{:S(2)}, u32[]{:S(2)}) %collective-permute-start.16) | collective-permute-done | bytes 589856 | tf_op jit(solution)/shard_map/ppermute | solution.py:47
  120.5 13.0 %collective-permute-done.17 = bf16[8,24,1536]{2,1,0:T(8,128)(2,1)} collective-permute-done((bf16[8,24,1536]{2,1,0:T(8,128)(2,1)S(1)}, bf16[8,24,1536]{2,1,0:T(8,128)(2,1)}, u32[]{:S(2)}, u32[]{:S(2)}) %collective-permute-start.17) | collective-permute-done | bytes 589856 | tf_op jit(solution)/shard_map/ppermute | solution.py:47
  134.0 1.7 collective-permute-start.20
  138.3 1.7 collective-permute-done.20
  142.9 6.5 %shard_map.170 = (f32[2,128,768]{2,1,0:T(8,128)}, bf16[2,128,768]{2,1,0:T(8,128)(2,1)}, bf16[512,768]{1,0:T(8,128)(2,1)}, f32[512,768]{1,0:T(8,128)}, f32[512,768]{1,0:T(8,128)}) custom-call(bf16[512,768]{1,0:T(8,128)(2,1)} %pad_maximum_fusion.2.refs_0_, bf16[768,1536]{1,0:T(8,128)(2,1)} %bitcast.302, bf16[768,768]{1,0:T(8,128)(2,1)} %bitcast.56.refs_2_.refs_4_), custom_call_target="tpu_custom_call" | custom-call | tf_op jit(solution)/shard_map/pallas_call | solution.py:294
  150.7 1.7 fusion.32
  152.6 1.7 collective-permute-start.23
  154.4 5.2 %collective-permute-done.23 = bf16[128,768]{1,0:T(8,128)(2,1)S(1)} collective-permute-done((bf16[128,768]{1,0:T(8,128)(2,1)S(1)}, bf16[128,768]{1,0:T(8,128)(2,1)S(1)}, u32[]{:S(2)}, u32[]{:S(2)}) %collective-permute-start.23) | collective-permute-done | bytes 196640 | tf_op jit(solution)/shard_map/ppermute | solution.py:47
  161.9 1.7 collective-permute-start.25
  163.6 4.4 %collective-permute-done.25 = bf16[128,768]{1,0:T(8,128)(2,1)S(1)} collective-permute-done((bf16[128,768]{1,0:T(8,128)(2,1)S(1)}, bf16[128,768]{1,0:T(8,128)(2,1)S(1)}, u32[]{:S(2)}, u32[]{:S(2)}) %collective-permute-start.25) | collective-permute-done | bytes 196640 | tf_op jit(solution)/shard_map/ppermute | solution.py:47
  176.3 7.3 %shard_map.171 = (f32[2,128,768]{2,1,0:T(8,128)}, bf16[2,128,768]{2,1,0:T(8,128)(2,1)}, bf16[512,1536]{1,0:T(8,128)(2,1)}) custom-call(bf16[512,768]{1,0:T(8,128)(2,1)} %pad_maximum_fusion.3.refs_0_, f32[512,768]{1,0:T(8,128)} %get-tuple-element.71.refs_1_, f32[512,768]{1,0:T(8,128)} %get-tuple-element.72.refs_2_, bf16[768,1536]{1,0:T(8,128)(2,1)} %bitcast.303, ...), custom_call_target="tpu_custom_call" | custom-call | tf_op jit(solution)/shard_map/pallas_call | solution.py:294
  183.7 2.8 fusion.56
  191.5 2.6 collective-permute-start.44
  195.8 5.3 %collective-permute-done.44 = bf16[96,768]{1,0:T(8,128)(2,1)S(1)} collective-permute-done((bf16[96,768]{1,0:T(8,128)(2,1)S(1)}, bf16[96,768]{1,0:T(8,128)(2,1)S(1)}, u32[]{:S(2)}, u32[]{:S(2)}) %collective-permute-start.44) | collective-permute-done | bytes 147488 | tf_op jit(solution)/shard_map/ppermute | solution.py:47
  203.0 13.4 %collective-permute-done.39 = bf16[8,24,1536]{2,1,0:T(8,128)(2,1)S(1)} collective-permute-done((bf16[8,24,1536]{2,1,0:T(8,128)(2,1)S(1)}, bf16[8,24,1536]{2,1,0:T(8,128)(2,1)S(1)}, u32[]{:S(2)}, u32[]{:S(2)}) %collective-permute-start.39) | collective-permute-done | bytes 589856 | tf_op jit(solution)/shard_map/ppermute | solution.py:47
  220.3 4.7 %all-to-all-start.3 = ((bf16[8,64,192]{2,1,0:T(8,128)(2,1)}), bf16[8,64,192]{2,1,0:T(8,128)(2,1)}, u32[]{:S(2)}, u32[]{:S(2)}) async-start(bf16[8,64,192]{2,1,0:T(8,128)(2,1)} %bitcast.64), calls=%async_computation.3 | async-start | bytes 524288 | tf_op jit(solution)/shard_map/all_to_all | solution.py:327
  230.1 4.7 %all-to-all-done.3 = bf16[8,64,192]{2,1,0:T(8,128)(2,1)} async-done(((bf16[8,64,192]{2,1,0:T(8,128)(2,1)}), bf16[8,64,192]{2,1,0:T(8,128)(2,1)}, u32[]{:S(2)}, u32[]{:S(2)}) %all-to-all-start.3) | async-done | bytes 196640 | tf_op jit(solution)/shard_map/all_to_all | solution.py:327
  234.8 3.5 %all-to-all-start.5 = ((bf16[8,24,1536]{2,1,0:T(8,128)(2,1)}), bf16[8,24,1536]{2,1,0:T(8,128)(2,1)S(1)}, u32[]{:S(2)}, u32[]{:S(2)}) async-start(bf16[8,24,1536]{2,1,0:T(8,128)(2,1)} %fusion.4), calls=%async_computation.5 | async-start | bytes 1179648 | tf_op jit(solution)/shard_map/all_to_all | solution.py:327
  238.4 9.5 %ab.1 = (bf16[512,576]{1,0:T(8,128)(2,1)}, f32[8,192]{1,0:T(8,128)}) custom-call(f32[3]{0:T(128)} %dynamic_slice.96.refs_0_, bf16[512,576]{1,0:T(8,128)(2,1)} %fusion.refs_1_, bf16[512,192]{1,0:T(8,128)(2,1)} %bitcast.65.refs_2_, f32[512,3]{1,0:T(8,128)} %get-tuple-element.75.refs_3_, f32[512,2]{1,0:T(8,128)} %copy.190.refs_2_.refs_4_, ...), custom_call_target="tpu_custom_call" | custom-call | tf_op jit(solution)/shard_map/ab/pallas_call | solution.py:231
  250.7 1.9 fusion.5
  255.7 1.5 collective-permute-start.34
  257.4 4.2 %collective-permute-done.32 = bf16[8,24,584]{2,1,0:T(8,128)(2,1)S(1)} collective-permute-done((bf16[8,24,584]{2,1,0:T(8,128)(2,1)S(1)}, bf16[8,24,584]{2,1,0:T(8,128)(2,1)S(1)}, u32[]{:S(2)}, u32[]{:S(2)}) %collective-permute-start.32) | collective-permute-done | bytes 224288 | tf_op jit(solution)/shard_map/ppermute | solution.py:47
  261.6 5.0 %collective-permute-done.33 = bf16[8,24,584]{2,1,0:T(8,128)(2,1)S(1)} collective-permute-done((bf16[8,24,584]{2,1,0:T(8,128)(2,1)S(1)}, bf16[8,24,584]{2,1,0:T(8,128)(2,1)S(1)}, u32[]{:S(2)}, u32[]{:S(2)}) %collective-permute-start.33) | collective-permute-done | bytes 224288 | tf_op jit(solution)/shard_map/ppermute | solution.py:47
  268.2 1.7 collective-permute-start.30
  270.8 3.7 %all-to-all-start.4 = ((bf16[8,24,1352]{2,1,0:T(8,128)(2,1)}), bf16[8,24,1352]{2,1,0:T(8,128)(2,1)S(1)}, u32[]{:S(2)}, u32[]{:S(2)}) async-start(bf16[8,24,1352]{2,1,0:T(8,128)(2,1)} %pad_maximum_fusion.5), calls=%async_computation.4 | async-start | bytes 1081344 | tf_op jit(solution)/shard_map/all_to_all | solution.py:327
  274.6 3.0 collective-permute-start.31
  279.6 14.8 %collective-permute-done.31 = bf16[64,768]{1,0:T(8,128)(2,1)S(1)} collective-permute-done((bf16[64,768]{1,0:T(8,128)(2,1)S(1)}, bf16[64,768]{1,0:T(8,128)(2,1)S(1)}, u32[]{:S(2)}, u32[]{:S(2)}) %collective-permute-start.31) | collective-permute-done | bytes 98336 | tf_op jit(solution)/shard_map/ppermute | solution.py:47
  (317 shorter events, 80.5 us)
Async XLA Ops:
  0.7 17.4 %collective-permute-start.10 = (bf16[24,768]{1,0:T(8,128)(2,1)}, bf16[24,768]{1,0:T(8,128)(2,1)S(1)}, u32[]{:S(2)}, u32[]{:S(2)}) collective-permute-start(bf16[24,768]{1,0:T(8,128)(2,1)} %param.15), channel_id=1, source_target_pairs={{0,1},{1,0},{2,3},{3,2},{4,5},{5,4},{6,7},{7,6},{8,9},{9,8},{10,11... | collective-permute-start | bytes 110600 | tf_op jit(solution)/shard_map/ppermute | solution.py:47
  3.7 14.4 %collective-permute-start.11 = (bf16[24,768]{1,0:T(8,128)(2,1)}, bf16[24,768]{1,0:T(8,128)(2,1)S(1)}, u32[]{:S(2)}, u32[]{:S(2)}) collective-permute-start(bf16[24,768]{1,0:T(8,128)(2,1)} %param.15), channel_id=1, source_target_pairs={{0,2},{1,3},{2,0},{3,1},{4,6},{5,7},{6,4},{7,5},{8,10},{9,11},{10,... | collective-permute-start | bytes 110600 | tf_op jit(solution)/shard_map/ppermute | solution.py:47
  5.2 12.9 %collective-permute-start.12 = (bf16[24,768]{1,0:T(8,128)(2,1)}, bf16[24,768]{1,0:T(8,128)(2,1)S(1)}, u32[]{:S(2)}, u32[]{:S(2)}) collective-permute-start(bf16[24,768]{1,0:T(8,128)(2,1)} %param.15), channel_id=1, source_target_pairs={{0,3},{1,2},{2,1},{3,0},{4,7},{5,6},{6,5},{7,4},{8,11},{9,10},{10,... | collective-permute-start | bytes 110600 | tf_op jit(solution)/shard_map/ppermute | solution.py:47
  8.3 31.7 %all-to-all-start = ((bf16[8,24,584]{2,1,0:T(8,128)(2,1)}), bf16[8,24,584]{2,1,0:T(8,128)(2,1)S(1)}, u32[]{:S(2)}, u32[]{:S(2)}) async-start(bf16[8,24,584]{2,1,0:T(8,128)(2,1)} %pad_maximum_fusion.7), calls=%async_computation | async-start | bytes 491520 | tf_op jit(solution)/shard_map/all_to_all | solution.py:327
  14.4 17.1 %collective-permute-start = (bf16[72,768]{1,0:T(8,128)(2,1)S(1)}, bf16[72,768]{1,0:T(8,128)(2,1)S(1)}, u32[]{:S(2)}, u32[]{:S(2)}) collective-permute-start(bf16[72,768]{1,0:T(8,128)(2,1)S(1)} %get-tuple-element.128), channel_id=1, source_target_pairs={{0,16},{4,20},{8,24},{12,28},{16,0},{20,4},{24,8},{28,12},{1,17},{... | collective-permute-start | bytes 331784 | tf_op jit(solution)/shard_map/ppermute | solution.py:47
  18.1 16.0 %collective-permute-start.13 = (bf16[1,96,768]{2,1,0:T(8,128)(2,1)S(1)}, bf16[1,96,768]{2,1,0:T(8,128)(2,1)S(1)}, u32[]{:S(2)}, u32[]{:S(2)}) collective-permute-start(bf16[1,96,768]{2,1,0:T(8,128)(2,1)S(1)} %bitcast.334), channel_id=1, source_target_pairs={{0,16},{4,20},{8,24},{12,28},{16,0},{20,4},{24,8},{28,12},{1,17},{... | collective-permute-start | bytes 442376 | tf_op jit(solution)/shard_map/ppermute | solution.py:47
  31.4 8.4 %collective-permute-start.1 = (bf16[2,72,768]{2,1,0:T(8,128)(2,1)S(1)}, bf16[2,72,768]{2,1,0:T(8,128)(2,1)S(1)}, u32[]{:S(2)}, u32[]{:S(2)}) collective-permute-start(bf16[2,72,768]{2,1,0:T(8,128)(2,1)S(1)} %bitcast_dynamic-update-slice_fusion.14), channel_id=1, source_target_pairs={{0,8},{4,12},{8,0},{12,4},{16,24},{20,28},{24,16},{28,20},{1,9},{5... | collective-permute-start | bytes 663560 | tf_op jit(solution)/shard_map/ppermute | solution.py:47
  34.9 16.2 %collective-permute-start.14 = (bf16[2,96,768]{2,1,0:T(8,128)(2,1)}, bf16[2,96,768]{2,1,0:T(8,128)(2,1)}, u32[]{:S(2)}, u32[]{:S(2)}) collective-permute-start(bf16[2,96,768]{2,1,0:T(8,128)(2,1)} %maximum_bitcast_fusion), channel_id=1, source_target_pairs={{0,8},{4,12},{8,0},{12,4},{16,24},{20,28},{24,16},{28,20},{1,9},{5... | collective-permute-start | bytes 884744 | tf_op jit(solution)/shard_map/ppermute | solution.py:47
  39.9 40.6 %collective-permute-start.2 = (bf16[4,72,768]{2,1,0:T(8,128)(2,1)S(1)}, bf16[4,72,768]{2,1,0:T(8,128)(2,1)S(1)}, u32[]{:S(2)}, u32[]{:S(2)}) collective-permute-start(bf16[4,72,768]{2,1,0:T(8,128)(2,1)S(1)} %bitcast.321), channel_id=1, source_target_pairs={{0,4},{4,0},{8,12},{12,8},{16,20},{20,16},{24,28},{28,24},{1,5},{5... | collective-permute-start | bytes 1327112 | tf_op jit(solution)/shard_map/ppermute | solution.py:47
  40.0 32.3 %collective-permute-start.3 = (bf16[8,24,584]{2,1,0:T(8,128)(2,1)S(1)}, bf16[8,24,584]{2,1,0:T(8,128)(2,1)}, u32[]{:S(2)}, u32[]{:S(2)}) collective-permute-start(bf16[8,24,584]{2,1,0:T(8,128)(2,1)S(1)} %all-to-all-done), channel_id=1, source_target_pairs={{0,1},{1,0},{2,3},{3,2},{4,5},{5,4},{6,7},{7,6},{8,9},{9,8},{10,11... | collective-permute-start | bytes 672776 | tf_op jit(solution)/shard_map/ppermute | solution.py:47
  41.5 33.2 %collective-permute-start.4 = (bf16[8,24,584]{2,1,0:T(8,128)(2,1)S(1)}, bf16[8,24,584]{2,1,0:T(8,128)(2,1)}, u32[]{:S(2)}, u32[]{:S(2)}) collective-permute-start(bf16[8,24,584]{2,1,0:T(8,128)(2,1)S(1)} %all-to-all-done), channel_id=1, source_target_pairs={{0,2},{1,3},{2,0},{3,1},{4,6},{5,7},{6,4},{7,5},{8,10},{9,11},{10,... | collective-permute-start | bytes 672776 | tf_op jit(solution)/shard_map/ppermute | solution.py:47
  43.1 34.2 %collective-permute-start.5 = (bf16[8,24,584]{2,1,0:T(8,128)(2,1)S(1)}, bf16[8,24,584]{2,1,0:T(8,128)(2,1)S(1)}, u32[]{:S(2)}, u32[]{:S(2)}) collective-permute-start(bf16[8,24,584]{2,1,0:T(8,128)(2,1)S(1)} %all-to-all-done), channel_id=1, source_target_pairs={{0,3},{1,2},{2,1},{3,0},{4,7},{5,6},{6,5},{7,4},{8,11},{9,10},{10,... | collective-permute-start | bytes 672776 | tf_op jit(solution)/shard_map/ppermute | solution.py:47
  45.0 54.8 %all-to-all-start.2 = ((bf16[8,24,1536]{2,1,0:T(8,128)(2,1)}), bf16[8,24,1536]{2,1,0:T(8,128)(2,1)S(1)}, u32[]{:S(2)}, u32[]{:S(2)}) async-start(bf16[8,24,1536]{2,1,0:T(8,128)(2,1)} %bitcast.40), calls=%async_computation.2 | async-start | bytes 1179648 | tf_op jit(solution)/shard_map/all_to_all | solution.py:327
  51.0 20.5 %collective-permute-start.6 = (bf16[96,768]{1,0:T(8,128)(2,1)}, bf16[96,768]{1,0:T(8,128)(2,1)S(1)}, u32[]{:S(2)}, u32[]{:S(2)}) collective-permute-start(bf16[96,768]{1,0:T(8,128)(2,1)} %param.17), channel_id=1, source_target_pairs={{0,16},{4,20},{8,24},{12,28},{16,0},{20,4},{24,8},{28,12},{1,17},{... | collective-permute-start | bytes 442376 | tf_op jit(solution)/shard_map/ppermute | solution.py:47
  71.6 36.1 %collective-permute-start.15 = (bf16[4,96,768]{2,1,0:T(8,128)(2,1)S(1)}, bf16[4,96,768]{2,1,0:T(8,128)(2,1)}, u32[]{:S(2)}, u32[]{:S(2)}) collective-permute-start(bf16[4,96,768]{2,1,0:T(8,128)(2,1)S(1)} %bitcast.316), channel_id=1, source_target_pairs={{0,4},{4,0},{8,12},{12,8},{16,20},{20,16},{24,28},{28,24},{1,5},{5... | collective-permute-start | bytes 1769480 | tf_op jit(solution)/shard_map/ppermute | solution.py:47
  72.2 19.7 %collective-permute-start.7 = (bf16[2,96,768]{2,1,0:T(8,128)(2,1)}, bf16[2,96,768]{2,1,0:T(8,128)(2,1)}, u32[]{:S(2)}, u32[]{:S(2)}) collective-permute-start(bf16[2,96,768]{2,1,0:T(8,128)(2,1)} %bitcast_dynamic-update-slice_fusion.12), channel_id=1, source_target_pairs={{0,1},{1,0},{2,3},{3,2},{4,5},{5,4},{6,7},{7,6},{8,9},{9,8},{10,11... | collective-permute-start | bytes 884744 | tf_op jit(solution)/shard_map/ppermute | solution.py:47
  74.7 17.2 %collective-permute-start.8 = (bf16[2,96,768]{2,1,0:T(8,128)(2,1)}, bf16[2,96,768]{2,1,0:T(8,128)(2,1)}, u32[]{:S(2)}, u32[]{:S(2)}) collective-permute-start(bf16[2,96,768]{2,1,0:T(8,128)(2,1)} %bitcast_dynamic-update-slice_fusion.12), channel_id=1, source_target_pairs={{0,2},{1,3},{2,0},{3,1},{4,6},{5,7},{6,4},{7,5},{8,10},{9,11},{10,... | collective-permute-start | bytes 884744 | tf_op jit(solution)/shard_map/ppermute | solution.py:47
  77.3 14.6 %collective-permute-start.9 = (bf16[2,96,768]{2,1,0:T(8,128)(2,1)}, bf16[2,96,768]{2,1,0:T(8,128)(2,1)}, u32[]{:S(2)}, u32[]{:S(2)}) collective-permute-start(bf16[2,96,768]{2,1,0:T(8,128)(2,1)} %bitcast_dynamic-update-slice_fusion.12), channel_id=1, source_target_pairs={{0,3},{1,2},{2,1},{3,0},{4,7},{5,6},{6,5},{7,4},{8,11},{9,10},{10,... | collective-permute-start | bytes 884744 | tf_op jit(solution)/shard_map/ppermute | solution.py:47
  99.9 13.8 %all-to-all-start.1 = ((bf16[8,64,192]{2,1,0:T(8,128)(2,1)}), bf16[8,64,192]{2,1,0:T(8,128)(2,1)}, u32[]{:S(2)}, u32[]{:S(2)}) async-start(bf16[8,64,192]{2,1,0:T(8,128)(2,1)} %bitcast.21), calls=%async_computation.1 | async-start | bytes 524288 | tf_op jit(solution)/shard_map/all_to_all | solution.py:327
  104.1 16.4 %collective-permute-start.16 = (bf16[8,24,1536]{2,1,0:T(8,128)(2,1)S(1)}, bf16[8,24,1536]{2,1,0:T(8,128)(2,1)}, u32[]{:S(2)}, u32[]{:S(2)}) collective-permute-start(bf16[8,24,1536]{2,1,0:T(8,128)(2,1)S(1)} %all-to-all-done.2), channel_id=1, source_target_pairs={{0,1},{1,0},{2,3},{3,2},{4,5},{5,4},{6,7},{7,6},{8,9},{9,8},{10,11... | collective-permute-start | bytes 1769480 | tf_op jit(solution)/shard_map/ppermute | solution.py:47
  105.7 27.8 %collective-permute-start.17 = (bf16[8,24,1536]{2,1,0:T(8,128)(2,1)S(1)}, bf16[8,24,1536]{2,1,0:T(8,128)(2,1)}, u32[]{:S(2)}, u32[]{:S(2)}) collective-permute-start(bf16[8,24,1536]{2,1,0:T(8,128)(2,1)S(1)} %all-to-all-done.2), channel_id=1, source_target_pairs={{0,2},{1,3},{2,0},{3,1},{4,6},{5,7},{6,4},{7,5},{8,10},{9,11},{10,... | collective-permute-start | bytes 1769480 | tf_op jit(solution)/shard_map/ppermute | solution.py:47
  107.2 26.3 %collective-permute-start.18 = (bf16[8,24,1536]{2,1,0:T(8,128)(2,1)S(1)}, bf16[8,24,1536]{2,1,0:T(8,128)(2,1)}, u32[]{:S(2)}, u32[]{:S(2)}) collective-permute-start(bf16[8,24,1536]{2,1,0:T(8,128)(2,1)S(1)} %all-to-all-done.2), channel_id=1, source_target_pairs={{0,3},{1,2},{2,1},{3,0},{4,7},{5,6},{6,5},{7,4},{8,11},{9,10},{10,... | collective-permute-start | bytes 1769480 | tf_op jit(solution)/shard_map/ppermute | solution.py:47
  134.0 5.9 %collective-permute-start.20 = (bf16[128,768]{1,0:T(8,128)(2,1)S(1)}, bf16[128,768]{1,0:T(8,128)(2,1)S(1)}, u32[]{:S(2)}, u32[]{:S(2)}) collective-permute-start(bf16[128,768]{1,0:T(8,128)(2,1)S(1)} %fusion.33), channel_id=1, source_target_pairs={{0,8},{4,12},{8,0},{12,4},{16,24},{20,28},{24,16},{28,20},{1,9},{5... | collective-permute-start | bytes 589832 | tf_op jit(solution)/shard_map/ppermute | solution.py:47
  135.7 5.4 %collective-permute-start.19 = (bf16[128,768]{1,0:T(8,128)(2,1)S(1)}, bf16[128,768]{1,0:T(8,128)(2,1)S(1)}, u32[]{:S(2)}, u32[]{:S(2)}) collective-permute-start(bf16[128,768]{1,0:T(8,128)(2,1)S(1)} %fusion.33), channel_id=1, source_target_pairs={{0,4},{4,0},{8,12},{12,8},{16,20},{20,16},{24,28},{28,24},{1,5},{5... | collective-permute-start | bytes 589832 | tf_op jit(solution)/shard_map/ppermute | solution.py:47
  152.6 7.0 %collective-permute-start.23 = (bf16[128,768]{1,0:T(8,128)(2,1)S(1)}, bf16[128,768]{1,0:T(8,128)(2,1)S(1)}, u32[]{:S(2)}, u32[]{:S(2)}) collective-permute-start(bf16[128,768]{1,0:T(8,128)(2,1)S(1)} %fusion.44), channel_id=1, source_target_pairs={{0,8},{4,12},{8,0},{12,4},{16,24},{20,28},{24,16},{28,20},{1,9},{5... | collective-permute-start | bytes 589832 | tf_op jit(solution)/shard_map/ppermute | solution.py:47
  161.9 6.1 %collective-permute-start.25 = (bf16[128,768]{1,0:T(8,128)(2,1)S(1)}, bf16[128,768]{1,0:T(8,128)(2,1)S(1)}, u32[]{:S(2)}, u32[]{:S(2)}) collective-permute-start(bf16[128,768]{1,0:T(8,128)(2,1)S(1)} %convert_element_type.279), channel_id=1, source_target_pairs={{0,8},{4,12},{8,0},{12,4},{16,24},{20,28},{24,16},{28,20},{1,9},{5... | collective-permute-start | bytes 589832 | tf_op jit(solution)/shard_map/ppermute | solution.py:47
  163.6 5.7 %collective-permute-start.24 = (bf16[128,768]{1,0:T(8,128)(2,1)S(1)}, bf16[128,768]{1,0:T(8,128)(2,1)S(1)}, u32[]{:S(2)}, u32[]{:S(2)}) collective-permute-start(bf16[128,768]{1,0:T(8,128)(2,1)S(1)} %convert_element_type.279), channel_id=1, source_target_pairs={{0,4},{4,0},{8,12},{12,8},{16,20},{20,16},{24,28},{28,24},{1,5},{5... | collective-permute-start | bytes 589832 | tf_op jit(solution)/shard_map/ppermute | solution.py:47
  171.8 16.4 %collective-permute-start.41 = (bf16[2,96,768]{2,1,0:T(8,128)(2,1)S(1)}, bf16[2,96,768]{2,1,0:T(8,128)(2,1)S(1)}, u32[]{:S(2)}, u32[]{:S(2)}) collective-permute-start(bf16[2,96,768]{2,1,0:T(8,128)(2,1)S(1)} %get-tuple-element.108), channel_id=1, source_target_pairs={{0,1},{1,0},{2,3},{3,2},{4,5},{5,4},{6,7},{7,6},{8,9},{9,8},{10,11... | collective-permute-start | bytes 884744 | tf_op jit(solution)/shard_map/ppermute | solution.py:47
  173.3 15.5 %collective-permute-start.42 = (bf16[2,96,768]{2,1,0:T(8,128)(2,1)S(1)}, bf16[2,96,768]{2,1,0:T(8,128)(2,1)S(1)}, u32[]{:S(2)}, u32[]{:S(2)}) collective-permute-start(bf16[2,96,768]{2,1,0:T(8,128)(2,1)S(1)} %get-tuple-element.109), channel_id=1, source_target_pairs={{0,2},{1,3},{2,0},{3,1},{4,6},{5,7},{6,4},{7,5},{8,10},{9,11},{10,... | collective-permute-start | bytes 884744 | tf_op jit(solution)/shard_map/ppermute | solution.py:47
  173.9 16.4 %collective-permute-start.43 = (bf16[2,96,768]{2,1,0:T(8,128)(2,1)S(1)}, bf16[2,96,768]{2,1,0:T(8,128)(2,1)S(1)}, u32[]{:S(2)}, u32[]{:S(2)}) collective-permute-start(bf16[2,96,768]{2,1,0:T(8,128)(2,1)S(1)} %get-tuple-element.110), channel_id=1, source_target_pairs={{0,3},{1,2},{2,1},{3,0},{4,7},{5,6},{6,5},{7,4},{8,11},{9,10},{10,... | collective-permute-start | bytes 884744 | tf_op jit(solution)/shard_map/ppermute | solution.py:47
  183.6 10.5 %collective-permute-start.27 = (bf16[2,128,768]{2,1,0:T(8,128)(2,1)}, bf16[2,128,768]{2,1,0:T(8,128)(2,1)S(1)}, u32[]{:S(2)}, u32[]{:S(2)}) collective-permute-start(bf16[2,128,768]{2,1,0:T(8,128)(2,1)} %get-tuple-element.74), channel_id=1, source_target_pairs={{0,4},{4,0},{8,12},{12,8},{16,20},{20,16},{24,28},{28,24},{1,5},{5... | collective-permute-start | bytes 1179656 | tf_op jit(solution)/shard_map/ppermute | solution.py:47
  186.7 16.3 %collective-permute-start.38 = (bf16[8,24,1536]{2,1,0:T(8,128)(2,1)S(1)}, bf16[8,24,1536]{2,1,0:T(8,128)(2,1)S(1)}, u32[]{:S(2)}, u32[]{:S(2)}) collective-permute-start(bf16[8,24,1536]{2,1,0:T(8,128)(2,1)S(1)} %get-tuple-element.105), channel_id=1, source_target_pairs={{0,1},{1,0},{2,3},{3,2},{4,5},{5,4},{6,7},{7,6},{8,9},{9,8},{10,11... | collective-permute-start | bytes 1769480 | tf_op jit(solution)/shard_map/ppermute | solution.py:47
  188.2 28.1 %collective-permute-start.39 = (bf16[8,24,1536]{2,1,0:T(8,128)(2,1)S(1)}, bf16[8,24,1536]{2,1,0:T(8,128)(2,1)S(1)}, u32[]{:S(2)}, u32[]{:S(2)}) collective-permute-start(bf16[8,24,1536]{2,1,0:T(8,128)(2,1)S(1)} %get-tuple-element.107), channel_id=1, source_target_pairs={{0,2},{1,3},{2,0},{3,1},{4,6},{5,7},{6,4},{7,5},{8,10},{9,11},{10,... | collective-permute-start | bytes 1769480 | tf_op jit(solution)/shard_map/ppermute | solution.py:47
  188.8 27.5 %collective-permute-start.40 = (bf16[8,24,1536]{2,1,0:T(8,128)(2,1)S(1)}, bf16[8,24,1536]{2,1,0:T(8,128)(2,1)S(1)}, u32[]{:S(2)}, u32[]{:S(2)}) collective-permute-start(bf16[8,24,1536]{2,1,0:T(8,128)(2,1)S(1)} %get-tuple-element.106), channel_id=1, source_target_pairs={{0,3},{1,2},{2,1},{3,0},{4,7},{5,6},{6,5},{7,4},{8,11},{9,10},{10,... | collective-permute-start | bytes 1769480 | tf_op jit(solution)/shard_map/ppermute | solution.py:47
  191.5 9.6 %collective-permute-start.44 = (bf16[96,768]{1,0:T(8,128)(2,1)S(1)}, bf16[96,768]{1,0:T(8,128)(2,1)S(1)}, u32[]{:S(2)}, u32[]{:S(2)}) collective-permute-start(bf16[96,768]{1,0:T(8,128)(2,1)S(1)} %fusion.46), channel_id=1, source_target_pairs={{0,16},{4,20},{8,24},{12,28},{16,0},{20,4},{24,8},{28,12},{1,17},{... | collective-permute-start | bytes 442376 | tf_op jit(solution)/shard_map/ppermute | solution.py:47
  194.2 23.2 %collective-permute-start.28 = (bf16[128,768]{1,0:T(8,128)(2,1)S(1)}, bf16[128,768]{1,0:T(8,128)(2,1)S(1)}, u32[]{:S(2)}, u32[]{:S(2)}) collective-permute-start(bf16[128,768]{1,0:T(8,128)(2,1)S(1)} %fusion.45), channel_id=1, source_target_pairs={{0,8},{4,12},{8,0},{12,4},{16,24},{20,28},{24,16},{28,20},{1,9},{5... | collective-permute-start | bytes 589832 | tf_op jit(solution)/shard_map/ppermute | solution.py:47
  220.3 14.6 %all-to-all-start.3 = ((bf16[8,64,192]{2,1,0:T(8,128)(2,1)}), bf16[8,64,192]{2,1,0:T(8,128)(2,1)}, u32[]{:S(2)}, u32[]{:S(2)}) async-start(bf16[8,64,192]{2,1,0:T(8,128)(2,1)} %bitcast.64), calls=%async_computation.3 | async-start | bytes 524288 | tf_op jit(solution)/shard_map/all_to_all | solution.py:327
  226.5 29.2 %collective-permute-start.35 = (bf16[8,24,768]{2,1,0:T(8,128)(2,1)}, bf16[8,24,768]{2,1,0:T(8,128)(2,1)}, u32[]{:S(2)}, u32[]{:S(2)}) collective-permute-start(bf16[8,24,768]{2,1,0:T(8,128)(2,1)} %get-tuple-element.113), channel_id=1, source_target_pairs={{0,1},{1,0},{2,3},{3,2},{4,5},{5,4},{6,7},{7,6},{8,9},{9,8},{10,11... | collective-permute-start | bytes 884744 | tf_op jit(solution)/shard_map/ppermute | solution.py:47
  227.0 30.3 %collective-permute-start.36 = (bf16[8,24,768]{2,1,0:T(8,128)(2,1)}, bf16[8,24,768]{2,1,0:T(8,128)(2,1)}, u32[]{:S(2)}, u32[]{:S(2)}) collective-permute-start(bf16[8,24,768]{2,1,0:T(8,128)(2,1)} %get-tuple-element.112), channel_id=1, source_target_pairs={{0,2},{1,3},{2,0},{3,1},{4,6},{5,7},{6,4},{7,5},{8,10},{9,11},{10,... | collective-permute-start | bytes 884744 | tf_op jit(solution)/shard_map/ppermute | solution.py:47
  228.5 29.0 %collective-permute-start.37 = (bf16[8,24,768]{2,1,0:T(8,128)(2,1)}, bf16[8,24,768]{2,1,0:T(8,128)(2,1)}, u32[]{:S(2)}, u32[]{:S(2)}) collective-permute-start(bf16[8,24,768]{2,1,0:T(8,128)(2,1)} %get-tuple-element.111), channel_id=1, source_target_pairs={{0,3},{1,2},{2,1},{3,0},{4,7},{5,6},{6,5},{7,4},{8,11},{9,10},{10,... | collective-permute-start | bytes 884744 | tf_op jit(solution)/shard_map/ppermute | solution.py:47
  234.8 36.0 %all-to-all-start.5 = ((bf16[8,24,1536]{2,1,0:T(8,128)(2,1)}), bf16[8,24,1536]{2,1,0:T(8,128)(2,1)S(1)}, u32[]{:S(2)}, u32[]{:S(2)}) async-start(bf16[8,24,1536]{2,1,0:T(8,128)(2,1)} %fusion.4), calls=%async_computation.5 | async-start | bytes 1179648 | tf_op jit(solution)/shard_map/all_to_all | solution.py:327
  252.7 8.9 %collective-permute-start.32 = (bf16[8,24,584]{2,1,0:T(8,128)(2,1)S(1)}, bf16[8,24,584]{2,1,0:T(8,128)(2,1)S(1)}, u32[]{:S(2)}, u32[]{:S(2)}) collective-permute-start(bf16[8,24,584]{2,1,0:T(8,128)(2,1)S(1)} %get-tuple-element.115), channel_id=1, source_target_pairs={{0,1},{1,0},{2,3},{3,2},{4,5},{5,4},{6,7},{7,6},{8,9},{9,8},{10,11... | collective-permute-start | bytes 672776 | tf_op jit(solution)/shard_map/ppermute | solution.py:47
  253.4 13.2 %collective-permute-start.33 = (bf16[8,24,584]{2,1,0:T(8,128)(2,1)S(1)}, bf16[8,24,584]{2,1,0:T(8,128)(2,1)S(1)}, u32[]{:S(2)}, u32[]{:S(2)}) collective-permute-start(bf16[8,24,584]{2,1,0:T(8,128)(2,1)S(1)} %get-tuple-element.116), channel_id=1, source_target_pairs={{0,2},{1,3},{2,0},{3,1},{4,6},{5,7},{6,4},{7,5},{8,10},{9,11},{10,... | collective-permute-start | bytes 672776 | tf_op jit(solution)/shard_map/ppermute | solution.py:47
  255.7 10.9 %collective-permute-start.34 = (bf16[8,24,584]{2,1,0:T(8,128)(2,1)S(1)}, bf16[8,24,584]{2,1,0:T(8,128)(2,1)S(1)}, u32[]{:S(2)}, u32[]{:S(2)}) collective-permute-start(bf16[8,24,584]{2,1,0:T(8,128)(2,1)S(1)} %get-tuple-element.114), channel_id=1, source_target_pairs={{0,3},{1,2},{2,1},{3,0},{4,7},{5,6},{6,5},{7,4},{8,11},{9,10},{10,... | collective-permute-start | bytes 672776 | tf_op jit(solution)/shard_map/ppermute | solution.py:47
  257.3 10.7 %collective-permute-start.29 = (bf16[4,64,768]{2,1,0:T(8,128)(2,1)S(1)}, bf16[4,64,768]{2,1,0:T(8,128)(2,1)S(1)}, u32[]{:S(2)}, u32[]{:S(2)}) collective-permute-start(bf16[4,64,768]{2,1,0:T(8,128)(2,1)S(1)} %dynamic-slice_bitcast_fusion.1), channel_id=1, source_target_pairs={{0,4},{4,0},{8,12},{12,8},{16,20},{20,16},{24,28},{28,24},{1,5},{5... | collective-permute-start | bytes 1179656 | tf_op jit(solution)/shard_map/ppermute | solution.py:47
  268.2 6.4 %collective-permute-start.30 = (bf16[2,64,768]{2,1,0:T(8,128)(2,1)S(1)}, bf16[2,64,768]{2,1,0:T(8,128)(2,1)S(1)}, u32[]{:S(2)}, u32[]{:S(2)}) collective-permute-start(bf16[2,64,768]{2,1,0:T(8,128)(2,1)S(1)} %fusion.43), channel_id=1, source_target_pairs={{0,8},{4,12},{8,0},{12,4},{16,24},{20,28},{24,16},{28,20},{1,9},{5... | collective-permute-start | bytes 589832 | tf_op jit(solution)/shard_map/ppermute | solution.py:47
  270.8 24.4 %all-to-all-start.4 = ((bf16[8,24,1352]{2,1,0:T(8,128)(2,1)}), bf16[8,24,1352]{2,1,0:T(8,128)(2,1)S(1)}, u32[]{:S(2)}, u32[]{:S(2)}) async-start(bf16[8,24,1352]{2,1,0:T(8,128)(2,1)} %pad_maximum_fusion.5), calls=%async_computation.4 | async-start | bytes 1081344 | tf_op jit(solution)/shard_map/all_to_all | solution.py:327
  274.6 19.8 %collective-permute-start.31 = (bf16[64,768]{1,0:T(8,128)(2,1)S(1)}, bf16[64,768]{1,0:T(8,128)(2,1)S(1)}, u32[]{:S(2)}, u32[]{:S(2)}) collective-permute-start(bf16[64,768]{1,0:T(8,128)(2,1)S(1)} %fusion.47), channel_id=1, source_target_pairs={{0,16},{4,20},{8,24},{12,28},{16,0},{20,4},{24,8},{28,12},{1,17},{... | collective-permute-start | bytes 294920 | tf_op jit(solution)/shard_map/ppermute | solution.py:47
  (43 other events, 350.1 us)
